TPU v7x, 512 devices: a whole 4x8x8 slice. The times are simulated.
512 devices in a mesh: fsdp: 128 (over z, y, core), seq: 4 (over x).
Axes of the slice: x: 4, y: 8, z: 8, core: 2. Of those that a mesh axis runs over, the one named last changes fastest.
Arguments:
- text_embeds: bfloat16 [35840, 4096], P('fsdp'), may hold values from -8 to 8
- vision_tokens: bfloat16 [16384, 4096], P('fsdp', 'seq'), may hold values from -6 to 6
- vision_request: int32 [16384, 1], P('fsdp'), may hold values from 0 to 127; in each aligned block of 128 rows (0 to 127, 128 to 255, ...) at most 2 rows name the same one
- image_start: int32 [128], P('fsdp'), may hold values from 1 to 16
- lengths: int32 [128], P('fsdp'), may hold values from 273 to 280
- attn_gain: float32 [4096], replicated, may hold values from 0.5 to 1.5
- w_query: bfloat16 [4096, 2048], P('fsdp', 'seq'), may hold values from -1 to 1
- w_key: bfloat16 [4096, 2048], P('fsdp', 'seq'), may hold values from -1 to 1
- w_value: bfloat16 [4096, 2048], P('fsdp', 'seq'), may hold values from -0.09375 to 0.09375
- w_out: bfloat16 [2048, 4096], P(None, 'fsdp'), may hold values from -0.125 to 0.125
- final_gain: float32 [4096], replicated, may hold values from 0.25 to 1.75
- lm_head: bfloat16 [4096, 32000], P(None, 'fsdp'), may hold values from -0.25 to 0.25
Outputs:
- state_rms: float32 [128], P('seq')
- max_logit: float32 [128], P('seq')
Inputs may be any that keep to these rules, and one draw needn't show every extreme that they name: `vision_request`: within the 128 vision tokens of one index of fsdp no request is named more than 2 times, a bound that some block reaches; every request is named by some vision token. `lengths`: each request's image tokens end before its last token.
All inputs are finite; a program needn't handle non-finite values.
Results may differ from a plain program's by a relative error of at most 0.0024.
Values may be sent and summed in bfloat16 or wider, within the bound.
No kernel may reach another device: no remote copies, remote signals or barrier semaphores. Data moves between devices by JAX's collectives and lax.ppermute only.
A program may use at most 128 MiB of HBM per device.

v0:
```python
import math

import jax
import jax.numpy as jnp
from jax import lax
from jax.sharding import PartitionSpec as P

HD = 128


norm_epsilon = 1e-05


def row_norm(rows, gain):
    widened = rows.astype(jnp.float32)
    return (
        widened
        * lax.rsqrt(jnp.mean(widened * widened, axis=1, keepdims=True) + norm_epsilon)
        * gain
    ).astype(jnp.bfloat16)


def pack_slots(tokens, destination, slot_index, groups, capacity):
    return (
        jnp.zeros((groups, capacity, tokens.shape[1]), jnp.bfloat16)
        .at[destination, slot_index]
        .set(tokens)
    )


def local(
    text_embeds,
    vision_tokens,
    vision_request,
    image_start,
    lengths,
    attn_gain,
    w_query,
    w_key,
    w_value,
    w_out,
    final_gain,
    lm_head,
):
    groups = lax.axis_size("fsdp")
    seq_count = lax.axis_size("seq")
    group_index = lax.axis_index("fsdp")
    seq_index = lax.axis_index("seq")
    seq_len = text_embeds.shape[0]
    width = text_embeds.shape[1]
    columns = w_key.shape[1]
    dpiece = width // groups
    quarter = groups // seq_count
    capacity = max(2, 2 * vision_tokens.shape[0] // groups)
    last_index = lengths[0] - 1
    final_text = lax.dynamic_slice_in_dim(text_embeds, last_index, 1, 0)
    text_pieces = final_text.reshape(groups, dpiece)
    destination = vision_request[:, 0]
    onehot = (destination[:, None] == jnp.arange(groups, dtype=jnp.int32)[None, :]).astype(
        jnp.int32
    )
    slot_index = jnp.sum((jnp.cumsum(onehot, axis=0) - onehot) * onehot, axis=1)
    counts = jnp.sum(onehot, axis=0)
    full_vision = lax.all_gather(vision_tokens, "seq", axis=1, tiled=True)
    outbox = pack_slots(full_vision, destination, slot_index, groups, capacity)
    received, arrived, text_part = (
        lax.all_to_all(outbox, "fsdp", split_axis=0, concat_axis=0, tiled=True),
        lax.all_to_all(counts[:, None], "fsdp", split_axis=0, concat_axis=0, tiled=True),
        lax.all_to_all(text_pieces, "fsdp", split_axis=0, concat_axis=0, tiled=True),
    )
    occupied = (
        (jnp.arange(capacity, dtype=jnp.int32)[None, :] < arrived).astype(jnp.int32).reshape(-1)
    )
    ranking = jnp.cumsum(occupied) - occupied
    positions = jnp.where(occupied > 0, image_start[0] + ranking, seq_len)
    states = text_embeds.at[positions].set(received.reshape(-1, width), mode="drop")
    normed = row_norm(states, attn_gain)
    last_row = lax.dynamic_slice_in_dim(normed, last_index, 1, 0)
    query_sum = jnp.dot(
        last_row,
        lax.all_gather(w_query, "fsdp", axis=0, tiled=True),
        preferred_element_type=jnp.float32,
    )
    key_sum = jnp.dot(
        normed,
        lax.all_gather(w_key, "fsdp", axis=0, tiled=True),
        preferred_element_type=jnp.float32,
    )
    value_sum = jnp.dot(
        normed,
        lax.all_gather(w_value, "fsdp", axis=0, tiled=True),
        preferred_element_type=jnp.float32,
    )
    heads_local = columns // HD
    query_heads = query_sum.astype(jnp.bfloat16).reshape(heads_local, HD)
    key_heads = key_sum.astype(jnp.bfloat16).reshape(seq_len, heads_local, HD)
    value_heads = value_sum.astype(jnp.bfloat16).reshape(seq_len, heads_local, HD)
    scores = jnp.einsum(
        "hc,jhc->hj", query_heads, key_heads, preferred_element_type=jnp.float32
    ) / math.sqrt(HD)
    live_keys = jnp.arange(seq_len, dtype=jnp.int32) < lengths[0]
    scores = jnp.where(live_keys[None, :], scores, -jnp.inf)
    peak = jnp.max(scores, axis=1, keepdims=True)
    shifted = jnp.exp(scores - peak)
    weights = (shifted / jnp.sum(shifted, axis=1, keepdims=True)).astype(jnp.bfloat16)
    attended = (
        jnp.einsum("hj,jhc->hc", weights, value_heads, preferred_element_type=jnp.float32)
        .astype(jnp.bfloat16)
        .reshape(1, columns)
    )
    gathered = lax.all_gather(attended, ("fsdp", "seq"), axis=0, tiled=True)
    attended_all = gathered.reshape(groups, seq_count * columns)
    attended_mine = lax.dynamic_slice_in_dim(attended_all, seq_index * quarter, quarter, 0)
    text_mine = lax.dynamic_slice_in_dim(text_part, seq_index * quarter, quarter, 0)
    residual_out = text_mine.astype(jnp.float32) + jnp.dot(
        attended_mine, w_out, preferred_element_type=jnp.float32
    )
    gain_part = lax.dynamic_slice_in_dim(final_gain, group_index * dpiece, dpiece, 0)
    scaled_out = (residual_out * gain_part[None, :]).astype(jnp.bfloat16)
    square_part = jnp.sum(residual_out * residual_out, axis=1)[None, :]
    full_scaled, square_parts = (
        lax.all_gather(scaled_out, "fsdp", axis=1, tiled=True),
        lax.all_gather(square_part.astype(jnp.bfloat16), "fsdp", axis=0, tiled=True).astype(
            square_part.dtype
        ),
    )
    mean_square = jnp.sum(square_parts, axis=0) / width
    logits = jnp.dot(full_scaled, lm_head, preferred_element_type=jnp.float32)
    local_max = jnp.max(logits, axis=1) * lax.rsqrt(mean_square + norm_epsilon)
    max_logit = lax.pmax(local_max, "fsdp")
    return (jnp.sqrt(mean_square), max_logit)


def solution(mesh):
    return jax.shard_map(
        local,
        mesh=mesh,
        in_specs=(
            P("fsdp", None),
            P("fsdp", "seq"),
            P("fsdp", None),
            P("fsdp"),
            P("fsdp"),
            P(),
            P("fsdp", "seq"),
            P("fsdp", "seq"),
            P("fsdp", "seq"),
            P(None, "fsdp"),
            P(),
            P(None, "fsdp"),
        ),
        out_specs=(P("seq"), P("seq")),
        check_vma=False,
    )
```

profile of v0, /device:TPU:1, one launch (start us, length us, event | category | flops | bytes accessed | tf_op | source)
XLA Modules:
  0.0 1028.2 jit_solution(9507899567333681766)
XLA Ops:
  7.2 0.0 copy-start
  7.2 0.0 all-gather.7.cloned.1.call-start
  7.2 3.4 copy.58
  10.7 0.0 all-gather.7.cloned.1.call-update
  10.7 0.0 all-gather.9.cloned.1.call-start
  10.7 0.7 all-gather.9.cloned.1.call-update
  11.4 0.0 all-gather.11.cloned.1.call-start
  11.5 0.7 all-gather.11.cloned.1.call-update
  12.2 0.0 all-gather.13.cloned.1.call-start
  12.2 0.5 all-gather.13.cloned.1.call-update
  12.8 0.1 fusion.12
  12.9 0.2 reduce_window_sum.35
  13.0 0.2 select_reduce_fusion
  13.2 0.7 copy.23
  13.9 18.4 %all-to-all-start.1 = ((s32[128,1,1]{2,1,0:T(1,128)}), s32[128,1,1]{2,1,0:T(1,128)S(1)}, u32[]{:S(2)}, u32[]{:S(2)}) async-start(s32[128,1,1]{2,1,0:T(1,128)} %copy.23), calls=%async_computation.1 | async-start | bytes 131072 | tf_op jit(solution)/shard_map/all_to_all | solution.py:68
  33.0 0.9 dynamic-slice_reduce_fusion
  33.9 0.7 all_to_all.20
  34.6 9.2 all-to-all-done.1
  43.8 5.7 all-to-all-start
  49.5 0.0 all-gather.7.cloned.1.call-done
  49.5 3.4 broadcast_in_dim.20
  53.0 30.0 %scatter_fusion = bf16[128,2,4096]{2,1,0:T(2,128)(2,1)} fusion(bf16[128,2,4096]{2,1,0:T(2,128)(2,1)} %broadcast_in_dim.20, s32[128]{0:T(128)S(1)} %fusion.27, bf16[128,4096]{1,0:T(8,128)(2,1)S(1)} %copy-done.2), kind=kCustom, calls=%fused_computation | custom fusion | bytes 3146752 | tf_op jit(solution)/shard_map/scatter | solution.py:27
  82.9 14.3 %all-to-all-start.2 = ((bf16[128,2,4096]{2,1,0:T(2,128)(2,1)}), bf16[128,2,4096]{2,1,0:T(2,128)(2,1)}, u32[]{:S(2)}, u32[]{:S(2)}) async-start(bf16[128,2,4096]{2,1,0:T(2,128)(2,1)} %scatter_fusion), calls=%async_computation.2 | async-start | bytes 4194304 | tf_op jit(solution)/shard_map/all_to_all | solution.py:67
  97.2 0.1 lt.93
  98.0 0.8 dynamic_slice.19
  98.8 1.3 dynamic-slice.1
  100.7 2.4 reduce.1
  103.0 0.1 lt.95
  103.1 0.1 lt.96
  103.2 0.2 lt.97
  103.4 0.3 reduce-window.9
  103.7 0.1 slice.7
  103.8 0.1 fusion.13
  103.9 0.1 reshape.167
  104.0 0.1 slice_reduce_fusion
  104.1 0.1 broadcast_add_fusion
  104.2 0.1 copy.30
  104.3 48.4 %all-to-all-done.2 = bf16[128,2,4096]{2,1,0:T(2,128)(2,1)} async-done(((bf16[128,2,4096]{2,1,0:T(2,128)(2,1)}), bf16[128,2,4096]{2,1,0:T(2,128)(2,1)}, u32[]{:S(2)}, u32[]{:S(2)}) %all-to-all-start.2) | async-done | bytes 2097184 | tf_op jit(solution)/shard_map/all_to_all | solution.py:67
  152.8 4.1 reshape.178
  156.9 7.8 scatter_fusion.1
  164.7 2.3 fusion
  167.1 2.1 fusion.2
  169.2 2.9 fusion.15
  172.1 80.4 %all-gather.11.cloned.1.call-done = bf16[4096,512]{1,0:T(8,128)(2,1)} async-done(((bf16[32,512]{1,0:T(8,128)(2,1)}), bf16[4096,512]{1,0:T(8,128)(2,1)}) %all-gather.11.cloned.1.call-update) | async-done | bytes 4194320 | tf_op jit(solution)/shard_map/all_gather | solution.py:86
  252.5 4.2 fusion.3
  256.7 0.2 fusion.8
  256.9 0.1 fusion.23
  257.0 0.2 fusion.20
  257.2 0.1 fusion.21
  257.3 79.7 %all-gather.13.cloned.1.call-done = bf16[4096,512]{1,0:T(8,128)(2,1)} async-done(((bf16[32,512]{1,0:T(8,128)(2,1)}), bf16[4096,512]{1,0:T(8,128)(2,1)}) %all-gather.13.cloned.1.call-update) | async-done | bytes 4194320 | tf_op jit(solution)/shard_map/all_gather | solution.py:91
  337.0 4.2 fusion.4
  341.2 0.0 copy-start.3
  341.2 0.1 fusion.5
  341.4 123.1 %all-gather.1 = bf16[512,1,512]{2,1,0:T(2,128)(2,1)S(1)} all-gather(bf16[1,1,512]{2,1,0:T(2,128)(2,1)S(1)} %reshape.187), channel_id=1, replica_groups=mesh['fsdp'=128,'seq'=4] {'fsdp','seq'}, dimensions={0}, use_global_device_ids=true | all-gather | bytes 525312 | tf_op jit(solution)/shard_map/all_gather | solution.py:111
  464.5 4.0 reduce.4
  468.4 1.4 reshape.165
  469.8 0.2 multiply_convert_fusion
  470.0 49.6 %all_gather.27 = bf16[32,4096]{0,1:T(8,128)(2,1)S(1)} all-gather(bf16[32,32]{0,1:T(8,128)(2,1)S(1)} %get-tuple-element.4), channel_id=1, replica_groups=mesh['fsdp'=128,'seq'=4] {'fsdp'}, dimensions={1}, use_global_device_ids=true | all-gather | bytes 264192 | tf_op jit(solution)/shard_map/all_gather | solution.py:122
  519.7 0.2 dynamic-update-slice
  519.9 250.5 %all-reduce = bf16[4096]{0:T(1024)(128)(2,1)S(1)} all-reduce(bf16[4096]{0:T(1024)(128)(2,1)S(1)} %dynamic-update-slice), channel_id=2, replica_groups=mesh['fsdp'=128,'seq'=4] {'fsdp'}, use_global_device_ids=true, to_apply=%add | all-reduce | flops 4096 | bytes 16384
  770.4 0.1 reshape.183
  770.5 0.6 convolution_reduce_fusion
  771.1 0.5 rsqrt_multiply_fusion
  771.7 250.0 %pmax.7 = f32[32]{0:T(128)} all-reduce(f32[32]{0:T(128)S(1)} %get-tuple-element.6), channel_id=1, replica_groups=mesh['fsdp'=128,'seq'=4] {'fsdp'}, use_global_device_ids=true, to_apply=%region_13.14 | all-reduce | flops 32 | bytes 256 | tf_op jit(solution)/shard_map/pmax | solution.py:130
  (25 shorter events, 0.2 us)
Async XLA Ops:
  7.2 763.3 %copy-start = (bf16[4096,250]{1,0:T(8,128)(2,1)S(1)}, bf16[4096,250]{1,0:T(8,128)(2,1)}, u32[]{:S(2)}) copy-start(bf16[4096,250]{1,0:T(8,128)(2,1)} %param.23) | copy-start | bytes 6144004
  7.2 5.6 copy-start.5
  7.2 42.3 %all-gather.7.cloned.1.call-start = ((), (), s32[]{:S(2)}) async-start(), calls=%async_computation.3 | async-start | bytes 1310720 | tf_op jit(solution)/shard_map/all_gather | solution.py:64
  10.7 158.5 %all-gather.9.cloned.1.call-start = ((), (), s32[]{:S(2)}) async-start(), calls=%async_computation.4 | async-start | bytes 4227072 | tf_op jit(solution)/shard_map/all_gather | solution.py:81
  11.4 241.0 %all-gather.11.cloned.1.call-start = ((), (), s32[]{:S(2)}) async-start(), calls=%async_computation.5 | async-start | bytes 4227072 | tf_op jit(solution)/shard_map/all_gather | solution.py:86
  12.2 324.8 %all-gather.13.cloned.1.call-start = ((), (), s32[]{:S(2)}) async-start(), calls=%async_computation.6 | async-start | bytes 4227072 | tf_op jit(solution)/shard_map/all_gather | solution.py:91
  13.9 29.9 %all-to-all-start.1 = ((s32[128,1,1]{2,1,0:T(1,128)}), s32[128,1,1]{2,1,0:T(1,128)S(1)}, u32[]{:S(2)}, u32[]{:S(2)}) async-start(s32[128,1,1]{2,1,0:T(1,128)} %copy.23), calls=%async_computation.1 | async-start | bytes 131072 | tf_op jit(solution)/shard_map/all_to_all | solution.py:68
  43.8 39.1 %all-to-all-start = ((bf16[128,1,32]{2,1,0:T(2,128)(2,1)}), bf16[128,1,32]{2,1,0:T(2,128)(2,1)S(1)}, u32[]{:S(2)}, u32[]{:S(2)}) async-start(bf16[128,1,32]{2,1,0:T(2,128)(2,1)} %all_to_all.20), calls=%async_computation | async-start | bytes 131072 | tf_op jit(solution)/shard_map/all_to_all | solution.py:69
  49.5 3.4 copy-start.2
  82.9 69.9 %all-to-all-start.2 = ((bf16[128,2,4096]{2,1,0:T(2,128)(2,1)}), bf16[128,2,4096]{2,1,0:T(2,128)(2,1)}, u32[]{:S(2)}, u32[]{:S(2)}) async-start(bf16[128,2,4096]{2,1,0:T(2,128)(2,1)} %scatter_fusion), calls=%async_computation.2 | async-start | bytes 4194304 | tf_op jit(solution)/shard_map/all_to_all | solution.py:67
  156.9 10.2 copy-start.4
  164.7 2.3 copy-start.1
  341.2 128.6 %copy-start.3 = (bf16[2048,32]{0,1:T(8,128)(2,1)S(1)}, bf16[2048,32]{0,1:T(8,128)(2,1)}, u32[]{:S(2)}) copy-start(bf16[2048,32]{0,1:T(8,128)(2,1)} %param.21) | copy-start | bytes 393220
Sparse Core Ops, SparseCore 0:
  10.8 33.8 all-gather.6
  47.8 118.9 all-gather.8
  170.0 82.4 all-gather.10
  255.4 81.4 all-gather.12
where the time goes:
time: 1030 us
  blocking collectives  673 us (65%)
  waiting for transfers between devices  220 us (21%)
  local copies, waits for them, and re-layouts  55.8 us (5%)
  starting transfers between devices  38.5 us (4%)
  between operations  15.9 us (2%)
  other arithmetic  12.7 us (1%)
  matrix products  12.4 us (1%)
    unnamed x1, blocking collectives  251 us
    pmax x1, blocking collectives, local(): max_logit = lax.pmax(local_max, 'fsdp')  250 us
    all_gather x1, blocking collectives, local(): gathered = lax.all_gather(attended, ('fsdp', 'seq'), axis=0, tiled=True)  123 us
    all_gather x1, waiting for transfers between devices, local(): lax.all_gather(w_key, 'fsdp', axis=0, tiled=True)  80.4 us
    all_gather x1, waiting for transfers between devices, local(): lax.all_gather(w_value, 'fsdp', axis=0, tiled=True)  79.7 us
    all_gather x1, blocking collectives, local(): lax.all_gather(scaled_out, 'fsdp', axis=1, tiled=True)  49.6 us
    all_to_all x1, waiting for transfers between devices, local(): lax.all_to_all(outbox, 'fsdp', split_axis=0, concat_axis=0, tiled=True)  48.4 us
    scatter x1, local copies, waits for them, and re-layouts, pack_slots(): return jnp.zeros((groups, capacity, tokens.shape[1]), jnp.bfloat16).at[de...  30 us
  transfers between devices with their start and end apart: 7, of which 4 were waited for; matrix products, arithmetic and copies ran while one was open for 6% of the time, Pallas kernels for 0%

commit v1 on v0

--- a/solution.py
+++ b/solution.py
@@ -26,6 +26,11 @@
         .at[destination, slot_index]
         .set(tokens)
     )
+
+
+def gather_by_exchange(piece, axis_name, count):
+    spread = jnp.broadcast_to(piece[None], (count,) + piece.shape)
+    return lax.all_to_all(spread, axis_name, split_axis=0, concat_axis=0, tiled=True)
 
 
 def local(
@@ -108,26 +113,20 @@
         .astype(jnp.bfloat16)
         .reshape(1, columns)
     )
-    gathered = lax.all_gather(attended, ("fsdp", "seq"), axis=0, tiled=True)
-    attended_all = gathered.reshape(groups, seq_count * columns)
-    attended_mine = lax.dynamic_slice_in_dim(attended_all, seq_index * quarter, quarter, 0)
+    attended_seq = gather_by_exchange(attended[0], "fsdp", groups)
+    out_rows = lax.dynamic_slice_in_dim(w_out, seq_index * columns, columns, 0)
+    partial_out = jnp.dot(attended_seq, out_rows, preferred_element_type=jnp.float32)
+    out_mine = lax.psum_scatter(partial_out, "seq", scatter_dimension=0, tiled=True)
     text_mine = lax.dynamic_slice_in_dim(text_part, seq_index * quarter, quarter, 0)
-    residual_out = text_mine.astype(jnp.float32) + jnp.dot(
-        attended_mine, w_out, preferred_element_type=jnp.float32
-    )
-    gain_part = lax.dynamic_slice_in_dim(final_gain, group_index * dpiece, dpiece, 0)
-    scaled_out = (residual_out * gain_part[None, :]).astype(jnp.bfloat16)
-    square_part = jnp.sum(residual_out * residual_out, axis=1)[None, :]
-    full_scaled, square_parts = (
-        lax.all_gather(scaled_out, "fsdp", axis=1, tiled=True),
-        lax.all_gather(square_part.astype(jnp.bfloat16), "fsdp", axis=0, tiled=True).astype(
-            square_part.dtype
-        ),
-    )
-    mean_square = jnp.sum(square_parts, axis=0) / width
-    logits = jnp.dot(full_scaled, lm_head, preferred_element_type=jnp.float32)
+    residual_out = text_mine.astype(jnp.float32) + out_mine
+    residual_all = gather_by_exchange(residual_out, "fsdp", groups)
+    last_state = jnp.transpose(residual_all, (1, 0, 2)).reshape(quarter, width)
+    mean_square = jnp.mean(last_state * last_state, axis=1)
+    scaled_out = (last_state * final_gain[None, :]).astype(jnp.bfloat16)
+    logits = jnp.dot(scaled_out, lm_head, preferred_element_type=jnp.float32)
     local_max = jnp.max(logits, axis=1) * lax.rsqrt(mean_square + norm_epsilon)
-    max_logit = lax.pmax(local_max, "fsdp")
+    max_all = gather_by_exchange(local_max, "fsdp", groups)
+    max_logit = jnp.max(max_all, axis=0)
     return (jnp.sqrt(mean_square), max_logit)
 
 

time: 1030 us -> 476 us (0.46)
  blocking collectives: 673 us -> 53.5 us
  waiting for transfers between devices: 220 us -> 262 us
  starting transfers between devices: 38.5 us -> 49.1 us
    unnamed x1 -> x0, blocking collectives: 251 us -> none
    pmax x1 -> x0, blocking collectives: 250 us -> none  [local(): max_logit = lax.pmax(local_max, 'fsdp')]
    all_gather x2 -> x0, blocking collectives: 173 us -> none  [the longest x1 123 us: local(): gathered = lax.all_gather(attended, ('fsdp', 'seq'), axis=0, tiled=True)]
    all_to_all x0 -> x2, blocking collectives: none -> 53.5 us  [gather_by_exchange(): lax.all_to_all(spread, axis_name, split_axis=0, concat_axis=0, tiled=True)]
    reduce_scatter x0 -> x1, waiting for transfers between devices: none -> 16 us  [local(): lax.psum_scatter(partial_out, 'seq', scatter_dimension=0, tiled=True)]
    all_gather x1, waiting for transfers between devices: 0.02 us -> 12.3 us  [local(): full_vision = lax.all_gather(vision_tokens, 'seq', axis=1, tiled=True)]
    all_to_all x0 -> x1, waiting for transfers between devices: none -> 12 us  [gather_by_exchange(): lax.all_to_all(spread, axis_name, split_axis=0, concat_axis=0, tiled=True)]
  transfers between devices with their start and end apart: 7 -> 9, of which waited for: 4 -> 7; matrix products, arithmetic and copies ran while one was open for 6% -> 14% of each run, Pallas kernels for 0% -> 0%
where the time goes in v1:
time: 476 us; the launch traced here: 475 us
  waiting for transfers between devices  262 us (55%)
  local copies, waits for them, and re-layouts  65.2 us (14%)
  blocking collectives  53.5 us (11%)
  starting transfers between devices  49.1 us (10%)
  other arithmetic  15.5 us (3%)
  between operations  15.3 us (3%)
  matrix products  13.7 us (3%)
    all_gather x1, waiting for transfers between devices, local(): lax.all_gather(w_key, 'fsdp', axis=0, tiled=True)  81.2 us
    all_gather x1, waiting for transfers between devices, local(): lax.all_gather(w_value, 'fsdp', axis=0, tiled=True)  79.7 us
    all_to_all x2, blocking collectives, gather_by_exchange(): lax.all_to_all(spread, axis_name, split_axis=0, concat_axis=0, tiled=True)  53.5 us
    all_to_all x1, waiting for transfers between devices, local(): lax.all_to_all(outbox, 'fsdp', split_axis=0, concat_axis=0, tiled=True)  49.1 us
    scatter x1, local copies, waits for them, and re-layouts, pack_slots(): return jnp.zeros((groups, capacity, tokens.shape[1]), jnp.bfloat16).at[de...  29.9 us
    all_to_all x1, starting transfers between devices, local(): lax.all_to_all(counts[:, None], 'fsdp', split_axis=0, concat_axis=0, tile...  18.4 us
    reduce_scatter x1, waiting for transfers between devices, local(): lax.psum_scatter(partial_out, 'seq', scatter_dimension=0, tiled=True)  16 us
    all_to_all x1, starting transfers between devices, local(): lax.all_to_all(outbox, 'fsdp', split_axis=0, concat_axis=0, tiled=True)  15.7 us
  transfers between devices with their start and end apart: 9, of which 7 were waited for; matrix products, arithmetic and copies ran while one was open for 14% of the time, Pallas kernels for 0%

profile of v1, /device:TPU:1, one launch (start us, length us, event | category | flops | bytes accessed | tf_op | source)
XLA Modules:
  0.0 474.6 jit_solution(8419667173884650167)
XLA Ops:
  7.2 3.4 copy.73
  10.7 0.7 all-gather.7.cloned.1.call-update
  11.5 0.7 all-gather.9.cloned.1.call-update
  12.2 0.5 all-gather.11.cloned.1.call-update
  12.8 0.1 fusion.15
  12.9 0.2 reduce_window_sum.35
  13.0 0.2 select_reduce_fusion
  13.2 0.7 copy.28
  13.9 18.4 %all-to-all-start.1 = ((s32[128,1,1]{2,1,0:T(1,128)}), s32[128,1,1]{2,1,0:T(1,128)S(1)}, u32[]{:S(2)}, u32[]{:S(2)}) async-start(s32[128,1,1]{2,1,0:T(1,128)} %copy.28), calls=%async_computation.1 | async-start | bytes 131072 | tf_op jit(solution)/shard_map/all_to_all | solution.py:73
  32.4 12.3 %all-gather.5.cloned.1.call-done = bf16[128,4096]{1,0:T(8,128)(2,1)} async-done(((bf16[128,1024]{1,0:T(8,128)(2,1)}), bf16[128,4096]{1,0:T(8,128)(2,1)}) %all-gather.5.cloned.1.call-update) | async-done | bytes 1048592 | tf_op jit(solution)/shard_map/all_gather | solution.py:69
  44.7 3.4 broadcast_in_dim.28
  48.1 29.9 %scatter_fusion = bf16[128,2,4096]{2,1,0:T(2,128)(2,1)} fusion(bf16[128,2,4096]{2,1,0:T(2,128)(2,1)} %broadcast_in_dim.28, s32[128]{0:T(128)S(1)} %fusion.31, bf16[128,4096]{1,0:T(8,128)(2,1)S(1)} %copy-done.3), kind=kCustom, calls=%fused_computation | custom fusion | bytes 3146752 | tf_op jit(solution)/shard_map/scatter | solution.py:27
  78.1 15.7 %all-to-all-start.2 = ((bf16[128,2,4096]{2,1,0:T(2,128)(2,1)}), bf16[128,2,4096]{2,1,0:T(2,128)(2,1)}, u32[]{:S(2)}, u32[]{:S(2)}) async-start(bf16[128,2,4096]{2,1,0:T(2,128)(2,1)} %scatter_fusion), calls=%async_computation.2 | async-start | bytes 4194304 | tf_op jit(solution)/shard_map/all_to_all | solution.py:72
  93.7 0.1 lt.92
  95.2 0.9 dynamic-slice_reduce_fusion
  96.1 2.4 reduce.3
  98.5 0.1 lt.94
  98.6 0.2 lt.96
  98.8 0.3 reduce-window.9
  99.2 0.1 fusion.16
  99.3 0.1 reshape.177
  99.4 0.1 slice_reduce_fusion
  99.6 49.1 %all-to-all-done.2 = bf16[128,2,4096]{2,1,0:T(2,128)(2,1)} async-done(((bf16[128,2,4096]{2,1,0:T(2,128)(2,1)}), bf16[128,2,4096]{2,1,0:T(2,128)(2,1)}, u32[]{:S(2)}, u32[]{:S(2)}) %all-to-all-start.2) | async-done | bytes 2097184 | tf_op jit(solution)/shard_map/all_to_all | solution.py:72
  148.8 4.1 reshape.188
  152.9 7.8 %scatter_fusion.1 = bf16[280,4096]{1,0:T(8,128)(2,1)} fusion(bf16[280,4096]{1,0:T(8,128)(2,1)} %copy.73, s32[256]{0:T(256)S(1)} %bitcast.68, bf16[256,4096]{1,0:T(8,128)(2,1)} %reshape.188), kind=kCustom, calls=%fused_computation.1 | custom fusion | bytes 6292480 | tf_op jit(solution)/shard_map/scatter | solution.py:81
  160.7 2.3 fusion
  163.0 2.1 fusion.2
  165.2 2.9 fusion.19
  168.0 81.2 %all-gather.9.cloned.1.call-done = bf16[4096,512]{1,0:T(8,128)(2,1)} async-done(((bf16[32,512]{1,0:T(8,128)(2,1)}), bf16[4096,512]{1,0:T(8,128)(2,1)}) %all-gather.9.cloned.1.call-update) | async-done | bytes 4194320 | tf_op jit(solution)/shard_map/all_gather | solution.py:91
  249.2 4.2 fusion.3
  253.5 0.2 fusion.8
  253.6 0.1 fusion.27
  253.8 0.2 fusion.24
  254.0 0.1 fusion.25
  254.1 79.7 %all-gather.11.cloned.1.call-done = bf16[4096,512]{1,0:T(8,128)(2,1)} async-done(((bf16[32,512]{1,0:T(8,128)(2,1)}), bf16[4096,512]{1,0:T(8,128)(2,1)}) %all-gather.11.cloned.1.call-update) | async-done | bytes 4194320 | tf_op jit(solution)/shard_map/all_gather | solution.py:96
  333.7 4.2 fusion.4
  338.0 0.1 fusion.5
  338.1 0.1 broadcast_in_dim.31
  338.3 0.5 broadcast.138
  338.8 1.4 reduce.8
  340.2 0.7 reshape.203
  340.9 9.4 %all-to-all-start.3 = ((bf16[128,2,256]{2,1,0:T(2,128)(2,1)}), bf16[128,2,256]{2,1,0:T(2,128)(2,1)S(1)}, u32[]{:S(2)}, u32[]{:S(2)}) async-start(bf16[128,2,256]{2,1,0:T(2,128)(2,1)} %reshape.203), calls=%async_computation.3 | async-start | bytes 262144 | tf_op jit(solution)/shard_map/all_to_all | solution.py:33
  350.2 0.7 all_to_all.37
  351.0 12.0 %all-to-all-done.3 = bf16[128,2,256]{2,1,0:T(2,128)(2,1)S(1)} async-done(((bf16[128,2,256]{2,1,0:T(2,128)(2,1)}), bf16[128,2,256]{2,1,0:T(2,128)(2,1)S(1)}, u32[]{:S(2)}, u32[]{:S(2)}) %all-to-all-start.3) | async-done | bytes 131104 | tf_op jit(solution)/shard_map/all_to_all | solution.py:33
  363.0 5.5 %all-to-all-start = ((bf16[128,1,32]{2,1,0:T(2,128)(2,1)}), bf16[128,1,32]{2,1,0:T(2,128)(2,1)S(1)}, u32[]{:S(2)}, u32[]{:S(2)}) async-start(bf16[128,1,32]{2,1,0:T(2,128)(2,1)} %all_to_all.37), calls=%async_computation | async-start | bytes 131072 | tf_op jit(solution)/shard_map/all_to_all | solution.py:74
  368.5 0.1 reshape.204
  368.6 1.5 fusion.12
  370.2 9.8 %all-to-all-done = bf16[128,1,32]{2,1,0:T(2,128)(2,1)S(1)} async-done(((bf16[128,1,32]{2,1,0:T(2,128)(2,1)}), bf16[128,1,32]{2,1,0:T(2,128)(2,1)S(1)}, u32[]{:S(2)}, u32[]{:S(2)}) %all-to-all-start) | async-done | bytes 8224 | tf_op jit(solution)/shard_map/all_to_all | solution.py:74
  380.0 16.0 %reduce-scatter.2.cloned.1.call-done = f32[32,32]{1,0:T(8,128)} async-done(((f32[128,32]{1,0:T(8,128)}), f32[32,32]{1,0:T(8,128)}) %reduce-scatter.2.cloned.1.call-update) | async-done | bytes 4112 | tf_op jit(solution)/shard_map/reduce_scatter | solution.py:119
  396.1 0.7 convert_add_fusion
  396.8 1.6 broadcast_in_dim.32
  398.4 2.5 reshape.205
  400.9 36.9 %all_to_all.44 = f32[128,1,1024]{2,1,0:T(1,128)S(1)} all-to-all(f32[128,1,1024]{2,1,0:T(1,128)S(1)} %reshape.205), channel_id=1, replica_groups=mesh['fsdp'=128,'seq'=4] {'fsdp'}, dimensions={0} | all-to-all | bytes 1048576 | tf_op jit(solution)/shard_map/all_to_all | solution.py:33
  437.8 0.5 broadcast.139
  438.3 1.9 reduce.9
  440.2 2.0 reshape.206
  442.2 2.1 multiply_reduce_fusion
  444.3 0.1 copy-done.2
  444.4 2.6 copy.29
  447.0 2.6 reshape.175
  449.6 0.5 convolution_reduce_fusion
  450.1 0.5 rsqrt_multiply_fusion
  450.7 16.7 %all_to_all.45 = f32[128,1,32]{2,1,0:T(1,128)S(1)} all-to-all(f32[128,1,32]{2,1,0:T(1,128)S(1)} %broadcast_in_dim.33), channel_id=1, replica_groups=mesh['fsdp'=128,'seq'=4] {'fsdp'}, dimensions={0} | all-to-all | bytes 32768 | tf_op jit(solution)/shard_map/all_to_all | solution.py:33
  467.4 0.7 reduce_max.29
  (36 shorter events, 0.6 us)
Async XLA Ops:
  7.2 442.4 %copy-start = (bf16[4096,250]{1,0:T(8,128)(2,1)S(1)}, bf16[4096,250]{1,0:T(8,128)(2,1)}, u32[]{:S(2)}) copy-start(bf16[4096,250]{1,0:T(8,128)(2,1)} %param.23) | copy-start | bytes 6144004
  7.2 5.6 %copy-start.6 = (s32[128,1]{0,1:T(1,128)S(1)}, s32[128,1]{0,1:T(1,128)}, u32[]{:S(2)}) copy-start(s32[128,1]{0,1:T(1,128)} %param.14) | copy-start | bytes 1540
  7.2 37.5 %all-gather.5.cloned.1.call-start = ((), (), s32[]{:S(2)}) async-start(), calls=%async_computation.7 | async-start | bytes 1310720 | tf_op jit(solution)/shard_map/all_gather | solution.py:69
  10.7 154.5 %all-gather.7.cloned.1.call-start = ((), (), s32[]{:S(2)}) async-start(), calls=%async_computation.8 | async-start | bytes 4227072 | tf_op jit(solution)/shard_map/all_gather | solution.py:86
  11.4 237.8 %all-gather.9.cloned.1.call-start = ((), (), s32[]{:S(2)}) async-start(), calls=%async_computation.9 | async-start | bytes 4227072 | tf_op jit(solution)/shard_map/all_gather | solution.py:91
  12.2 321.5 %all-gather.11.cloned.1.call-start = ((), (), s32[]{:S(2)}) async-start(), calls=%async_computation.10 | async-start | bytes 4227072 | tf_op jit(solution)/shard_map/all_gather | solution.py:96
  13.9 64.1 %all-to-all-start.1 = ((s32[128,1,1]{2,1,0:T(1,128)}), s32[128,1,1]{2,1,0:T(1,128)S(1)}, u32[]{:S(2)}, u32[]{:S(2)}) async-start(s32[128,1,1]{2,1,0:T(1,128)} %copy.28), calls=%async_computation.1 | async-start | bytes 131072 | tf_op jit(solution)/shard_map/all_to_all | solution.py:73
  44.7 3.4 copy-start.3
  78.1 70.7 %all-to-all-start.2 = ((bf16[128,2,4096]{2,1,0:T(2,128)(2,1)}), bf16[128,2,4096]{2,1,0:T(2,128)(2,1)}, u32[]{:S(2)}, u32[]{:S(2)}) async-start(bf16[128,2,4096]{2,1,0:T(2,128)(2,1)} %scatter_fusion), calls=%async_computation.2 | async-start | bytes 4194304 | tf_op jit(solution)/shard_map/all_to_all | solution.py:72
  152.9 10.1 %copy-start.4 = (f32[4096]{0:T(1024)S(1)}, f32[4096]{0:T(1024)}, u32[]{:S(2)}) copy-start(f32[4096]{0:T(1024)} %param.17) | copy-start | bytes 49156
  160.7 2.3 copy-start.1
  340.9 22.1 %all-to-all-start.3 = ((bf16[128,2,256]{2,1,0:T(2,128)(2,1)}), bf16[128,2,256]{2,1,0:T(2,128)(2,1)S(1)}, u32[]{:S(2)}, u32[]{:S(2)}) async-start(bf16[128,2,256]{2,1,0:T(2,128)(2,1)} %reshape.203), calls=%async_computation.3 | async-start | bytes 262144 | tf_op jit(solution)/shard_map/all_to_all | solution.py:33
  363.0 17.0 %all-to-all-start = ((bf16[128,1,32]{2,1,0:T(2,128)(2,1)}), bf16[128,1,32]{2,1,0:T(2,128)(2,1)S(1)}, u32[]{:S(2)}, u32[]{:S(2)}) async-start(bf16[128,1,32]{2,1,0:T(2,128)(2,1)} %all_to_all.37), calls=%async_computation | async-start | bytes 131072 | tf_op jit(solution)/shard_map/all_to_all | solution.py:74
  368.5 27.6 %reduce-scatter.2.cloned.1.call-start = ((), (), s32[]{:S(2)}) async-start(), calls=%async_computation.11 | async-start | bytes 81920 | tf_op jit(solution)/shard_map/reduce_scatter | solution.py:119
  442.2 2.2 copy-start.2
  447.0 2.6 copy-start.5
Sparse Core Ops, SparseCore 0:
  10.8 33.8 all-gather.4
  47.8 114.6 all-gather.6
  165.7 83.4 all-gather.8
  252.2 81.4 all-gather.10
  371.8 24.2 reduce-scatter.1

commit v2 on v1

--- a/solution.py
+++ b/solution.py
@@ -20,17 +20,19 @@
     ).astype(jnp.bfloat16)
 
 
-def pack_slots(tokens, destination, slot_index, groups, capacity):
-    return (
-        jnp.zeros((groups, capacity, tokens.shape[1]), jnp.bfloat16)
-        .at[destination, slot_index]
-        .set(tokens)
-    )
+def exchange(rows, axis_name):
+    return lax.all_to_all(rows, axis_name, split_axis=0, concat_axis=0, tiled=True)
 
 
 def gather_by_exchange(piece, axis_name, count):
     spread = jnp.broadcast_to(piece[None], (count,) + piece.shape)
-    return lax.all_to_all(spread, axis_name, split_axis=0, concat_axis=0, tiled=True)
+    return exchange(spread, axis_name)
+
+
+def select_rows(selector, rows):
+    return jnp.dot(
+        selector.astype(jnp.bfloat16), rows, preferred_element_type=jnp.float32
+    ).astype(jnp.bfloat16)
 
 
 def local(
@@ -49,17 +51,37 @@
 ):
     groups = lax.axis_size("fsdp")
     seq_count = lax.axis_size("seq")
-    group_index = lax.axis_index("fsdp")
     seq_index = lax.axis_index("seq")
     seq_len = text_embeds.shape[0]
     width = text_embeds.shape[1]
     columns = w_key.shape[1]
+    heads_local = columns // HD
     dpiece = width // groups
     quarter = groups // seq_count
     capacity = max(2, 2 * vision_tokens.shape[0] // groups)
     last_index = lengths[0] - 1
+
     final_text = lax.dynamic_slice_in_dim(text_embeds, last_index, 1, 0)
-    text_pieces = final_text.reshape(groups, dpiece)
+    last_normed = row_norm(final_text, attn_gain)
+    pieces = jnp.stack(
+        [final_text.reshape(groups, dpiece), last_normed.reshape(groups, dpiece)], axis=1
+    )
+    pieces_in = exchange(pieces, "fsdp")
+    text_part = pieces_in[:, 0]
+    normed_part = pieces_in[:, 1]
+
+    query_partial = jnp.dot(normed_part, w_query, preferred_element_type=jnp.float32)
+    query_mine = jnp.sum(exchange(query_partial, "fsdp"), axis=0).astype(jnp.bfloat16)
+    query_all = gather_by_exchange(query_mine, "fsdp", groups)
+
+    query_heads = query_all.astype(jnp.float32).reshape(groups, heads_local, HD)
+    key_rows = w_key.astype(jnp.float32).reshape(dpiece, heads_local, HD)
+    probe_part = jnp.einsum(
+        "rhc,dhc->rhd", query_heads, key_rows, precision=lax.Precision.HIGHEST
+    )
+    probe_in = exchange(probe_part, "fsdp")
+    probe = jnp.transpose(probe_in, (1, 0, 2)).reshape(heads_local, width)
+
     destination = vision_request[:, 0]
     onehot = (destination[:, None] == jnp.arange(groups, dtype=jnp.int32)[None, :]).astype(
         jnp.int32
@@ -67,42 +89,33 @@
     slot_index = jnp.sum((jnp.cumsum(onehot, axis=0) - onehot) * onehot, axis=1)
     counts = jnp.sum(onehot, axis=0)
     full_vision = lax.all_gather(vision_tokens, "seq", axis=1, tiled=True)
-    outbox = pack_slots(full_vision, destination, slot_index, groups, capacity)
-    received, arrived, text_part = (
-        lax.all_to_all(outbox, "fsdp", split_axis=0, concat_axis=0, tiled=True),
-        lax.all_to_all(counts[:, None], "fsdp", split_axis=0, concat_axis=0, tiled=True),
-        lax.all_to_all(text_pieces, "fsdp", split_axis=0, concat_axis=0, tiled=True),
+    slot_of = destination * capacity + slot_index
+    outbox_select = (
+        jnp.arange(groups * capacity, dtype=jnp.int32)[:, None] == slot_of[None, :]
     )
+    outbox = select_rows(outbox_select, full_vision).reshape(groups, capacity, width)
+    received = exchange(outbox, "fsdp")
+    arrived = exchange(counts[:, None], "fsdp")
     occupied = (
         (jnp.arange(capacity, dtype=jnp.int32)[None, :] < arrived).astype(jnp.int32).reshape(-1)
     )
     ranking = jnp.cumsum(occupied) - occupied
     positions = jnp.where(occupied > 0, image_start[0] + ranking, seq_len)
-    states = text_embeds.at[positions].set(received.reshape(-1, width), mode="drop")
+    place = jnp.arange(seq_len, dtype=jnp.int32)[:, None] == positions[None, :]
+    placed = select_rows(place, received.reshape(-1, width))
+    replaced = jnp.any(place, axis=1, keepdims=True)
+    states = jnp.where(replaced, placed, text_embeds)
     normed = row_norm(states, attn_gain)
-    last_row = lax.dynamic_slice_in_dim(normed, last_index, 1, 0)
-    query_sum = jnp.dot(
-        last_row,
-        lax.all_gather(w_query, "fsdp", axis=0, tiled=True),
-        preferred_element_type=jnp.float32,
-    )
-    key_sum = jnp.dot(
-        normed,
-        lax.all_gather(w_key, "fsdp", axis=0, tiled=True),
-        preferred_element_type=jnp.float32,
-    )
+
     value_sum = jnp.dot(
         normed,
         lax.all_gather(w_value, "fsdp", axis=0, tiled=True),
         preferred_element_type=jnp.float32,
     )
-    heads_local = columns // HD
-    query_heads = query_sum.astype(jnp.bfloat16).reshape(heads_local, HD)
-    key_heads = key_sum.astype(jnp.bfloat16).reshape(seq_len, heads_local, HD)
     value_heads = value_sum.astype(jnp.bfloat16).reshape(seq_len, heads_local, HD)
-    scores = jnp.einsum(
-        "hc,jhc->hj", query_heads, key_heads, preferred_element_type=jnp.float32
-    ) / math.sqrt(HD)
+    scores = jnp.dot(
+        normed.astype(jnp.float32), probe.T, precision=lax.Precision.HIGHEST
+    ).T / math.sqrt(HD)
     live_keys = jnp.arange(seq_len, dtype=jnp.int32) < lengths[0]
     scores = jnp.where(live_keys[None, :], scores, -jnp.inf)
     peak = jnp.max(scores, axis=1, keepdims=True)
@@ -111,9 +124,10 @@
     attended = (
         jnp.einsum("hj,jhc->hc", weights, value_heads, preferred_element_type=jnp.float32)
         .astype(jnp.bfloat16)
-        .reshape(1, columns)
+        .reshape(columns)
     )
-    attended_seq = gather_by_exchange(attended[0], "fsdp", groups)
+
+    attended_seq = gather_by_exchange(attended, "fsdp", groups)
     out_rows = lax.dynamic_slice_in_dim(w_out, seq_index * columns, columns, 0)
     partial_out = jnp.dot(attended_seq, out_rows, preferred_element_type=jnp.float32)
     out_mine = lax.psum_scatter(partial_out, "seq", scatter_dimension=0, tiled=True)

time: 476 us -> 318 us (0.67)
  waiting for transfers between devices: 262 us -> 116 us
  local copies, waits for them, and re-layouts: 65.2 us -> 27.3 us
  blocking collectives: 53.5 us -> 83.2 us
  starting transfers between devices: 49.1 us -> 42.1 us
    all_gather x2 -> x0, waiting for transfers between devices: 81.2 us -> none  [the longest x1 81.2 us: local(): lax.all_gather(w_key, 'fsdp', axis=0, tiled=True)]
    all_gather x1, waiting for transfers between devices: 79.7 us -> 0.02 us  [local(): lax.all_gather(w_value, 'fsdp', axis=0, tiled=True)]
    scatter x2 -> x0, local copies, waits for them, and re-layouts: 37.7 us -> none  [the longest x1 29.9 us: pack_slots(): return jnp.zeros((groups, capacity, tokens.shape[1]), jnp.bfloat16).at[de...]
    all_to_all x2 -> x3, blocking collectives: 53.5 us -> 83.2 us  [exchange(): lax.all_to_all(rows, axis_name, split_axis=0, concat_axis=0, tiled=True)]
    all_to_all x4 -> x6, waiting for transfers between devices: 71 us -> 98.8 us  [exchange(): lax.all_to_all(rows, axis_name, split_axis=0, concat_axis=0, tiled=True)]
    all_gather x1, waiting for transfers between devices: 12.3 us -> 0.02 us  [local(): full_vision = lax.all_gather(vision_tokens, 'seq', axis=1, tiled=True)]
    all_to_all x4 -> x6, starting transfers between devices: 48.9 us -> 42 us  [exchange(): lax.all_to_all(rows, axis_name, split_axis=0, concat_axis=0, tiled=True)]
    dot_general x3 -> x5, matrix products: 7.27 us -> 9.84 us  [the longest x2 6.62 us: select_rows(): jnp.dot(selector.astype(jnp.bfloat16), rows, preferred_element_type=jnp.f...]
  transfers between devices with their start and end apart: 9 -> 9, of which waited for: 7 -> 7; matrix products, arithmetic and copies ran while one was open for 14% -> 11% of each run, Pallas kernels for 0% -> 0%
where the time goes in v2:
time: 318 us; the launch traced here: 316 us
  waiting for transfers between devices  116 us (36%)
  blocking collectives  83.2 us (26%)
  starting transfers between devices  42.1 us (13%)
  local copies, waits for them, and re-layouts  27.3 us (9%)
  matrix products  16.4 us (5%)
  between operations  16.1 us (5%)
  other arithmetic  15.7 us (5%)
    all_to_all x6, waiting for transfers between devices, exchange(): lax.all_to_all(rows, axis_name, split_axis=0, concat_axis=0, tiled=True)  98.8 us
    all_to_all x3, blocking collectives, exchange(): lax.all_to_all(rows, axis_name, split_axis=0, concat_axis=0, tiled=True)  83.2 us
    all_to_all x6, starting transfers between devices, exchange(): lax.all_to_all(rows, axis_name, split_axis=0, concat_axis=0, tiled=True)  42 us
    reduce_scatter x1, waiting for transfers between devices, local(): lax.psum_scatter(partial_out, 'seq', scatter_dimension=0, tiled=True)  15.4 us
    unnamed x23, local copies, waits for them, and re-layouts  7.31 us
    dot_general x2, matrix products, select_rows(): jnp.dot(selector.astype(jnp.bfloat16), rows, preferred_element_type=jnp.f...  6.62 us
  transfers between devices with their start and end apart: 9, of which 7 were waited for; matrix products, arithmetic and copies ran while one was open for 11% of the time, Pallas kernels for 0%

profile of v2, /device:TPU:1, one launch (start us, length us, event | category | flops | bytes accessed | tf_op | source)
XLA Modules:
  0.0 316.4 jit_solution(192889501139038299)
XLA Ops:
  7.2 0.7 all-gather.3.cloned.1.call-update
  8.0 0.7 all-gather.5.cloned.1.call-update
  9.3 1.5 multiply_reduce_fusion.1
  11.5 0.9 fusion.30
  12.7 29.7 %all_to_all.59 = bf16[128,2,32]{2,1,0:T(2,128)(2,1)S(1)} all-to-all(bf16[128,2,32]{2,1,0:T(2,128)(2,1)S(1)} %copy.54), channel_id=1, replica_groups=mesh['fsdp'=128,'seq'=4] {'fsdp'}, dimensions={0} | all-to-all | bytes 32768 | tf_op jit(solution)/shard_map/all_to_all | solution.py:24
  42.6 1.0 convolution_bitcast_fusion
  43.6 1.0 copy.57
  44.6 5.7 %all-to-all-start.1 = ((f32[128,1,512]{2,1,0:T(1,128)}), f32[128,1,512]{2,1,0:T(1,128)S(1)}, u32[]{:S(2)}, u32[]{:S(2)}) async-start(f32[128,1,512]{2,1,0:T(1,128)} %copy.57), calls=%async_computation.1 | async-start | bytes 524288 | tf_op jit(solution)/shard_map/all_to_all | solution.py:24
  50.4 0.2 reduce_window_sum.32
  50.6 15.1 %all-to-all-done.1 = f32[128,1,512]{2,1,0:T(1,128)S(1)} async-done(((f32[128,1,512]{2,1,0:T(1,128)}), f32[128,1,512]{2,1,0:T(1,128)S(1)}, u32[]{:S(2)}, u32[]{:S(2)}) %all-to-all-start.1) | async-done | bytes 262176 | tf_op jit(solution)/shard_map/all_to_all | solution.py:24
  65.7 0.2 reduce_sum.64
  65.9 0.1 broadcast_in_dim.38
  66.0 0.5 broadcast.82
  66.5 1.3 reduce.12
  67.8 0.7 reshape.165
  68.5 5.5 %all-to-all-start.2 = ((bf16[128,2,256]{2,1,0:T(2,128)(2,1)}), bf16[128,2,256]{2,1,0:T(2,128)(2,1)S(1)}, u32[]{:S(2)}, u32[]{:S(2)}) async-start(bf16[128,2,256]{2,1,0:T(2,128)(2,1)} %reshape.165), calls=%async_computation.2 | async-start | bytes 262144 | tf_op jit(solution)/shard_map/all_to_all | solution.py:24
  74.0 0.2 fusion.20
  74.2 0.7 copy.63
  74.9 12.2 %all-to-all-done.2 = bf16[128,2,256]{2,1,0:T(2,128)(2,1)S(1)} async-done(((bf16[128,2,256]{2,1,0:T(2,128)(2,1)}), bf16[128,2,256]{2,1,0:T(2,128)(2,1)S(1)}, u32[]{:S(2)}, u32[]{:S(2)}) %all-to-all-start.2) | async-done | bytes 131104 | tf_op jit(solution)/shard_map/all_to_all | solution.py:24
  87.1 5.5 %all-to-all-start.4 = ((s32[128,1,1]{2,1,0:T(1,128)}), s32[128,1,1]{2,1,0:T(1,128)S(1)}, u32[]{:S(2)}, u32[]{:S(2)}) async-start(s32[128,1,1]{2,1,0:T(1,128)} %copy.63), calls=%async_computation.4 | async-start | bytes 131072 | tf_op jit(solution)/shard_map/all_to_all | solution.py:24
  92.7 0.2 copy.58
  92.9 0.1 convolution_bitcast_fusion.1
  93.1 0.2 copy.61
  93.2 0.8 reshape.167
  94.1 10.1 %all-to-all-done.4 = s32[128,1,1]{2,1,0:T(1,128)S(1)} async-done(((s32[128,1,1]{2,1,0:T(1,128)}), s32[128,1,1]{2,1,0:T(1,128)S(1)}, u32[]{:S(2)}, u32[]{:S(2)}) %all-to-all-start.4) | async-done | bytes 544 | tf_op jit(solution)/shard_map/all_to_all | solution.py:24
  104.2 5.8 %all-to-all-start.3 = ((f32[128,1,128]{2,1,0:T(1,128)}), f32[128,1,128]{2,1,0:T(1,128)S(1)}, u32[]{:S(2)}, u32[]{:S(2)}) async-start(f32[128,1,128]{2,1,0:T(1,128)} %reshape.167), calls=%async_computation.3 | async-start | bytes 131072 | tf_op jit(solution)/shard_map/all_to_all | solution.py:24
  110.1 3.3 %convolution_convert_fusion.1 = bf16[256,4096]{1,0:T(8,128)(2,1)} fusion(bf16[128,4096]{1,0:T(8,128)(2,1)} %all-gather.3.cloned.1.call-done, s32[128]{0:T(128)S(1)} %multiply_add_fusion), kind=kOutput, calls=%fused_computation.3 | convolution fusion | flops 269516800 | bytes 3146240 | tf_op jit(solution)/shard_map/dot_general | solution.py:33
  113.3 4.4 %reshape.152 = bf16[128,2,4096]{2,1,0:T(2,128)(2,1)} reshape(bf16[256,4096]{1,0:T(8,128)(2,1)} %convolution_convert_fusion.1) | data formatting | bytes 4194304 | tf_op jit(solution)/shard_map/reshape | solution.py:96
  117.7 4.0 %all-to-all-done.3 = f32[128,1,128]{2,1,0:T(1,128)S(1)} async-done(((f32[128,1,128]{2,1,0:T(1,128)}), f32[128,1,128]{2,1,0:T(1,128)S(1)}, u32[]{:S(2)}, u32[]{:S(2)}) %all-to-all-start.3) | async-done | bytes 65568 | tf_op jit(solution)/shard_map/all_to_all | solution.py:24
  121.7 10.3 %all-to-all-start.5 = ((bf16[128,2,4096]{2,1,0:T(2,128)(2,1)}), bf16[128,2,4096]{2,1,0:T(2,128)(2,1)}, u32[]{:S(2)}, u32[]{:S(2)}) async-start(bf16[128,2,4096]{2,1,0:T(2,128)(2,1)} %reshape.152), calls=%async_computation.5 | async-start | bytes 4194304 | tf_op jit(solution)/shard_map/all_to_all | solution.py:24
  132.9 2.4 reduce.6
  135.6 0.3 reduce-window.9
  136.4 0.2 fusion.11
  136.6 0.5 broadcast.83
  137.1 0.8 reduce.13
  137.9 0.2 reshape.168
  138.1 0.2 reshape.150
  138.3 44.7 %all-to-all-done.5 = bf16[128,2,4096]{2,1,0:T(2,128)(2,1)} async-done(((bf16[128,2,4096]{2,1,0:T(2,128)(2,1)}), bf16[128,2,4096]{2,1,0:T(2,128)(2,1)}, u32[]{:S(2)}, u32[]{:S(2)}) %all-to-all-start.5) | async-done | bytes 2097184 | tf_op jit(solution)/shard_map/all_to_all | solution.py:24
  183.0 4.1 %reshape.153 = bf16[256,4096]{1,0:T(8,128)(2,1)} reshape(bf16[128,2,4096]{2,1,0:T(2,128)(2,1)} %all-to-all-done.5) | data formatting | bytes 4194304 | tf_op jit(solution)/shard_map/reshape | solution.py:105
  187.1 3.4 %fusion.1 = (f32[280]{0:T(512)S(1)}, bf16[280,4096]{1,0:T(8,128)(2,1)S(1)}) fusion(bf16[280,4096]{1,0:T(8,128)(2,1)} %param.12, bf16[256,4096]{1,0:T(8,128)(2,1)} %reshape.153, s32[256]{0:T(256)S(1)} %compare_select_fusion, pred[280]{0:T(512)(128)(4,1)S(1)} %fusion.11), kind=kOutput, calls=%fused_computation.5 | convolution fusion | flops 593008384 | bytes 6687096 | tf_op jit(solution)/shard_map/dot_general | solution.py:33
  190.5 2.1 fusion.32
  192.6 0.2 fusion.26
  192.9 4.3 %fusion.4 = bf16[35,4,8,128]{3,2,1,0:T(8,128)(2,1)S(1)} fusion(bf16[4096,512]{1,0:T(8,128)(2,1)} %all-gather.5.cloned.1.call-done, bf16[280,4096]{1,0:T(8,128)(2,1)} %copy-done.6, f32[4096]{0:T(1024)S(1)} %copy-done.4, f32[280]{0:T(512)S(1)} %add_rsqrt_fusion), kind=kOutput, calls=%fused_computation.10 | convolution fusion | flops 1179136000 | bytes 6792288 | tf_op jit(solution)/shard_map/dot_general | solution.py:110
  197.2 0.1 fusion.8
  197.4 0.1 broadcast_in_dim.43
  197.5 1.3 reduce.14
  198.8 0.7 reshape.169
  199.5 9.1 %all-to-all-start.6 = ((bf16[128,2,256]{2,1,0:T(2,128)(2,1)}), bf16[128,2,256]{2,1,0:T(2,128)(2,1)S(1)}, u32[]{:S(2)}, u32[]{:S(2)}) async-start(bf16[128,2,256]{2,1,0:T(2,128)(2,1)} %reshape.169), calls=%async_computation.6 | async-start | bytes 262144 | tf_op jit(solution)/shard_map/all_to_all | solution.py:24
  208.6 12.7 %all-to-all-done.6 = bf16[128,2,256]{2,1,0:T(2,128)(2,1)S(1)} async-done(((bf16[128,2,256]{2,1,0:T(2,128)(2,1)}), bf16[128,2,256]{2,1,0:T(2,128)(2,1)S(1)}, u32[]{:S(2)}, u32[]{:S(2)}) %all-to-all-start.6) | async-done | bytes 131104 | tf_op jit(solution)/shard_map/all_to_all | solution.py:24
  221.4 1.5 fusion.14
  223.0 15.4 %reduce-scatter.2.cloned.1.call-done = f32[32,32]{1,0:T(8,128)} async-done(((f32[128,32]{1,0:T(8,128)}), f32[32,32]{1,0:T(8,128)}) %reduce-scatter.2.cloned.1.call-update) | async-done | bytes 4112 | tf_op jit(solution)/shard_map/reduce_scatter | solution.py:133
  238.5 0.7 convert_add_fusion
  239.2 1.6 broadcast_in_dim.44
  240.8 2.5 reshape.171
  243.3 36.9 %all_to_all.60 = f32[128,1,1024]{2,1,0:T(1,128)S(1)} all-to-all(f32[128,1,1024]{2,1,0:T(1,128)S(1)} %reshape.171), channel_id=1, replica_groups=mesh['fsdp'=128,'seq'=4] {'fsdp'}, dimensions={0} | all-to-all | bytes 1048576 | tf_op jit(solution)/shard_map/all_to_all | solution.py:24
  280.2 1.9 reduce.15
  282.1 2.0 reshape.172
  284.1 2.1 multiply_reduce_fusion
  286.3 2.6 copy.64
  288.9 2.6 reshape.155
  291.5 0.5 convolution_reduce_fusion
  292.0 0.5 rsqrt_multiply_fusion
  292.6 16.7 %all_to_all.61 = f32[128,1,32]{2,1,0:T(1,128)S(1)} all-to-all(f32[128,1,32]{2,1,0:T(1,128)S(1)} %broadcast_in_dim.45), channel_id=1, replica_groups=mesh['fsdp'=128,'seq'=4] {'fsdp'}, dimensions={0} | all-to-all | bytes 32768 | tf_op jit(solution)/shard_map/all_to_all | solution.py:24
  309.2 0.7 reduce_max.29
  (49 shorter events, 2.2 us)
Async XLA Ops:
  7.2 284.3 %copy-start = (bf16[4096,250]{1,0:T(8,128)(2,1)S(1)}, bf16[4096,250]{1,0:T(8,128)(2,1)}, u32[]{:S(2)}) copy-start(bf16[4096,250]{1,0:T(8,128)(2,1)} %param.23) | copy-start | bytes 6144004
  7.2 43.1 %copy-start.5 = (s32[128,1]{0,1:T(1,128)S(1)}, s32[128,1]{0,1:T(1,128)}, u32[]{:S(2)}) copy-start(s32[128,1]{0,1:T(1,128)} %param.14) | copy-start | bytes 1540
  7.2 102.9 %all-gather.3.cloned.1.call-start = ((), (), s32[]{:S(2)}) async-start(), calls=%async_computation.10 | async-start | bytes 1310720 | tf_op jit(solution)/shard_map/all_gather | solution.py:91
  7.9 185.0 %all-gather.5.cloned.1.call-start = ((), (), s32[]{:S(2)}) async-start(), calls=%async_computation.11 | async-start | bytes 4227072 | tf_op jit(solution)/shard_map/all_gather | solution.py:112
  12.7 80.2 %copy-start.2 = (bf16[32,512]{1,0:T(8,128)(2,1)S(1)}, bf16[32,512]{1,0:T(8,128)(2,1)}, u32[]{:S(2)}) copy-start(bf16[32,512]{1,0:T(8,128)(2,1)} %param.19) | copy-start | bytes 98308
  44.6 21.1 %all-to-all-start.1 = ((f32[128,1,512]{2,1,0:T(1,128)}), f32[128,1,512]{2,1,0:T(1,128)S(1)}, u32[]{:S(2)}, u32[]{:S(2)}) async-start(f32[128,1,512]{2,1,0:T(1,128)} %copy.57), calls=%async_computation.1 | async-start | bytes 524288 | tf_op jit(solution)/shard_map/all_to_all | solution.py:24
  68.5 18.7 %all-to-all-start.2 = ((bf16[128,2,256]{2,1,0:T(2,128)(2,1)}), bf16[128,2,256]{2,1,0:T(2,128)(2,1)S(1)}, u32[]{:S(2)}, u32[]{:S(2)}) async-start(bf16[128,2,256]{2,1,0:T(2,128)(2,1)} %reshape.165), calls=%async_computation.2 | async-start | bytes 262144 | tf_op jit(solution)/shard_map/all_to_all | solution.py:24
  87.1 17.1 %all-to-all-start.4 = ((s32[128,1,1]{2,1,0:T(1,128)}), s32[128,1,1]{2,1,0:T(1,128)S(1)}, u32[]{:S(2)}, u32[]{:S(2)}) async-start(s32[128,1,1]{2,1,0:T(1,128)} %copy.63), calls=%async_computation.4 | async-start | bytes 131072 | tf_op jit(solution)/shard_map/all_to_all | solution.py:24
  104.2 17.5 %all-to-all-start.3 = ((f32[128,1,128]{2,1,0:T(1,128)}), f32[128,1,128]{2,1,0:T(1,128)S(1)}, u32[]{:S(2)}, u32[]{:S(2)}) async-start(f32[128,1,128]{2,1,0:T(1,128)} %reshape.167), calls=%async_computation.3 | async-start | bytes 131072 | tf_op jit(solution)/shard_map/all_to_all | solution.py:24
  121.7 61.2 %all-to-all-start.5 = ((bf16[128,2,4096]{2,1,0:T(2,128)(2,1)}), bf16[128,2,4096]{2,1,0:T(2,128)(2,1)}, u32[]{:S(2)}, u32[]{:S(2)}) async-start(bf16[128,2,4096]{2,1,0:T(2,128)(2,1)} %reshape.152), calls=%async_computation.5 | async-start | bytes 4194304 | tf_op jit(solution)/shard_map/all_to_all | solution.py:24
  187.1 3.4 %copy-start.4 = (f32[4096]{0:T(1024)S(1)}, f32[4096]{0:T(1024)}, u32[]{:S(2)}) copy-start(f32[4096]{0:T(1024)} %param.17) | copy-start | bytes 49156
  190.4 2.1 copy-start.6
  199.5 21.8 %all-to-all-start.6 = ((bf16[128,2,256]{2,1,0:T(2,128)(2,1)}), bf16[128,2,256]{2,1,0:T(2,128)(2,1)S(1)}, u32[]{:S(2)}, u32[]{:S(2)}) async-start(bf16[128,2,256]{2,1,0:T(2,128)(2,1)} %reshape.169), calls=%async_computation.6 | async-start | bytes 262144 | tf_op jit(solution)/shard_map/all_to_all | solution.py:24
  208.6 29.9 %reduce-scatter.2.cloned.1.call-start = ((), (), s32[]{:S(2)}) async-start(), calls=%async_computation.12 | async-start | bytes 81920 | tf_op jit(solution)/shard_map/reduce_scatter | solution.py:133
  284.1 2.2 copy-start.1
  288.9 2.6 copy-start.3
Sparse Core Ops, SparseCore 0:
  10.1 33.8 all-gather.2
  47.2 88.4 all-gather.4
  223.1 15.3 reduce-scatter.1

commit v3 on v2

--- a/solution.py
+++ b/solution.py
@@ -61,18 +61,30 @@
     capacity = max(2, 2 * vision_tokens.shape[0] // groups)
     last_index = lengths[0] - 1
 
+    destination = vision_request[:, 0]
+    onehot = (destination[:, None] == jnp.arange(groups, dtype=jnp.int32)[None, :]).astype(
+        jnp.int32
+    )
+    slot_index = jnp.sum((jnp.cumsum(onehot, axis=0) - onehot) * onehot, axis=1)
+    counts = jnp.sum(onehot, axis=0)
+
     final_text = lax.dynamic_slice_in_dim(text_embeds, last_index, 1, 0)
     last_normed = row_norm(final_text, attn_gain)
     pieces = jnp.stack(
-        [final_text.reshape(groups, dpiece), last_normed.reshape(groups, dpiece)], axis=1
+        [
+            final_text.reshape(groups, dpiece),
+            last_normed.reshape(groups, dpiece),
+            jnp.broadcast_to(counts.astype(jnp.bfloat16)[:, None], (groups, dpiece)),
+        ],
+        axis=1,
     )
     pieces_in = exchange(pieces, "fsdp")
     text_part = pieces_in[:, 0]
     normed_part = pieces_in[:, 1]
+    arrived = pieces_in[:, 2, :1].astype(jnp.int32)
 
     query_partial = jnp.dot(normed_part, w_query, preferred_element_type=jnp.float32)
-    query_mine = jnp.sum(exchange(query_partial, "fsdp"), axis=0).astype(jnp.bfloat16)
-    query_all = gather_by_exchange(query_mine, "fsdp", groups)
+    query_all = lax.psum(query_partial, "fsdp").astype(jnp.bfloat16)
 
     query_heads = query_all.astype(jnp.float32).reshape(groups, heads_local, HD)
     key_rows = w_key.astype(jnp.float32).reshape(dpiece, heads_local, HD)
@@ -82,12 +94,6 @@
     probe_in = exchange(probe_part, "fsdp")
     probe = jnp.transpose(probe_in, (1, 0, 2)).reshape(heads_local, width)
 
-    destination = vision_request[:, 0]
-    onehot = (destination[:, None] == jnp.arange(groups, dtype=jnp.int32)[None, :]).astype(
-        jnp.int32
-    )
-    slot_index = jnp.sum((jnp.cumsum(onehot, axis=0) - onehot) * onehot, axis=1)
-    counts = jnp.sum(onehot, axis=0)
     full_vision = lax.all_gather(vision_tokens, "seq", axis=1, tiled=True)
     slot_of = destination * capacity + slot_index
     outbox_select = (
@@ -95,7 +101,6 @@
     )
     outbox = select_rows(outbox_select, full_vision).reshape(groups, capacity, width)
     received = exchange(outbox, "fsdp")
-    arrived = exchange(counts[:, None], "fsdp")
     occupied = (
         (jnp.arange(capacity, dtype=jnp.int32)[None, :] < arrived).astype(jnp.int32).reshape(-1)
     )
@@ -107,12 +112,6 @@
     states = jnp.where(replaced, placed, text_embeds)
     normed = row_norm(states, attn_gain)
 
-    value_sum = jnp.dot(
-        normed,
-        lax.all_gather(w_value, "fsdp", axis=0, tiled=True),
-        preferred_element_type=jnp.float32,
-    )
-    value_heads = value_sum.astype(jnp.bfloat16).reshape(seq_len, heads_local, HD)
     scores = jnp.dot(
         normed.astype(jnp.float32), probe.T, precision=lax.Precision.HIGHEST
     ).T / math.sqrt(HD)
@@ -121,13 +120,15 @@
     peak = jnp.max(scores, axis=1, keepdims=True)
     shifted = jnp.exp(scores - peak)
     weights = (shifted / jnp.sum(shifted, axis=1, keepdims=True)).astype(jnp.bfloat16)
-    attended = (
-        jnp.einsum("hj,jhc->hc", weights, value_heads, preferred_element_type=jnp.float32)
-        .astype(jnp.bfloat16)
-        .reshape(columns)
-    )
 
-    attended_seq = gather_by_exchange(attended, "fsdp", groups)
+    mixed = jnp.dot(weights, normed, preferred_element_type=jnp.float32)
+    mixed_pieces = jnp.transpose(mixed.reshape(heads_local, groups, dpiece), (1, 0, 2))
+    mixed_in = exchange(mixed_pieces, "fsdp")
+    value_rows = w_value.astype(jnp.float32).reshape(dpiece, heads_local, HD)
+    attended_partial = jnp.einsum(
+        "rhd,dhc->rhc", mixed_in, value_rows, precision=lax.Precision.HIGHEST
+    ).reshape(groups, columns)
+    attended_seq = lax.psum(attended_partial, "fsdp").astype(jnp.bfloat16)
     out_rows = lax.dynamic_slice_in_dim(w_out, seq_index * columns, columns, 0)
     partial_out = jnp.dot(attended_seq, out_rows, preferred_element_type=jnp.float32)
     out_mine = lax.psum_scatter(partial_out, "seq", scatter_dimension=0, tiled=True)

time: 318 us -> 1240 us (3.90)
  blocking collectives: 83.2 us -> 1030 us
  waiting for transfers between devices: 116 us -> 94.8 us
    psum x0 -> x2, blocking collectives: none -> 972 us  [the longest x1 486 us: local(): attended_seq = lax.psum(attended_partial, 'fsdp').astype(jnp.bfloat16)]
    all_to_all x3 -> x2, blocking collectives: 83.2 us -> 53.6 us  [exchange(): lax.all_to_all(rows, axis_name, split_axis=0, concat_axis=0, tiled=True)]
    all_to_all x6 -> x4, waiting for transfers between devices: 98.8 us -> 72 us  [exchange(): lax.all_to_all(rows, axis_name, split_axis=0, concat_axis=0, tiled=True)]
    all_to_all x6 -> x4, starting transfers between devices: 42 us -> 49.5 us  [exchange(): lax.all_to_all(rows, axis_name, split_axis=0, concat_axis=0, tiled=True)]
  transfers between devices with their start and end apart: 9 -> 6, of which waited for: 7 -> 5; matrix products, arithmetic and copies ran while one was open for 11% -> 2% of each run, Pallas kernels for 0% -> 0%
where the time goes in v3:
time: 1240 us
  blocking collectives  1030 us (83%)
  waiting for transfers between devices  94.8 us (8%)
  starting transfers between devices  49.6 us (4%)
  local copies, waits for them, and re-layouts  25.1 us (2%)
  between operations  16.3 us (1%)
  other arithmetic  15.6 us (1%)
  matrix products  13.1 us (1%)
    psum x1, blocking collectives, local(): attended_seq = lax.psum(attended_partial, 'fsdp').astype(jnp.bfloat16)  486 us
    psum x1, blocking collectives, local(): query_all = lax.psum(query_partial, 'fsdp').astype(jnp.bfloat16)  486 us
    all_to_all x4, waiting for transfers between devices, exchange(): lax.all_to_all(rows, axis_name, split_axis=0, concat_axis=0, tiled=True)  72 us
    all_to_all x2, blocking collectives, exchange(): lax.all_to_all(rows, axis_name, split_axis=0, concat_axis=0, tiled=True)  53.6 us
    all_to_all x4, starting transfers between devices, exchange(): lax.all_to_all(rows, axis_name, split_axis=0, concat_axis=0, tiled=True)  49.5 us
  transfers between devices with their start and end apart: 6, of which 5 were waited for; matrix products, arithmetic and copies ran while one was open for 2% of the time, Pallas kernels for 0%

profile of v3, /device:TPU:1, one launch (start us, length us, event | category | flops | bytes accessed | tf_op | source)
XLA Modules:
  0.0 1239.9 jit_solution(17929459743585523007)
XLA Ops:
  7.2 0.7 all-gather.2.cloned.1.call-update
  8.6 1.5 multiply_reduce_fusion.1
  10.8 0.9 fusion.34
  11.9 0.7 fusion.19
  12.6 0.2 reduce_window_sum.32
  12.8 0.8 fusion.21
  13.8 0.7 copy.59
  14.5 18.4 %all-to-all-start = ((bf16[128,3,32]{2,1,0:T(4,128)(2,1)}), bf16[128,3,32]{2,1,0:T(4,128)(2,1)S(1)}, u32[]{:S(2)}, u32[]{:S(2)}) async-start(bf16[128,3,32]{2,1,0:T(4,128)(2,1)} %copy.59), calls=%async_computation | async-start | bytes 262144 | tf_op jit(solution)/shard_map/all_to_all | solution.py:24
  32.9 0.7 multiply_add_fusion
  33.6 12.1 all-to-all-done
  45.7 0.1 fusion.35
  45.8 1.0 fusion.27
  46.8 485.9 %all-reduce.2 = bf16[128,512]{1,0:T(8,128)(2,1)S(1)} all-reduce(f32[128,512]{1,0:T(8,128)S(1)} %fusion.27), channel_id=1, replica_groups=mesh['fsdp'=128,'seq'=4] {'fsdp'}, use_global_device_ids=true, to_apply=%region_2.3 | all-reduce | flops 65536 | bytes 393216 | tf_op jit(solution)/shard_map/psum | solution.py:87
  532.7 0.2 convolution_bitcast_fusion
  532.8 0.2 copy.64
  533.0 0.8 reshape.161
  533.8 11.7 all-to-all-start.1
  545.6 3.2 convolution_convert_fusion.1
  548.8 4.4 reshape.146
  553.2 3.8 all-to-all-done.1
  557.0 10.4 all-to-all-start.2
  568.1 0.1 lt.59
  568.2 2.4 fusion.17
  570.6 0.1 reshape.155
  570.7 0.2 lt.62
  570.9 0.3 reduce-window.9
  571.4 0.1 reshape.154
  571.6 0.1 slice_reduce_fusion
  571.8 0.2 fusion.8
  571.9 0.5 broadcast.78
  572.4 0.8 reduce.12
  573.2 0.2 reshape.162
  573.4 0.2 reshape.144
  573.6 44.7 %all-to-all-done.2 = bf16[128,2,4096]{2,1,0:T(2,128)(2,1)} async-done(((bf16[128,2,4096]{2,1,0:T(2,128)(2,1)}), bf16[128,2,4096]{2,1,0:T(2,128)(2,1)}, u32[]{:S(2)}, u32[]{:S(2)}) %all-to-all-start.2) | async-done | bytes 2097184 | tf_op jit(solution)/shard_map/all_to_all | solution.py:24
  618.3 4.1 reshape.147
  622.4 3.3 fusion.1
  625.8 2.1 fusion.36
  627.9 0.2 fusion.29
  628.1 0.7 fusion.5
  628.9 0.1 reshape.148
  629.0 0.2 copy.66
  629.2 0.8 reshape.163
  630.0 8.9 all-to-all-start.3
  639.0 11.4 all-to-all-done.3
  650.4 0.8 reduce.13
  651.2 0.2 reshape.164
  651.4 0.4 fusion.9
  651.8 486.1 %all-reduce.3 = bf16[128,512]{0,1:T(8,128)(2,1)S(1)} all-reduce(f32[128,512]{0,1:T(8,128)S(1)} %bitcast.64), channel_id=1, replica_groups=mesh['fsdp'=128,'seq'=4] {'fsdp'}, use_global_device_ids=true, to_apply=%region_11.12 | all-reduce | flops 65536 | bytes 393216 | tf_op jit(solution)/shard_map/psum | solution.py:131
  1137.9 1.6 fusion.15
  1139.5 22.1 %reduce-scatter.2.cloned.1.call-done = f32[32,32]{1,0:T(8,128)} async-done(((f32[128,32]{1,0:T(8,128)}), f32[32,32]{1,0:T(8,128)}) %reduce-scatter.2.cloned.1.call-update) | async-done | bytes 4112 | tf_op jit(solution)/shard_map/reduce_scatter | solution.py:134
  1161.6 0.7 convert_add_fusion
  1162.3 1.6 broadcast_in_dim.35
  1164.0 2.5 reshape.165
  1166.5 36.9 %all_to_all.31 = f32[128,1,1024]{2,1,0:T(1,128)S(1)} all-to-all(f32[128,1,1024]{2,1,0:T(1,128)S(1)} %reshape.165), channel_id=1, replica_groups=mesh['fsdp'=128,'seq'=4] {'fsdp'}, dimensions={0} | all-to-all | bytes 1048576 | tf_op jit(solution)/shard_map/all_to_all | solution.py:24
  1203.4 1.9 reduce.14
  1205.3 2.0 reshape.166
  1207.3 2.1 multiply_reduce_fusion
  1209.4 0.1 copy-done.1
  1209.5 2.6 copy.69
  1212.1 2.6 reshape.151
  1214.7 0.5 convolution_reduce_fusion
  1215.2 0.5 rsqrt_multiply_fusion
  1215.8 16.7 %all_to_all.32 = f32[128,1,32]{2,1,0:T(1,128)S(1)} all-to-all(f32[128,1,32]{2,1,0:T(1,128)S(1)} %broadcast_in_dim.36), channel_id=1, replica_groups=mesh['fsdp'=128,'seq'=4] {'fsdp'}, dimensions={0} | all-to-all | bytes 32768 | tf_op jit(solution)/shard_map/all_to_all | solution.py:24
  1232.4 0.7 reduce_max.29
  (33 shorter events, 1.0 us)
Async XLA Ops:
  7.2 1207.5 %copy-start = (bf16[4096,250]{1,0:T(8,128)(2,1)S(1)}, bf16[4096,250]{1,0:T(8,128)(2,1)}, u32[]{:S(2)}) copy-start(bf16[4096,250]{1,0:T(8,128)(2,1)} %param.23) | copy-start | bytes 6144004
  7.2 525.5 %copy-start.2 = (bf16[32,512]{1,0:T(8,128)(2,1)S(1)}, bf16[32,512]{1,0:T(8,128)(2,1)}, u32[]{:S(2)}) copy-start(bf16[32,512]{1,0:T(8,128)(2,1)} %param.19) | copy-start | bytes 98308
  7.2 538.4 %all-gather.2.cloned.1.call-start = ((), (), s32[]{:S(2)}) async-start(), calls=%async_computation.7 | async-start | bytes 1310720 | tf_op jit(solution)/shard_map/all_gather | solution.py:97
  14.5 31.2 %all-to-all-start = ((bf16[128,3,32]{2,1,0:T(4,128)(2,1)}), bf16[128,3,32]{2,1,0:T(4,128)(2,1)S(1)}, u32[]{:S(2)}, u32[]{:S(2)}) async-start(bf16[128,3,32]{2,1,0:T(4,128)(2,1)} %copy.59), calls=%async_computation | async-start | bytes 262144 | tf_op jit(solution)/shard_map/all_to_all | solution.py:24
  533.8 23.2 %all-to-all-start.1 = ((f32[128,1,128]{2,1,0:T(1,128)}), f32[128,1,128]{2,1,0:T(1,128)S(1)}, u32[]{:S(2)}, u32[]{:S(2)}) async-start(f32[128,1,128]{2,1,0:T(1,128)} %reshape.161), calls=%async_computation.1 | async-start | bytes 131072 | tf_op jit(solution)/shard_map/all_to_all | solution.py:24
  557.0 61.3 %all-to-all-start.2 = ((bf16[128,2,4096]{2,1,0:T(2,128)(2,1)}), bf16[128,2,4096]{2,1,0:T(2,128)(2,1)}, u32[]{:S(2)}, u32[]{:S(2)}) async-start(bf16[128,2,4096]{2,1,0:T(2,128)(2,1)} %reshape.146), calls=%async_computation.2 | async-start | bytes 4194304 | tf_op jit(solution)/shard_map/all_to_all | solution.py:24
  622.4 3.4 copy-start.5
  628.1 23.3 %copy-start.3 = (bf16[32,512]{1,0:T(8,128)(2,1)S(1)}, bf16[32,512]{1,0:T(8,128)(2,1)}, u32[]{:S(2)}) copy-start(bf16[32,512]{1,0:T(8,128)(2,1)} %param.20) | copy-start | bytes 98308
  630.0 20.4 %all-to-all-start.3 = ((f32[128,1,128]{2,1,0:T(1,128)}), f32[128,1,128]{2,1,0:T(1,128)S(1)}, u32[]{:S(2)}, u32[]{:S(2)}) async-start(f32[128,1,128]{2,1,0:T(1,128)} %reshape.163), calls=%async_computation.3 | async-start | bytes 131072 | tf_op jit(solution)/shard_map/all_to_all | solution.py:24
  639.0 522.7 %reduce-scatter.2.cloned.1.call-start = ((), (), s32[]{:S(2)}) async-start(), calls=%async_computation.8 | async-start | bytes 81920 | tf_op jit(solution)/shard_map/reduce_scatter | solution.py:134
  1207.3 2.2 copy-start.1
  1212.1 2.6 copy-start.4
Sparse Core Ops, SparseCore 0:
  10.1 33.8 all-gather.1
  1139.6 21.9 reduce-scatter.1

commit v4 on v2

--- a/solution.py
+++ b/solution.py
@@ -61,14 +61,27 @@
     capacity = max(2, 2 * vision_tokens.shape[0] // groups)
     last_index = lengths[0] - 1
 
+    destination = vision_request[:, 0]
+    onehot = (destination[:, None] == jnp.arange(groups, dtype=jnp.int32)[None, :]).astype(
+        jnp.int32
+    )
+    slot_index = jnp.sum((jnp.cumsum(onehot, axis=0) - onehot) * onehot, axis=1)
+    counts = jnp.sum(onehot, axis=0)
+
     final_text = lax.dynamic_slice_in_dim(text_embeds, last_index, 1, 0)
     last_normed = row_norm(final_text, attn_gain)
     pieces = jnp.stack(
-        [final_text.reshape(groups, dpiece), last_normed.reshape(groups, dpiece)], axis=1
+        [
+            final_text.reshape(groups, dpiece),
+            last_normed.reshape(groups, dpiece),
+            jnp.broadcast_to(counts.astype(jnp.bfloat16)[:, None], (groups, dpiece)),
+        ],
+        axis=1,
     )
     pieces_in = exchange(pieces, "fsdp")
     text_part = pieces_in[:, 0]
     normed_part = pieces_in[:, 1]
+    arrived = pieces_in[:, 2, :1].astype(jnp.int32)
 
     query_partial = jnp.dot(normed_part, w_query, preferred_element_type=jnp.float32)
     query_mine = jnp.sum(exchange(query_partial, "fsdp"), axis=0).astype(jnp.bfloat16)
@@ -82,12 +95,6 @@
     probe_in = exchange(probe_part, "fsdp")
     probe = jnp.transpose(probe_in, (1, 0, 2)).reshape(heads_local, width)
 
-    destination = vision_request[:, 0]
-    onehot = (destination[:, None] == jnp.arange(groups, dtype=jnp.int32)[None, :]).astype(
-        jnp.int32
-    )
-    slot_index = jnp.sum((jnp.cumsum(onehot, axis=0) - onehot) * onehot, axis=1)
-    counts = jnp.sum(onehot, axis=0)
     full_vision = lax.all_gather(vision_tokens, "seq", axis=1, tiled=True)
     slot_of = destination * capacity + slot_index
     outbox_select = (
@@ -95,7 +102,6 @@
     )
     outbox = select_rows(outbox_select, full_vision).reshape(groups, capacity, width)
     received = exchange(outbox, "fsdp")
-    arrived = exchange(counts[:, None], "fsdp")
     occupied = (
         (jnp.arange(capacity, dtype=jnp.int32)[None, :] < arrived).astype(jnp.int32).reshape(-1)
     )
@@ -133,10 +139,18 @@
     out_mine = lax.psum_scatter(partial_out, "seq", scatter_dimension=0, tiled=True)
     text_mine = lax.dynamic_slice_in_dim(text_part, seq_index * quarter, quarter, 0)
     residual_out = text_mine.astype(jnp.float32) + out_mine
-    residual_all = gather_by_exchange(residual_out, "fsdp", groups)
-    last_state = jnp.transpose(residual_all, (1, 0, 2)).reshape(quarter, width)
-    mean_square = jnp.mean(last_state * last_state, axis=1)
-    scaled_out = (last_state * final_gain[None, :]).astype(jnp.bfloat16)
+    gain_part = lax.dynamic_slice_in_dim(final_gain, lax.axis_index("fsdp") * dpiece, dpiece, 0)
+    scaled_part = (residual_out * gain_part[None, :]).astype(jnp.bfloat16)
+    square_part = jnp.sum(residual_out * residual_out, axis=1, keepdims=True)
+    square_high = square_part.astype(jnp.bfloat16)
+    square_low = (square_part - square_high.astype(jnp.float32)).astype(jnp.bfloat16)
+    payload = jnp.concatenate([scaled_part, square_high, square_low], axis=1)
+    payload_all = gather_by_exchange(payload, "fsdp", groups)
+    scaled_out = jnp.transpose(payload_all[:, :, :dpiece], (1, 0, 2)).reshape(quarter, width)
+    square_sum = jnp.sum(
+        payload_all[:, :, dpiece:].astype(jnp.float32), axis=(0, 2)
+    )
+    mean_square = square_sum / width
     logits = jnp.dot(scaled_out, lm_head, preferred_element_type=jnp.float32)
     local_max = jnp.max(logits, axis=1) * lax.rsqrt(mean_square + norm_epsilon)
     max_all = gather_by_exchange(local_max, "fsdp", groups)

time: 318 us -> 294 us (0.925)
  waiting for transfers between devices: 116 us -> 94 us
  blocking collectives: 83.2 us -> 101 us
  starting transfers between devices: 42.1 us -> 30.5 us
  local copies, waits for them, and re-layouts: 27.3 us -> 21.7 us
    all_to_all x6 -> x4, waiting for transfers between devices: 98.8 us -> 77.2 us  [exchange(): lax.all_to_all(rows, axis_name, split_axis=0, concat_axis=0, tiled=True)]
    all_to_all x3 -> x4, blocking collectives: 83.2 us -> 101 us  [exchange(): lax.all_to_all(rows, axis_name, split_axis=0, concat_axis=0, tiled=True)]
    all_to_all x6 -> x4, starting transfers between devices: 42 us -> 30.1 us  [exchange(): lax.all_to_all(rows, axis_name, split_axis=0, concat_axis=0, tiled=True)]
    all_to_all x3 -> x1, other arithmetic: 5.04 us -> 0.8 us  [exchange(): lax.all_to_all(rows, axis_name, split_axis=0, concat_axis=0, tiled=True)]
    convert_element_type x0 -> x5, other arithmetic: none -> 3.2 us  [the longest x1 2.35 us: local(): arrived = pieces_in[:, 2, :1].astype(jnp.int32)]
    unnamed x23 -> x19, local copies, waits for them, and re-layouts: 7.31 us -> 7.11 us
  transfers between devices with their start and end apart: 9 -> 7, of which waited for: 7 -> 5; matrix products, arithmetic and copies ran while one was open for 11% -> 12% of each run, Pallas kernels for 0% -> 0%
where the time goes in v4:
time: 294 us; the launch traced here: 293 us
  blocking collectives  101 us (34%)
  waiting for transfers between devices  94 us (32%)
  starting transfers between devices  30.5 us (10%)
  local copies, waits for them, and re-layouts  21.7 us (7%)
  matrix products  16.4 us (6%)
  between operations  16.2 us (6%)
  other arithmetic  13.8 us (5%)
    all_to_all x4, blocking collectives, exchange(): lax.all_to_all(rows, axis_name, split_axis=0, concat_axis=0, tiled=True)  101 us
    all_to_all x4, waiting for transfers between devices, exchange(): lax.all_to_all(rows, axis_name, split_axis=0, concat_axis=0, tiled=True)  77.2 us
    all_to_all x4, starting transfers between devices, exchange(): lax.all_to_all(rows, axis_name, split_axis=0, concat_axis=0, tiled=True)  30.1 us
    reduce_scatter x1, waiting for transfers between devices, local(): lax.psum_scatter(partial_out, 'seq', scatter_dimension=0, tiled=True)  15.4 us
    unnamed x19, local copies, waits for them, and re-layouts  7.11 us
    dot_general x2, matrix products, select_rows(): jnp.dot(selector.astype(jnp.bfloat16), rows, preferred_element_type=jnp.f...  6.61 us
  transfers between devices with their start and end apart: 7, of which 5 were waited for; matrix products, arithmetic and copies ran while one was open for 12% of the time, Pallas kernels for 0%

profile of v4, /device:TPU:1, one launch (start us, length us, event | category | flops | bytes accessed | tf_op | source)
XLA Modules:
  0.0 293.1 jit_solution(10621809913605731600)
XLA Ops:
  7.2 0.7 all-gather.3.cloned.1.call-update
  8.0 0.7 all-gather.5.cloned.1.call-update
  9.3 1.5 multiply_reduce_fusion.1
  11.5 0.9 fusion.31
  12.6 0.7 fusion.18
  13.4 0.2 reduce_window_sum.32
  13.5 0.8 fusion.20
  14.6 31.0 %all_to_all.50 = bf16[128,3,32]{2,1,0:T(4,128)(2,1)S(1)} all-to-all(bf16[128,3,32]{2,1,0:T(4,128)(2,1)S(1)} %copy.74), channel_id=1, replica_groups=mesh['fsdp'=128,'seq'=4] {'fsdp'}, dimensions={0} | all-to-all | bytes 49152 | tf_op jit(solution)/shard_map/all_to_all | solution.py:24
  45.7 1.0 convolution_bitcast_fusion
  46.7 0.3 copy.77
  47.0 20.3 %all_to_all.51 = f32[128,1,512]{2,1,0:T(1,128)S(1)} all-to-all(f32[128,1,512]{2,1,0:T(1,128)S(1)} %copy.77), channel_id=1, replica_groups=mesh['fsdp'=128,'seq'=4] {'fsdp'}, dimensions={0} | all-to-all | bytes 524288 | tf_op jit(solution)/shard_map/all_to_all | solution.py:24
  67.3 0.2 reduce_sum.76
  67.5 0.1 broadcast_in_dim.38
  67.6 0.5 broadcast.86
  68.1 1.3 reduce.12
  69.4 0.7 reshape.199
  70.1 5.5 %all-to-all-start.2 = ((bf16[128,2,256]{2,1,0:T(2,128)(2,1)}), bf16[128,2,256]{2,1,0:T(2,128)(2,1)S(1)}, u32[]{:S(2)}, u32[]{:S(2)}) async-start(bf16[128,2,256]{2,1,0:T(2,128)(2,1)} %reshape.199), calls=%async_computation.2 | async-start | bytes 262144 | tf_op jit(solution)/shard_map/all_to_all | solution.py:24
  75.7 12.9 %all-to-all-done.2 = bf16[128,2,256]{2,1,0:T(2,128)(2,1)S(1)} async-done(((bf16[128,2,256]{2,1,0:T(2,128)(2,1)}), bf16[128,2,256]{2,1,0:T(2,128)(2,1)S(1)}, u32[]{:S(2)}, u32[]{:S(2)}) %all-to-all-start.2) | async-done | bytes 131104 | tf_op jit(solution)/shard_map/all_to_all | solution.py:24
  88.7 0.2 copy.78
  88.9 0.1 convolution_bitcast_fusion.1
  89.0 0.2 copy.81
  89.2 0.8 reshape.201
  90.0 5.5 %all-to-all-start.3 = ((f32[128,1,128]{2,1,0:T(1,128)}), f32[128,1,128]{2,1,0:T(1,128)S(1)}, u32[]{:S(2)}, u32[]{:S(2)}) async-start(f32[128,1,128]{2,1,0:T(1,128)} %reshape.201), calls=%async_computation.3 | async-start | bytes 131072 | tf_op jit(solution)/shard_map/all_to_all | solution.py:24
  95.5 3.3 %convolution_convert_fusion.1 = bf16[256,4096]{1,0:T(8,128)(2,1)} fusion(bf16[128,4096]{1,0:T(8,128)(2,1)} %all-gather.3.cloned.1.call-done, s32[128]{0:T(128)S(1)} %multiply_add_fusion), kind=kOutput, calls=%fused_computation.3 | convolution fusion | flops 269516800 | bytes 3146240 | tf_op jit(solution)/shard_map/dot_general | solution.py:33
  98.8 4.4 %reshape.184 = bf16[128,2,4096]{2,1,0:T(2,128)(2,1)} reshape(bf16[256,4096]{1,0:T(8,128)(2,1)} %convolution_convert_fusion.1) | data formatting | bytes 4194304 | tf_op jit(solution)/shard_map/reshape | solution.py:103
  103.2 3.9 %all-to-all-done.3 = f32[128,1,128]{2,1,0:T(1,128)S(1)} async-done(((f32[128,1,128]{2,1,0:T(1,128)}), f32[128,1,128]{2,1,0:T(1,128)S(1)}, u32[]{:S(2)}, u32[]{:S(2)}) %all-to-all-start.3) | async-done | bytes 65568 | tf_op jit(solution)/shard_map/all_to_all | solution.py:24
  107.1 10.6 %all-to-all-start.4 = ((bf16[128,2,4096]{2,1,0:T(2,128)(2,1)}), bf16[128,2,4096]{2,1,0:T(2,128)(2,1)}, u32[]{:S(2)}, u32[]{:S(2)}) async-start(bf16[128,2,4096]{2,1,0:T(2,128)(2,1)} %reshape.184), calls=%async_computation.4 | async-start | bytes 4194304 | tf_op jit(solution)/shard_map/all_to_all | solution.py:24
  118.5 2.4 fusion.16
  121.0 0.2 lt.65
  121.2 0.3 reduce-window.9
  121.7 0.1 reshape.190
  122.0 0.2 fusion.11
  122.2 0.5 broadcast.87
  122.7 0.8 reduce.13
  123.5 0.2 reshape.202
  123.7 0.2 reshape.182
  123.9 48.7 %all-to-all-done.4 = bf16[128,2,4096]{2,1,0:T(2,128)(2,1)} async-done(((bf16[128,2,4096]{2,1,0:T(2,128)(2,1)}), bf16[128,2,4096]{2,1,0:T(2,128)(2,1)}, u32[]{:S(2)}, u32[]{:S(2)}) %all-to-all-start.4) | async-done | bytes 2097184 | tf_op jit(solution)/shard_map/all_to_all | solution.py:24
  172.6 4.1 %reshape.185 = bf16[256,4096]{1,0:T(8,128)(2,1)} reshape(bf16[128,2,4096]{2,1,0:T(2,128)(2,1)} %all-to-all-done.4) | data formatting | bytes 4194304 | tf_op jit(solution)/shard_map/reshape | solution.py:111
  176.7 3.3 %fusion.1 = (f32[280]{0:T(512)S(1)}, bf16[280,4096]{1,0:T(8,128)(2,1)S(1)}) fusion(bf16[280,4096]{1,0:T(8,128)(2,1)} %param.12, bf16[256,4096]{1,0:T(8,128)(2,1)} %reshape.185, s32[256]{0:T(256)S(1)} %compare_select_fusion, pred[280]{0:T(512)(128)(4,1)S(1)} %fusion.11), kind=kOutput, calls=%fused_computation.5 | convolution fusion | flops 593008384 | bytes 6687096 | tf_op jit(solution)/shard_map/dot_general | solution.py:33
  180.1 2.1 fusion.33
  182.2 0.2 fusion.26
  182.5 4.3 %fusion.4 = bf16[35,4,8,128]{3,2,1,0:T(8,128)(2,1)S(1)} fusion(bf16[4096,512]{1,0:T(8,128)(2,1)} %all-gather.5.cloned.1.call-done, bf16[280,4096]{1,0:T(8,128)(2,1)} %copy-done.4, f32[4096]{0:T(1024)S(1)} %copy-done.2, f32[280]{0:T(512)S(1)} %add_rsqrt_fusion), kind=kOutput, calls=%fused_computation.10 | convolution fusion | flops 1179136000 | bytes 6792288 | tf_op jit(solution)/shard_map/dot_general | solution.py:116
  186.8 0.1 fusion.8
  186.9 0.1 broadcast_in_dim.43
  187.1 1.3 reduce.14
  188.4 0.7 reshape.203
  189.1 8.5 %all-to-all-start.5 = ((bf16[128,2,256]{2,1,0:T(2,128)(2,1)}), bf16[128,2,256]{2,1,0:T(2,128)(2,1)S(1)}, u32[]{:S(2)}, u32[]{:S(2)}) async-start(bf16[128,2,256]{2,1,0:T(2,128)(2,1)} %reshape.203), calls=%async_computation.5 | async-start | bytes 262144 | tf_op jit(solution)/shard_map/all_to_all | solution.py:24
  197.6 0.3 reduce-scatter.2.cloned.1.call-start
  197.9 0.8 dynamic_slice.15
  198.6 11.7 %all-to-all-done.5 = bf16[128,2,256]{2,1,0:T(2,128)(2,1)S(1)} async-done(((bf16[128,2,256]{2,1,0:T(2,128)(2,1)}), bf16[128,2,256]{2,1,0:T(2,128)(2,1)S(1)}, u32[]{:S(2)}, u32[]{:S(2)}) %all-to-all-start.5) | async-done | bytes 131104 | tf_op jit(solution)/shard_map/all_to_all | solution.py:24
  210.4 1.6 fusion.13
  212.1 15.4 %reduce-scatter.2.cloned.1.call-done = f32[32,32]{1,0:T(8,128)} async-done(((f32[128,32]{1,0:T(8,128)}), f32[32,32]{1,0:T(8,128)}) %reduce-scatter.2.cloned.1.call-update) | async-done | bytes 4112 | tf_op jit(solution)/shard_map/reduce_scatter | solution.py:139
  227.4 0.8 multiply_convert_fusion
  228.6 0.1 broadcast_in_dim.44
  228.7 1.6 reshape.205
  230.3 33.0 %all_to_all.52 = bf16[128,2,544]{2,1,0:T(2,128)(2,1)} all-to-all(bf16[128,2,544]{2,1,0:T(2,128)(2,1)S(1)} %reshape.205), channel_id=1, replica_groups=mesh['fsdp'=128,'seq'=4] {'fsdp'}, dimensions={0} | all-to-all | bytes 557056 | tf_op jit(solution)/shard_map/all_to_all | solution.py:24
  263.3 2.9 reshape.206
  266.3 0.5 convert_reduce_fusion
  266.8 0.4 copy.85
  267.2 1.1 reshape.187
  268.3 0.6 convolution_reduce_fusion
  268.9 0.5 rsqrt_multiply_fusion
  269.4 16.5 %all_to_all.53 = f32[128,1,32]{2,1,0:T(1,128)S(1)} all-to-all(f32[128,1,32]{2,1,0:T(1,128)S(1)} %broadcast_in_dim.45), channel_id=1, replica_groups=mesh['fsdp'=128,'seq'=4] {'fsdp'}, dimensions={0} | all-to-all | bytes 32768 | tf_op jit(solution)/shard_map/all_to_all | solution.py:24
  285.9 0.7 reduce_max.29
  (49 shorter events, 2.1 us)
Async XLA Ops:
  7.2 261.1 %copy-start = (bf16[4096,250]{1,0:T(8,128)(2,1)S(1)}, bf16[4096,250]{1,0:T(8,128)(2,1)}, u32[]{:S(2)}) copy-start(bf16[4096,250]{1,0:T(8,128)(2,1)} %param.23) | copy-start | bytes 6144004
  7.2 68.5 %copy-start.3 = (s32[128,1]{0,1:T(1,128)S(1)}, s32[128,1]{0,1:T(1,128)}, u32[]{:S(2)}) copy-start(s32[128,1]{0,1:T(1,128)} %param.14) | copy-start | bytes 1540
  7.2 88.3 %all-gather.3.cloned.1.call-start = ((), (), s32[]{:S(2)}) async-start(), calls=%async_computation.9 | async-start | bytes 1310720 | tf_op jit(solution)/shard_map/all_gather | solution.py:98
  7.9 174.5 %all-gather.5.cloned.1.call-start = ((), (), s32[]{:S(2)}) async-start(), calls=%async_computation.10 | async-start | bytes 4227072 | tf_op jit(solution)/shard_map/all_gather | solution.py:118
  14.5 74.4 %copy-start.1 = (bf16[32,512]{1,0:T(8,128)(2,1)S(1)}, bf16[32,512]{1,0:T(8,128)(2,1)}, u32[]{:S(2)}) copy-start(bf16[32,512]{1,0:T(8,128)(2,1)} %param.19) | copy-start | bytes 98308
  70.1 18.5 %all-to-all-start.2 = ((bf16[128,2,256]{2,1,0:T(2,128)(2,1)}), bf16[128,2,256]{2,1,0:T(2,128)(2,1)S(1)}, u32[]{:S(2)}, u32[]{:S(2)}) async-start(bf16[128,2,256]{2,1,0:T(2,128)(2,1)} %reshape.199), calls=%async_computation.2 | async-start | bytes 262144 | tf_op jit(solution)/shard_map/all_to_all | solution.py:24
  90.0 17.0 %all-to-all-start.3 = ((f32[128,1,128]{2,1,0:T(1,128)}), f32[128,1,128]{2,1,0:T(1,128)S(1)}, u32[]{:S(2)}, u32[]{:S(2)}) async-start(f32[128,1,128]{2,1,0:T(1,128)} %reshape.201), calls=%async_computation.3 | async-start | bytes 131072 | tf_op jit(solution)/shard_map/all_to_all | solution.py:24
  107.1 65.5 %all-to-all-start.4 = ((bf16[128,2,4096]{2,1,0:T(2,128)(2,1)}), bf16[128,2,4096]{2,1,0:T(2,128)(2,1)}, u32[]{:S(2)}, u32[]{:S(2)}) async-start(bf16[128,2,4096]{2,1,0:T(2,128)(2,1)} %reshape.184), calls=%async_computation.4 | async-start | bytes 4194304 | tf_op jit(solution)/shard_map/all_to_all | solution.py:24
  176.7 3.4 %copy-start.2 = (f32[4096]{0:T(1024)S(1)}, f32[4096]{0:T(1024)}, u32[]{:S(2)}) copy-start(f32[4096]{0:T(1024)} %param.17) | copy-start | bytes 49156
  180.0 2.2 copy-start.4
  189.1 21.3 %all-to-all-start.5 = ((bf16[128,2,256]{2,1,0:T(2,128)(2,1)}), bf16[128,2,256]{2,1,0:T(2,128)(2,1)S(1)}, u32[]{:S(2)}, u32[]{:S(2)}) async-start(bf16[128,2,256]{2,1,0:T(2,128)(2,1)} %reshape.203), calls=%async_computation.5 | async-start | bytes 262144 | tf_op jit(solution)/shard_map/all_to_all | solution.py:24
  197.6 29.8 %reduce-scatter.2.cloned.1.call-start = ((), (), s32[]{:S(2)}) async-start(), calls=%async_computation.11 | async-start | bytes 81920 | tf_op jit(solution)/shard_map/reduce_scatter | solution.py:139
Sparse Core Ops, SparseCore 0:
  10.1 33.8 all-gather.2
  47.2 115.1 all-gather.4
  212.1 15.2 reduce-scatter.1

commit v5 on v4

--- a/solution.py
+++ b/solution.py
@@ -1,8 +1,12 @@
 import math
+
+import functools
 
 import jax
 import jax.numpy as jnp
 from jax import lax
+from jax.experimental import pallas as pl
+from jax.experimental.pallas import tpu as pltpu
 from jax.sharding import PartitionSpec as P
 
 HD = 128
@@ -18,6 +22,54 @@
         * lax.rsqrt(jnp.mean(widened * widened, axis=1, keepdims=True) + norm_epsilon)
         * gain
     ).astype(jnp.bfloat16)
+
+
+def attention_kernel(heads, length_ref, normed_ref, values_w_ref, probe_ref, out_ref):
+    normed = normed_ref[...]
+    seq_len = normed.shape[0]
+    values = jnp.dot(normed, values_w_ref[...], preferred_element_type=jnp.float32).astype(
+        jnp.bfloat16
+    )
+    probe = probe_ref[...]
+    probe_high = probe.astype(jnp.bfloat16)
+    probe_low = (probe - probe_high.astype(jnp.float32)).astype(jnp.bfloat16)
+    contract = (((1,), (1,)), ((), ()))
+    scores = lax.dot_general(
+        probe_high, normed, contract, preferred_element_type=jnp.float32
+    ) + lax.dot_general(probe_low, normed, contract, preferred_element_type=jnp.float32)
+    scores = scores / math.sqrt(HD)
+    live = lax.broadcasted_iota(jnp.int32, (heads, seq_len), 1) < length_ref[0]
+    scores = jnp.where(live, scores, -jnp.inf)
+    peak = jnp.max(scores, axis=1, keepdims=True)
+    shifted = jnp.exp(scores - peak)
+    weights = (shifted / jnp.sum(shifted, axis=1, keepdims=True)).astype(jnp.bfloat16)
+    mixed = jnp.dot(weights, values, preferred_element_type=jnp.float32)
+    for head in range(heads):
+        block = slice(head * HD, (head + 1) * HD)
+        out_ref[:, block] = mixed[head : head + 1, block].astype(out_ref.dtype)
+
+
+def attend(length, normed, values_w, probe):
+    heads = probe.shape[0]
+    seq_len, width = normed.shape
+    columns = values_w.shape[1]
+    flops = 2 * seq_len * width * columns + 4 * heads * seq_len * width + 2 * heads * seq_len * columns
+    return pl.pallas_call(
+        functools.partial(attention_kernel, heads),
+        out_shape=jax.ShapeDtypeStruct((1, columns), jnp.bfloat16),
+        in_specs=[
+            pl.BlockSpec(memory_space=pltpu.SMEM),
+            pl.BlockSpec(memory_space=pltpu.VMEM),
+            pl.BlockSpec(memory_space=pltpu.VMEM),
+            pl.BlockSpec(memory_space=pltpu.VMEM),
+        ],
+        out_specs=pl.BlockSpec(memory_space=pltpu.VMEM),
+        cost_estimate=pl.CostEstimate(
+            flops=flops,
+            bytes_accessed=2 * seq_len * width + 2 * width * columns + 4 * heads * width,
+            transcendentals=heads * seq_len,
+        ),
+    )(length, normed, values_w, probe)
 
 
 def exchange(rows, axis_name):
@@ -113,25 +165,9 @@
     states = jnp.where(replaced, placed, text_embeds)
     normed = row_norm(states, attn_gain)
 
-    value_sum = jnp.dot(
-        normed,
-        lax.all_gather(w_value, "fsdp", axis=0, tiled=True),
-        preferred_element_type=jnp.float32,
-    )
-    value_heads = value_sum.astype(jnp.bfloat16).reshape(seq_len, heads_local, HD)
-    scores = jnp.dot(
-        normed.astype(jnp.float32), probe.T, precision=lax.Precision.HIGHEST
-    ).T / math.sqrt(HD)
-    live_keys = jnp.arange(seq_len, dtype=jnp.int32) < lengths[0]
-    scores = jnp.where(live_keys[None, :], scores, -jnp.inf)
-    peak = jnp.max(scores, axis=1, keepdims=True)
-    shifted = jnp.exp(scores - peak)
-    weights = (shifted / jnp.sum(shifted, axis=1, keepdims=True)).astype(jnp.bfloat16)
-    attended = (
-        jnp.einsum("hj,jhc->hc", weights, value_heads, preferred_element_type=jnp.float32)
-        .astype(jnp.bfloat16)
-        .reshape(columns)
-    )
+    attended = attend(
+        lengths, normed, lax.all_gather(w_value, "fsdp", axis=0, tiled=True), probe
+    ).reshape(columns)
 
     attended_seq = gather_by_exchange(attended, "fsdp", groups)
     out_rows = lax.dynamic_slice_in_dim(w_out, seq_index * columns, columns, 0)

time: 294 us -> 297 us (1.010)
  matrix products: 16.4 us -> 9.86 us
  Pallas kernels: 0 us -> 6.42 us
    dot_general x3 -> x0, matrix products: 6.55 us -> none  [the longest x1 4.28 us: local(): jnp.dot(normed, lax.all_gather(w_value, 'fsdp', axis=0, tiled=True), pref...]
    pallas_call x0 -> x1, Pallas kernels: none -> 6.42 us  [attend(): pl.pallas_call(functools.partial(attention_kernel, heads), out_shape=jax....]
    unnamed x19 -> x17, local copies, waits for them, and re-layouts: 7.11 us -> 7.1 us
where the time goes in v5:
time: 297 us; the launch traced here: 295 us
  blocking collectives  101 us (34%)
  waiting for transfers between devices  92.8 us (31%)
  starting transfers between devices  30.8 us (10%)
  local copies, waits for them, and re-layouts  22.3 us (8%)
  other arithmetic  16.5 us (6%)
  between operations  16.1 us (5%)
  matrix products  9.86 us (3%)
  Pallas kernels  6.42 us (2%)
    all_to_all x4, blocking collectives, exchange(): lax.all_to_all(rows, axis_name, split_axis=0, concat_axis=0, tiled=True)  101 us
    all_to_all x4, waiting for transfers between devices, exchange(): lax.all_to_all(rows, axis_name, split_axis=0, concat_axis=0, tiled=True)  75.9 us
    all_to_all x4, starting transfers between devices, exchange(): lax.all_to_all(rows, axis_name, split_axis=0, concat_axis=0, tiled=True)  30.5 us
    reduce_scatter x1, waiting for transfers between devices, local(): lax.psum_scatter(partial_out, 'seq', scatter_dimension=0, tiled=True)  15.5 us
    unnamed x17, local copies, waits for them, and re-layouts  7.1 us
    dot_general x2, matrix products, select_rows(): jnp.dot(selector.astype(jnp.bfloat16), rows, preferred_element_type=jnp.f...  6.62 us
    pallas_call x1, Pallas kernels, attend(): pl.pallas_call(functools.partial(attention_kernel, heads), out_shape=jax....  6.42 us
  transfers between devices with their start and end apart: 7, of which 5 were waited for; matrix products, arithmetic and copies ran while one was open for 12% of the time, Pallas kernels for 0%

profile of v5, /device:TPU:1, one launch (start us, length us, event | category | flops | bytes accessed | tf_op | source)
XLA Modules:
  0.0 295.4 jit_solution(14296962720114105297)
XLA Ops:
  7.2 0.7 all-gather.3.cloned.1.call-update
  8.0 0.7 all-gather.5.cloned.1.call-update
  9.3 1.5 multiply_reduce_fusion.1
  11.5 0.9 fusion.21
  12.6 0.7 fusion.11
  13.4 0.2 reduce_window_sum.32
  13.5 0.8 fusion.13
  14.6 31.0 %all_to_all.50 = bf16[128,3,32]{2,1,0:T(4,128)(2,1)S(1)} all-to-all(bf16[128,3,32]{2,1,0:T(4,128)(2,1)S(1)} %copy.75), channel_id=1, replica_groups=mesh['fsdp'=128,'seq'=4] {'fsdp'}, dimensions={0} | all-to-all | bytes 49152 | tf_op jit(solution)/shard_map/all_to_all | solution.py:76
  45.7 1.0 convolution_bitcast_fusion
  46.7 0.3 copy.78
  47.0 20.3 %all_to_all.51 = f32[128,1,512]{2,1,0:T(1,128)S(1)} all-to-all(f32[128,1,512]{2,1,0:T(1,128)S(1)} %copy.78), channel_id=1, replica_groups=mesh['fsdp'=128,'seq'=4] {'fsdp'}, dimensions={0} | all-to-all | bytes 524288 | tf_op jit(solution)/shard_map/all_to_all | solution.py:76
  67.3 0.2 reduce_sum.69
  67.5 0.1 broadcast_in_dim.25
  67.6 0.5 broadcast.81
  68.2 1.4 reduce.13
  69.6 0.7 reshape.190
  70.2 5.5 %all-to-all-start.3 = ((bf16[128,2,256]{2,1,0:T(2,128)(2,1)}), bf16[128,2,256]{2,1,0:T(2,128)(2,1)S(1)}, u32[]{:S(2)}, u32[]{:S(2)}) async-start(bf16[128,2,256]{2,1,0:T(2,128)(2,1)} %reshape.190), calls=%async_computation.3 | async-start | bytes 262144 | tf_op jit(solution)/shard_map/all_to_all | solution.py:76
  75.8 12.8 %all-to-all-done.3 = bf16[128,2,256]{2,1,0:T(2,128)(2,1)S(1)} async-done(((bf16[128,2,256]{2,1,0:T(2,128)(2,1)}), bf16[128,2,256]{2,1,0:T(2,128)(2,1)S(1)}, u32[]{:S(2)}, u32[]{:S(2)}) %all-to-all-start.3) | async-done | bytes 131104 | tf_op jit(solution)/shard_map/all_to_all | solution.py:76
  88.6 0.2 copy.79
  88.8 0.1 convolution_bitcast_fusion.1
  89.0 0.2 copy.82
  89.1 0.8 reshape.192
  90.0 5.5 %all-to-all-start.4 = ((f32[128,1,128]{2,1,0:T(1,128)}), f32[128,1,128]{2,1,0:T(1,128)S(1)}, u32[]{:S(2)}, u32[]{:S(2)}) async-start(f32[128,1,128]{2,1,0:T(1,128)} %reshape.192), calls=%async_computation.4 | async-start | bytes 131072 | tf_op jit(solution)/shard_map/all_to_all | solution.py:76
  95.5 3.3 %convolution_convert_fusion.1 = bf16[256,4096]{1,0:T(8,128)(2,1)} fusion(bf16[128,4096]{1,0:T(8,128)(2,1)} %all-gather.3.cloned.1.call-done, s32[128]{0:T(128)S(1)} %multiply_add_fusion), kind=kOutput, calls=%fused_computation.3 | convolution fusion | flops 269516800 | bytes 3146240 | tf_op jit(solution)/shard_map/dot_general | solution.py:85
  98.7 4.4 %reshape.174 = bf16[128,2,4096]{2,1,0:T(2,128)(2,1)} reshape(bf16[256,4096]{1,0:T(8,128)(2,1)} %convolution_convert_fusion.1) | data formatting | bytes 4194304 | tf_op jit(solution)/shard_map/reshape | solution.py:155
  103.1 3.9 %all-to-all-done.4 = f32[128,1,128]{2,1,0:T(1,128)S(1)} async-done(((f32[128,1,128]{2,1,0:T(1,128)}), f32[128,1,128]{2,1,0:T(1,128)S(1)}, u32[]{:S(2)}, u32[]{:S(2)}) %all-to-all-start.4) | async-done | bytes 65568 | tf_op jit(solution)/shard_map/all_to_all | solution.py:76
  107.0 10.6 %all-to-all-start.1 = ((bf16[128,2,4096]{2,1,0:T(2,128)(2,1)}), bf16[128,2,4096]{2,1,0:T(2,128)(2,1)}, u32[]{:S(2)}, u32[]{:S(2)}) async-start(bf16[128,2,4096]{2,1,0:T(2,128)(2,1)} %reshape.174), calls=%async_computation.1 | async-start | bytes 4194304 | tf_op jit(solution)/shard_map/all_to_all | solution.py:76
  117.6 0.1 lt.50
  118.4 2.4 fusion.9
  121.0 0.2 lt.53
  121.1 0.3 reduce-window.9
  121.6 0.1 reshape.182
  122.0 0.2 fusion.4
  122.1 0.5 broadcast.82
  122.6 0.8 reduce.14
  123.5 0.2 reshape.193
  123.7 0.8 reshape.178.probe_ref
  124.4 47.6 %all-to-all-done.1 = bf16[128,2,4096]{2,1,0:T(2,128)(2,1)} async-done(((bf16[128,2,4096]{2,1,0:T(2,128)(2,1)}), bf16[128,2,4096]{2,1,0:T(2,128)(2,1)}, u32[]{:S(2)}, u32[]{:S(2)}) %all-to-all-start.1) | async-done | bytes 2097184 | tf_op jit(solution)/shard_map/all_to_all | solution.py:76
  172.0 4.1 %reshape.175 = bf16[256,4096]{1,0:T(8,128)(2,1)} reshape(bf16[128,2,4096]{2,1,0:T(2,128)(2,1)} %all-to-all-done.1) | data formatting | bytes 4194304 | tf_op jit(solution)/shard_map/reshape | solution.py:163
  176.1 3.4 %fusion.1 = (f32[280]{0:T(512)S(1)}, bf16[280,4096]{1,0:T(8,128)(2,1)S(1)}) fusion(bf16[280,4096]{1,0:T(8,128)(2,1)} %param.12, bf16[256,4096]{1,0:T(8,128)(2,1)} %reshape.175, s32[256]{0:T(256)S(1)} %compare_select_fusion, pred[280]{0:T(512)(128)(4,1)S(1)} %fusion.4), kind=kOutput, calls=%fused_computation.5 | convolution fusion | flops 593008384 | bytes 6687096 | tf_op jit(solution)/shard_map/dot_general | solution.py:85
  179.5 2.1 fusion.3.normed_ref
  181.6 6.4 %shard_map.131 = bf16[1,512]{1,0:T(2,128)(2,1)} custom-call(s32[1]{0:T(128)S(6)} %copy.109.length_ref, bf16[280,4096]{1,0:T(8,128)(2,1)} %fusion.3.normed_ref, bf16[4096,512]{1,0:T(8,128)(2,1)} %all-gather.5.cloned.1.call-done.values_w_ref, f32[4,4096]{1,0:T(4,128)} %reshape.178.probe_ref), custom_call_target="tpu_custom_call" | custom-call | flops 1193902080 | bytes 6553600 | tf_op jit(solution)/shard_map/pallas_call | solution.py:57
  188.0 0.7 reduce.8
  188.7 0.1 broadcast_in_dim.26
  188.9 1.4 reduce.15
  190.3 0.7 reshape.194
  190.9 8.9 %all-to-all-start.5 = ((bf16[128,2,256]{2,1,0:T(2,128)(2,1)}), bf16[128,2,256]{2,1,0:T(2,128)(2,1)S(1)}, u32[]{:S(2)}, u32[]{:S(2)}) async-start(bf16[128,2,256]{2,1,0:T(2,128)(2,1)} %reshape.194), calls=%async_computation.5 | async-start | bytes 262144 | tf_op jit(solution)/shard_map/all_to_all | solution.py:76
  199.8 0.3 reduce-scatter.2.cloned.1.call-start
  200.1 0.8 dynamic_slice.15
  200.9 11.7 %all-to-all-done.5 = bf16[128,2,256]{2,1,0:T(2,128)(2,1)S(1)} async-done(((bf16[128,2,256]{2,1,0:T(2,128)(2,1)}), bf16[128,2,256]{2,1,0:T(2,128)(2,1)S(1)}, u32[]{:S(2)}, u32[]{:S(2)}) %all-to-all-start.5) | async-done | bytes 131104 | tf_op jit(solution)/shard_map/all_to_all | solution.py:76
  212.7 1.6 fusion.6
  214.3 15.5 %reduce-scatter.2.cloned.1.call-done = f32[32,32]{1,0:T(8,128)} async-done(((f32[128,32]{1,0:T(8,128)}), f32[32,32]{1,0:T(8,128)}) %reduce-scatter.2.cloned.1.call-update) | async-done | bytes 4112 | tf_op jit(solution)/shard_map/reduce_scatter | solution.py:175
  229.8 0.8 multiply_convert_fusion
  230.9 0.1 broadcast_in_dim.27
  231.0 1.6 reshape.196
  232.6 33.0 %all_to_all.52 = bf16[128,2,544]{2,1,0:T(2,128)(2,1)} all-to-all(bf16[128,2,544]{2,1,0:T(2,128)(2,1)S(1)} %reshape.196), channel_id=1, replica_groups=mesh['fsdp'=128,'seq'=4] {'fsdp'}, dimensions={0} | all-to-all | bytes 557056 | tf_op jit(solution)/shard_map/all_to_all | solution.py:76
  265.6 2.9 reshape.197
  268.6 0.5 convert_reduce_fusion
  269.1 0.4 copy.86
  269.5 1.1 reshape.179
  270.6 0.6 convolution_reduce_fusion
  271.2 0.5 rsqrt_multiply_fusion
  271.8 16.5 %all_to_all.53 = f32[128,1,32]{2,1,0:T(1,128)S(1)} all-to-all(f32[128,1,32]{2,1,0:T(1,128)S(1)} %broadcast_in_dim.28), channel_id=1, replica_groups=mesh['fsdp'=128,'seq'=4] {'fsdp'}, dimensions={0} | all-to-all | bytes 32768 | tf_op jit(solution)/shard_map/all_to_all | solution.py:76
  288.2 0.7 reduce_max.19
  (43 shorter events, 1.9 us)
Async XLA Ops:
  7.2 263.5 %copy-start = (bf16[4096,250]{1,0:T(8,128)(2,1)S(1)}, bf16[4096,250]{1,0:T(8,128)(2,1)}, u32[]{:S(2)}) copy-start(bf16[4096,250]{1,0:T(8,128)(2,1)} %param.23) | copy-start | bytes 6144004
  7.2 68.6 %copy-start.3 = (s32[128,1]{0,1:T(1,128)S(1)}, s32[128,1]{0,1:T(1,128)}, u32[]{:S(2)}) copy-start(s32[128,1]{0,1:T(1,128)} %param.14) | copy-start | bytes 1540
  7.2 88.3 %all-gather.3.cloned.1.call-start = ((), (), s32[]{:S(2)}) async-start(), calls=%async_computation.9 | async-start | bytes 1310720 | tf_op jit(solution)/shard_map/all_gather | solution.py:150
  7.9 173.7 %all-gather.5.cloned.1.call-start = ((), (), s32[]{:S(2)}) async-start(), calls=%async_computation.10 | async-start | bytes 4227072 | tf_op jit(solution)/shard_map/all_gather | solution.py:169
  14.5 74.3 %copy-start.2 = (bf16[32,512]{1,0:T(8,128)(2,1)S(1)}, bf16[32,512]{1,0:T(8,128)(2,1)}, u32[]{:S(2)}) copy-start(bf16[32,512]{1,0:T(8,128)(2,1)} %param.19) | copy-start | bytes 98308
  70.2 18.3 %all-to-all-start.3 = ((bf16[128,2,256]{2,1,0:T(2,128)(2,1)}), bf16[128,2,256]{2,1,0:T(2,128)(2,1)S(1)}, u32[]{:S(2)}, u32[]{:S(2)}) async-start(bf16[128,2,256]{2,1,0:T(2,128)(2,1)} %reshape.190), calls=%async_computation.3 | async-start | bytes 262144 | tf_op jit(solution)/shard_map/all_to_all | solution.py:76
  90.0 17.0 %all-to-all-start.4 = ((f32[128,1,128]{2,1,0:T(1,128)}), f32[128,1,128]{2,1,0:T(1,128)S(1)}, u32[]{:S(2)}, u32[]{:S(2)}) async-start(f32[128,1,128]{2,1,0:T(1,128)} %reshape.192), calls=%async_computation.4 | async-start | bytes 131072 | tf_op jit(solution)/shard_map/all_to_all | solution.py:76
  107.0 65.0 %all-to-all-start.1 = ((bf16[128,2,4096]{2,1,0:T(2,128)(2,1)}), bf16[128,2,4096]{2,1,0:T(2,128)(2,1)}, u32[]{:S(2)}, u32[]{:S(2)}) async-start(bf16[128,2,4096]{2,1,0:T(2,128)(2,1)} %reshape.174), calls=%async_computation.1 | async-start | bytes 4194304 | tf_op jit(solution)/shard_map/all_to_all | solution.py:76
  176.1 3.4 %copy-start.1 = (f32[4096]{0:T(1024)S(1)}, f32[4096]{0:T(1024)}, u32[]{:S(2)}) copy-start(f32[4096]{0:T(1024)} %param.17) | copy-start | bytes 49156
  190.9 21.6 %all-to-all-start.5 = ((bf16[128,2,256]{2,1,0:T(2,128)(2,1)}), bf16[128,2,256]{2,1,0:T(2,128)(2,1)S(1)}, u32[]{:S(2)}, u32[]{:S(2)}) async-start(bf16[128,2,256]{2,1,0:T(2,128)(2,1)} %reshape.194), calls=%async_computation.5 | async-start | bytes 262144 | tf_op jit(solution)/shard_map/all_to_all | solution.py:76
  199.8 29.9 %reduce-scatter.2.cloned.1.call-start = ((), (), s32[]{:S(2)}) async-start(), calls=%async_computation.11 | async-start | bytes 81920 | tf_op jit(solution)/shard_map/reduce_scatter | solution.py:175
Sparse Core Ops, SparseCore 0:
  10.1 33.8 all-gather.2
  47.2 112.2 all-gather.4
  214.4 15.3 reduce-scatter.1

commit v6 on v4

--- a/solution.py
+++ b/solution.py
@@ -95,13 +95,15 @@
     probe_in = exchange(probe_part, "fsdp")
     probe = jnp.transpose(probe_in, (1, 0, 2)).reshape(heads_local, width)
 
-    full_vision = lax.all_gather(vision_tokens, "seq", axis=1, tiled=True)
+    piece_width = vision_tokens.shape[1]
     slot_of = destination * capacity + slot_index
     outbox_select = (
         jnp.arange(groups * capacity, dtype=jnp.int32)[:, None] == slot_of[None, :]
     )
-    outbox = select_rows(outbox_select, full_vision).reshape(groups, capacity, width)
-    received = exchange(outbox, "fsdp")
+    outbox = select_rows(outbox_select, vision_tokens).reshape(groups, capacity, piece_width)
+    received_piece = exchange(outbox, "fsdp").reshape(groups * capacity, piece_width)
+    received_all = gather_by_exchange(received_piece, "seq", seq_count)
+    received = jnp.transpose(received_all, (1, 0, 2)).reshape(groups * capacity, width)
     occupied = (
         (jnp.arange(capacity, dtype=jnp.int32)[None, :] < arrived).astype(jnp.int32).reshape(-1)
     )

time: 294 us -> 280 us (0.952)
  waiting for transfers between devices: 94 us -> 88.2 us
  local copies, waits for them, and re-layouts: 21.7 us -> 16 us
  matrix products: 16.4 us -> 13.4 us
    reshape x2 -> x1, local copies, waits for them, and re-layouts: 8.51 us -> 0.99 us  [local(): select_rows(outbox_select, vision_tokens)]
    all_to_all x4 -> x5, waiting for transfers between devices: 77.2 us -> 73.8 us  [exchange(): lax.all_to_all(rows, axis_name, split_axis=0, concat_axis=0, tiled=True)]
    dot_general x2, matrix products: 6.61 us -> 3.62 us  [select_rows(): jnp.dot(selector.astype(jnp.bfloat16), rows, preferred_element_type=jnp.f...]
    all_to_all x4 -> x5, starting transfers between devices: 30.1 us -> 29.4 us  [exchange(): lax.all_to_all(rows, axis_name, split_axis=0, concat_axis=0, tiled=True)]
    unnamed x19 -> x21, local copies, waits for them, and re-layouts: 7.11 us -> 7.11 us
  transfers between devices with their start and end apart: 7 -> 7, of which waited for: 5 -> 6; matrix products, arithmetic and copies ran while one was open for 12% -> 9% of each run, Pallas kernels for 0% -> 0%
where the time goes in v6:
time: 280 us; the launch traced here: 279 us
  blocking collectives  101 us (36%)
  waiting for transfers between devices  88.2 us (32%)
  starting transfers between devices  29.7 us (11%)
  between operations  16.5 us (6%)
  local copies, waits for them, and re-layouts  16 us (6%)
  other arithmetic  13.8 us (5%)
  matrix products  13.4 us (5%)
    all_to_all x4, blocking collectives, exchange(): lax.all_to_all(rows, axis_name, split_axis=0, concat_axis=0, tiled=True)  101 us
    all_to_all x5, waiting for transfers between devices, exchange(): lax.all_to_all(rows, axis_name, split_axis=0, concat_axis=0, tiled=True)  73.8 us
    all_to_all x5, starting transfers between devices, exchange(): lax.all_to_all(rows, axis_name, split_axis=0, concat_axis=0, tiled=True)  29.4 us
    reduce_scatter x1, waiting for transfers between devices, local(): lax.psum_scatter(partial_out, 'seq', scatter_dimension=0, tiled=True)  13.6 us
    unnamed x21, local copies, waits for them, and re-layouts  7.11 us
  transfers between devices with their start and end apart: 7, of which 6 were waited for; matrix products, arithmetic and copies ran while one was open for 9% of the time, Pallas kernels for 0%

profile of v6, /device:TPU:1, one launch (start us, length us, event | category | flops | bytes accessed | tf_op | source)
XLA Modules:
  0.0 278.6 jit_solution(2235904961388581934)
XLA Ops:
  7.2 0.7 all-gather.2.cloned.1.call-update
  8.6 1.5 multiply_reduce_fusion.1
  10.8 0.9 fusion.31
  11.9 0.7 fusion.18
  12.6 0.2 reduce_window_sum.32
  12.8 0.8 fusion.20
  13.9 31.1 %all_to_all.55 = bf16[128,3,32]{2,1,0:T(4,128)(2,1)S(1)} all-to-all(bf16[128,3,32]{2,1,0:T(4,128)(2,1)S(1)} %copy.79), channel_id=1, replica_groups=mesh['fsdp'=128,'seq'=4] {'fsdp'}, dimensions={0} | all-to-all | bytes 49152 | tf_op jit(solution)/shard_map/all_to_all | solution.py:24
  45.2 1.0 convolution_bitcast_fusion
  46.2 0.3 copy.82
  46.4 20.4 %all_to_all.56 = f32[128,1,512]{2,1,0:T(1,128)S(1)} all-to-all(f32[128,1,512]{2,1,0:T(1,128)S(1)} %copy.82), channel_id=1, replica_groups=mesh['fsdp'=128,'seq'=4] {'fsdp'}, dimensions={0} | all-to-all | bytes 524288 | tf_op jit(solution)/shard_map/all_to_all | solution.py:24
  66.8 0.2 reduce_sum.76
  67.2 0.5 broadcast.86
  67.7 1.3 reduce.12
  69.0 0.7 reshape.200
  69.7 5.5 %all-to-all-start.2 = ((bf16[128,2,256]{2,1,0:T(2,128)(2,1)}), bf16[128,2,256]{2,1,0:T(2,128)(2,1)S(1)}, u32[]{:S(2)}, u32[]{:S(2)}) async-start(bf16[128,2,256]{2,1,0:T(2,128)(2,1)} %reshape.200), calls=%async_computation.2 | async-start | bytes 262144 | tf_op jit(solution)/shard_map/all_to_all | solution.py:24
  75.3 0.3 convolution_convert_fusion.1
  75.6 1.0 reshape.185
  76.6 12.4 %all-to-all-done.2 = bf16[128,2,256]{2,1,0:T(2,128)(2,1)S(1)} async-done(((bf16[128,2,256]{2,1,0:T(2,128)(2,1)}), bf16[128,2,256]{2,1,0:T(2,128)(2,1)S(1)}, u32[]{:S(2)}, u32[]{:S(2)}) %all-to-all-start.2) | async-done | bytes 131104 | tf_op jit(solution)/shard_map/all_to_all | solution.py:24
  89.0 5.6 %all-to-all-start.4 = ((bf16[128,2,1024]{2,1,0:T(2,128)(2,1)}), bf16[128,2,1024]{2,1,0:T(2,128)(2,1)S(1)}, u32[]{:S(2)}, u32[]{:S(2)}) async-start(bf16[128,2,1024]{2,1,0:T(2,128)(2,1)} %reshape.185), calls=%async_computation.4 | async-start | bytes 1048576 | tf_op jit(solution)/shard_map/all_to_all | solution.py:24
  94.7 0.2 copy.83
  94.8 0.1 convolution_bitcast_fusion.1
  95.0 0.2 copy.86
  95.2 0.8 reshape.202
  96.0 18.9 %all-to-all-done.4 = bf16[128,2,1024]{2,1,0:T(2,128)(2,1)S(1)} async-done(((bf16[128,2,1024]{2,1,0:T(2,128)(2,1)}), bf16[128,2,1024]{2,1,0:T(2,128)(2,1)S(1)}, u32[]{:S(2)}, u32[]{:S(2)}) %all-to-all-start.4) | async-done | bytes 524320 | tf_op jit(solution)/shard_map/all_to_all | solution.py:24
  114.9 7.3 %all-to-all-start.3 = ((f32[128,1,128]{2,1,0:T(1,128)}), f32[128,1,128]{2,1,0:T(1,128)S(1)}, u32[]{:S(2)}, u32[]{:S(2)}) async-start(f32[128,1,128]{2,1,0:T(1,128)} %reshape.202), calls=%async_computation.3 | async-start | bytes 131072 | tf_op jit(solution)/shard_map/all_to_all | solution.py:24
  122.2 0.2 broadcast_in_dim.45
  122.4 0.2 copy.88
  122.6 11.0 %all-to-all-done.3 = f32[128,1,128]{2,1,0:T(1,128)S(1)} async-done(((f32[128,1,128]{2,1,0:T(1,128)}), f32[128,1,128]{2,1,0:T(1,128)S(1)}, u32[]{:S(2)}, u32[]{:S(2)}) %all-to-all-start.3) | async-done | bytes 65568 | tf_op jit(solution)/shard_map/all_to_all | solution.py:24
  133.6 1.5 broadcast_in_dim.46
  135.1 4.4 %all-to-all-start.5 = ((bf16[4,256,1024]{1,2,0:T(8,128)(2,1)}), bf16[4,256,1024]{1,2,0:T(8,128)(2,1)}, u32[]{:S(2)}, u32[]{:S(2)}) async-start(bf16[4,256,1024]{1,2,0:T(8,128)(2,1)} %broadcast_in_dim.46), calls=%async_computation.5 | async-start | bytes 4194304 | tf_op jit(solution)/shard_map/all_to_all | solution.py:24
  140.4 2.4 fusion.16
  142.9 0.2 lt.65
  143.1 0.3 reduce-window.9
  143.9 0.2 fusion.11
  144.1 0.5 broadcast.87
  144.6 0.8 reduce.13
  145.4 0.2 reshape.203
  145.6 0.2 reshape.183
  145.7 19.7 %all-to-all-done.5 = bf16[4,256,1024]{1,2,0:T(8,128)(2,1)} async-done(((bf16[4,256,1024]{1,2,0:T(8,128)(2,1)}), bf16[4,256,1024]{1,2,0:T(8,128)(2,1)}, u32[]{:S(2)}, u32[]{:S(2)}) %all-to-all-start.5) | async-done | bytes 2097184 | tf_op jit(solution)/shard_map/all_to_all | solution.py:24
  165.5 3.3 %fusion.1 = (f32[280]{0:T(512)S(1)}, bf16[280,4096]{1,0:T(8,128)(2,1)S(1)}) fusion(bf16[280,4096]{1,0:T(8,128)(2,1)} %param.12, bf16[256,4096]{0,1:T(8,128)(2,1)} %bitcast.12, s32[256]{0:T(256)S(1)} %compare_select_fusion, pred[280]{0:T(512)(128)(4,1)S(1)} %fusion.11), kind=kOutput, calls=%fused_computation.4 | convolution fusion | flops 593008384 | bytes 6687096 | tf_op jit(solution)/shard_map/dot_general | solution.py:33
  168.8 2.1 fusion.33
  171.0 0.2 fusion.26
  171.2 4.3 %fusion.4 = bf16[35,4,8,128]{3,2,1,0:T(8,128)(2,1)S(1)} fusion(bf16[4096,512]{1,0:T(8,128)(2,1)} %all-gather.2.cloned.1.call-done, bf16[280,4096]{1,0:T(8,128)(2,1)} %copy-done.5, f32[4096]{0:T(1024)S(1)} %copy-done.3, f32[280]{0:T(512)S(1)} %add_rsqrt_fusion), kind=kOutput, calls=%fused_computation.10 | convolution fusion | flops 1179136000 | bytes 6792288 | tf_op jit(solution)/shard_map/dot_general | solution.py:118
  175.5 0.1 fusion.8
  175.7 0.1 broadcast_in_dim.49
  175.9 1.3 reduce.14
  177.2 0.7 reshape.204
  177.9 6.6 %all-to-all-start.6 = ((bf16[128,2,256]{2,1,0:T(2,128)(2,1)}), bf16[128,2,256]{2,1,0:T(2,128)(2,1)S(1)}, u32[]{:S(2)}, u32[]{:S(2)}) async-start(bf16[128,2,256]{2,1,0:T(2,128)(2,1)} %reshape.204), calls=%async_computation.6 | async-start | bytes 262144 | tf_op jit(solution)/shard_map/all_to_all | solution.py:24
  184.5 0.3 reduce-scatter.2.cloned.1.call-start
  184.8 0.8 dynamic_slice.15
  185.5 11.8 %all-to-all-done.6 = bf16[128,2,256]{2,1,0:T(2,128)(2,1)S(1)} async-done(((bf16[128,2,256]{2,1,0:T(2,128)(2,1)}), bf16[128,2,256]{2,1,0:T(2,128)(2,1)S(1)}, u32[]{:S(2)}, u32[]{:S(2)}) %all-to-all-start.6) | async-done | bytes 131104 | tf_op jit(solution)/shard_map/all_to_all | solution.py:24
  197.4 1.5 fusion.13
  199.0 13.6 %reduce-scatter.2.cloned.1.call-done = f32[32,32]{1,0:T(8,128)} async-done(((f32[128,32]{1,0:T(8,128)}), f32[32,32]{1,0:T(8,128)}) %reduce-scatter.2.cloned.1.call-update) | async-done | bytes 4112 | tf_op jit(solution)/shard_map/reduce_scatter | solution.py:141
  212.7 0.8 multiply_convert_fusion
  213.9 1.6 reshape.206
  215.5 33.0 %all_to_all.57 = bf16[128,2,544]{2,1,0:T(2,128)(2,1)} all-to-all(bf16[128,2,544]{2,1,0:T(2,128)(2,1)S(1)} %reshape.206), channel_id=1, replica_groups=mesh['fsdp'=128,'seq'=4] {'fsdp'}, dimensions={0} | all-to-all | bytes 557056 | tf_op jit(solution)/shard_map/all_to_all | solution.py:24
  248.5 2.9 %reshape.207 = bf16[128,32,34]{2,1,0:T(8,128)(2,1)S(1)} reshape(bf16[128,2,544]{2,1,0:T(2,128)(2,1)} %all_to_all.57) | data formatting | bytes 557056
  251.5 0.5 convert_reduce_fusion
  252.0 0.4 copy.91
  252.4 1.1 reshape.188
  253.5 0.6 convolution_reduce_fusion
  254.1 0.5 rsqrt_multiply_fusion
  254.7 16.5 %all_to_all.58 = f32[128,1,32]{2,1,0:T(1,128)S(1)} all-to-all(f32[128,1,32]{2,1,0:T(1,128)S(1)} %broadcast_in_dim.86), channel_id=1, replica_groups=mesh['fsdp'=128,'seq'=4] {'fsdp'}, dimensions={0} | all-to-all | bytes 32768 | tf_op jit(solution)/shard_map/all_to_all | solution.py:24
  271.1 0.7 reduce_max.29
  (52 shorter events, 2.5 us)
Async XLA Ops:
  7.2 246.3 %copy-start = (bf16[4096,250]{1,0:T(8,128)(2,1)S(1)}, bf16[4096,250]{1,0:T(8,128)(2,1)}, u32[]{:S(2)}) copy-start(bf16[4096,250]{1,0:T(8,128)(2,1)} %param.23) | copy-start | bytes 6144004
  7.2 68.1 %copy-start.4 = (s32[128,1]{0,1:T(1,128)S(1)}, s32[128,1]{0,1:T(1,128)}, u32[]{:S(2)}) copy-start(s32[128,1]{0,1:T(1,128)} %param.14) | copy-start | bytes 1540
  7.2 68.1 %copy-start.1 = (bf16[128,1024]{1,0:T(8,128)(2,1)S(1)}, bf16[128,1024]{1,0:T(8,128)(2,1)}, u32[]{:S(2)}) copy-start(bf16[128,1024]{1,0:T(8,128)(2,1)} %param.13) | copy-start | bytes 786436
  7.2 164.0 %all-gather.2.cloned.1.call-start = ((), (), s32[]{:S(2)}) async-start(), calls=%async_computation.10 | async-start | bytes 4227072 | tf_op jit(solution)/shard_map/all_gather | solution.py:120
  67.7 27.1 %copy-start.2 = (bf16[32,512]{1,0:T(8,128)(2,1)S(1)}, bf16[32,512]{1,0:T(8,128)(2,1)}, u32[]{:S(2)}) copy-start(bf16[32,512]{1,0:T(8,128)(2,1)} %param.19) | copy-start | bytes 98308
  69.7 19.2 %all-to-all-start.2 = ((bf16[128,2,256]{2,1,0:T(2,128)(2,1)}), bf16[128,2,256]{2,1,0:T(2,128)(2,1)S(1)}, u32[]{:S(2)}, u32[]{:S(2)}) async-start(bf16[128,2,256]{2,1,0:T(2,128)(2,1)} %reshape.200), calls=%async_computation.2 | async-start | bytes 262144 | tf_op jit(solution)/shard_map/all_to_all | solution.py:24
  89.0 25.9 %all-to-all-start.4 = ((bf16[128,2,1024]{2,1,0:T(2,128)(2,1)}), bf16[128,2,1024]{2,1,0:T(2,128)(2,1)S(1)}, u32[]{:S(2)}, u32[]{:S(2)}) async-start(bf16[128,2,1024]{2,1,0:T(2,128)(2,1)} %reshape.185), calls=%async_computation.4 | async-start | bytes 1048576 | tf_op jit(solution)/shard_map/all_to_all | solution.py:24
  114.9 18.7 %all-to-all-start.3 = ((f32[128,1,128]{2,1,0:T(1,128)}), f32[128,1,128]{2,1,0:T(1,128)S(1)}, u32[]{:S(2)}, u32[]{:S(2)}) async-start(f32[128,1,128]{2,1,0:T(1,128)} %reshape.202), calls=%async_computation.3 | async-start | bytes 131072 | tf_op jit(solution)/shard_map/all_to_all | solution.py:24
  135.1 30.4 %all-to-all-start.5 = ((bf16[4,256,1024]{1,2,0:T(8,128)(2,1)}), bf16[4,256,1024]{1,2,0:T(8,128)(2,1)}, u32[]{:S(2)}, u32[]{:S(2)}) async-start(bf16[4,256,1024]{1,2,0:T(8,128)(2,1)} %broadcast_in_dim.46), calls=%async_computation.5 | async-start | bytes 4194304 | tf_op jit(solution)/shard_map/all_to_all | solution.py:24
  165.5 3.4 %copy-start.3 = (f32[4096]{0:T(1024)S(1)}, f32[4096]{0:T(1024)}, u32[]{:S(2)}) copy-start(f32[4096]{0:T(1024)} %param.17) | copy-start | bytes 49156
  168.8 2.1 copy-start.5
  177.9 19.4 %all-to-all-start.6 = ((bf16[128,2,256]{2,1,0:T(2,128)(2,1)}), bf16[128,2,256]{2,1,0:T(2,128)(2,1)S(1)}, u32[]{:S(2)}, u32[]{:S(2)}) async-start(bf16[128,2,256]{2,1,0:T(2,128)(2,1)} %reshape.204), calls=%async_computation.6 | async-start | bytes 262144 | tf_op jit(solution)/shard_map/all_to_all | solution.py:24
  184.5 28.2 %reduce-scatter.2.cloned.1.call-start = ((), (), s32[]{:S(2)}) async-start(), calls=%async_computation.11 | async-start | bytes 81920 | tf_op jit(solution)/shard_map/reduce_scatter | solution.py:141
Sparse Core Ops, SparseCore 0:
  11.2 97.0 all-gather.1
  199.1 13.4 reduce-scatter.1

commit v7 on v6

--- a/solution.py
+++ b/solution.py
@@ -102,8 +102,7 @@
     )
     outbox = select_rows(outbox_select, vision_tokens).reshape(groups, capacity, piece_width)
     received_piece = exchange(outbox, "fsdp").reshape(groups * capacity, piece_width)
-    received_all = gather_by_exchange(received_piece, "seq", seq_count)
-    received = jnp.transpose(received_all, (1, 0, 2)).reshape(groups * capacity, width)
+    received = lax.all_gather(received_piece, "seq", axis=1, tiled=True)
     occupied = (
         (jnp.arange(capacity, dtype=jnp.int32)[None, :] < arrived).astype(jnp.int32).reshape(-1)
     )

time: 280 us -> 281 us (level)
  blocking collectives: 101 us -> 106 us
  starting transfers between devices: 29.7 us -> 26.6 us
    all_to_all x5 -> x4, waiting for transfers between devices: 73.8 us -> 47.3 us  [exchange(): lax.all_to_all(rows, axis_name, split_axis=0, concat_axis=0, tiled=True)]
    all_gather x1, waiting for transfers between devices: 0.02 us -> 24.5 us  [local(): lax.all_gather(w_value, 'fsdp', axis=0, tiled=True)]
    all_to_all x4, blocking collectives: 101 us -> 106 us  [exchange(): lax.all_to_all(rows, axis_name, split_axis=0, concat_axis=0, tiled=True)]
    all_to_all x5 -> x4, starting transfers between devices: 29.4 us -> 26.2 us  [exchange(): lax.all_to_all(rows, axis_name, split_axis=0, concat_axis=0, tiled=True)]
    unnamed x21 -> x19, local copies, waits for them, and re-layouts: 7.11 us -> 7.1 us
  transfers between devices with their start and end apart: 7 -> 7, of which waited for: 6 -> 6; matrix products, arithmetic and copies ran while one was open for 9% -> 7% of each run, Pallas kernels for 0% -> 0%
where the time goes in v7:
time: 281 us; the launch traced here: 280 us
  blocking collectives  106 us (38%)
  waiting for transfers between devices  88 us (31%)
  starting transfers between devices  26.6 us (9%)
  between operations  16.1 us (6%)
  local copies, waits for them, and re-layouts  15.1 us (5%)
  other arithmetic  14.8 us (5%)
  matrix products  13.6 us (5%)
    all_to_all x4, blocking collectives, exchange(): lax.all_to_all(rows, axis_name, split_axis=0, concat_axis=0, tiled=True)  106 us
    all_to_all x4, waiting for transfers between devices, exchange(): lax.all_to_all(rows, axis_name, split_axis=0, concat_axis=0, tiled=True)  47.3 us
    all_to_all x4, starting transfers between devices, exchange(): lax.all_to_all(rows, axis_name, split_axis=0, concat_axis=0, tiled=True)  26.2 us
    all_gather x1, waiting for transfers between devices, local(): lax.all_gather(w_value, 'fsdp', axis=0, tiled=True)  24.5 us
    reduce_scatter x1, waiting for transfers between devices, local(): lax.psum_scatter(partial_out, 'seq', scatter_dimension=0, tiled=True)  15.4 us
    unnamed x19, local copies, waits for them, and re-layouts  7.1 us
  transfers between devices with their start and end apart: 7, of which 6 were waited for; matrix products, arithmetic and copies ran while one was open for 7% of the time, Pallas kernels for 0%

profile of v7, /device:TPU:1, one launch (start us, length us, event | category | flops | bytes accessed | tf_op | source)
XLA Modules:
  0.0 280.3 jit_solution(3312572786251778090)
XLA Ops:
  7.2 0.9 fusion.18
  8.1 0.2 reduce_window_sum.32
  8.3 0.8 fusion.20
  9.1 0.7 multiply_add_fusion
  9.8 1.2 convolution_convert_fusion.1
  11.1 0.2 reshape.184
  11.3 38.8 %all_to_all.50 = bf16[128,2,1024]{2,1,0:T(2,128)(2,1)S(1)} all-to-all(bf16[128,2,1024]{2,1,0:T(2,128)(2,1)S(1)} %reshape.184), channel_id=1, replica_groups=mesh['fsdp'=128,'seq'=4] {'fsdp'}, dimensions={0} | all-to-all | bytes 1048576 | tf_op jit(solution)/shard_map/all_to_all | solution.py:24
  50.1 1.0 reshape.185
  51.1 0.7 all-gather.5.cloned.1.call-update
  52.5 1.5 multiply_reduce_fusion.1
  54.7 0.9 fusion.31
  56.0 17.9 %all_to_all.51 = bf16[128,3,32]{2,1,0:T(4,128)(2,1)S(1)} all-to-all(bf16[128,3,32]{2,1,0:T(4,128)(2,1)S(1)} %copy.74), channel_id=1, replica_groups=mesh['fsdp'=128,'seq'=4] {'fsdp'}, dimensions={0} | all-to-all | bytes 49152 | tf_op jit(solution)/shard_map/all_to_all | solution.py:24
  74.2 0.2 convolution_bitcast_fusion
  74.4 1.0 copy.77
  75.4 5.6 %all-to-all-start.1 = ((f32[128,1,512]{2,1,0:T(1,128)}), f32[128,1,512]{2,1,0:T(1,128)S(1)}, u32[]{:S(2)}, u32[]{:S(2)}) async-start(f32[128,1,512]{2,1,0:T(1,128)} %copy.77), calls=%async_computation.1 | async-start | bytes 524288 | tf_op jit(solution)/shard_map/all_to_all | solution.py:24
  81.8 2.4 fusion.16
  84.3 0.2 lt.65
  84.5 0.3 reduce-window.9
  84.9 11.4 %all-to-all-done.1 = f32[128,1,512]{2,1,0:T(1,128)S(1)} async-done(((f32[128,1,512]{2,1,0:T(1,128)}), f32[128,1,512]{2,1,0:T(1,128)S(1)}, u32[]{:S(2)}, u32[]{:S(2)}) %all-to-all-start.1) | async-done | bytes 262176 | tf_op jit(solution)/shard_map/all_to_all | solution.py:24
  96.3 0.2 reduce_sum.76
  96.5 0.1 broadcast_in_dim.38
  96.7 0.5 broadcast.86
  97.2 1.4 reduce.12
  98.6 0.7 reshape.199
  99.3 5.7 %all-to-all-start.2 = ((bf16[128,2,256]{2,1,0:T(2,128)(2,1)}), bf16[128,2,256]{2,1,0:T(2,128)(2,1)S(1)}, u32[]{:S(2)}, u32[]{:S(2)}) async-start(bf16[128,2,256]{2,1,0:T(2,128)(2,1)} %reshape.199), calls=%async_computation.2 | async-start | bytes 262144 | tf_op jit(solution)/shard_map/all_to_all | solution.py:24
  105.3 12.9 %all-to-all-done.2 = bf16[128,2,256]{2,1,0:T(2,128)(2,1)S(1)} async-done(((bf16[128,2,256]{2,1,0:T(2,128)(2,1)}), bf16[128,2,256]{2,1,0:T(2,128)(2,1)S(1)}, u32[]{:S(2)}, u32[]{:S(2)}) %all-to-all-start.2) | async-done | bytes 131104 | tf_op jit(solution)/shard_map/all_to_all | solution.py:24
  118.3 0.2 copy.78
  118.5 0.1 convolution_bitcast_fusion.1
  118.7 0.2 copy.81
  118.8 0.8 reshape.201
  119.7 5.6 %all-to-all-start.3 = ((f32[128,1,128]{2,1,0:T(1,128)}), f32[128,1,128]{2,1,0:T(1,128)S(1)}, u32[]{:S(2)}, u32[]{:S(2)}) async-start(f32[128,1,128]{2,1,0:T(1,128)} %reshape.201), calls=%async_computation.3 | async-start | bytes 131072 | tf_op jit(solution)/shard_map/all_to_all | solution.py:24
  125.3 0.2 fusion.11
  125.5 11.3 %all-to-all-done.3 = f32[128,1,128]{2,1,0:T(1,128)S(1)} async-done(((f32[128,1,128]{2,1,0:T(1,128)}), f32[128,1,128]{2,1,0:T(1,128)S(1)}, u32[]{:S(2)}, u32[]{:S(2)}) %all-to-all-start.3) | async-done | bytes 65568 | tf_op jit(solution)/shard_map/all_to_all | solution.py:24
  136.7 0.5 broadcast.87
  137.3 0.8 reduce.13
  138.1 0.2 reshape.202
  138.3 0.2 reshape.182
  138.5 3.3 %fusion.1 = (f32[280]{0:T(512)S(1)}, bf16[280,4096]{1,0:T(8,128)(2,1)S(1)}) fusion(bf16[280,4096]{1,0:T(8,128)(2,1)} %param.12, bf16[256,4096]{1,0:T(8,128)(2,1)} %all-gather.3.cloned.1.call-done, s32[256]{0:T(256)S(1)} %compare_select_fusion, pred[280]{0:T(512)(128)(4,1)S(1)} %fusion.11), kind=kOutput, calls=%fused_computation.4 | convolution fusion | flops 593008384 | bytes 6687096 | tf_op jit(solution)/shard_map/dot_general | solution.py:33
  141.8 2.1 fusion.33
  143.9 0.2 fusion.26
  144.2 24.5 %all-gather.5.cloned.1.call-done = bf16[4096,512]{1,0:T(8,128)(2,1)} async-done(((bf16[32,512]{1,0:T(8,128)(2,1)}), bf16[4096,512]{1,0:T(8,128)(2,1)}) %all-gather.5.cloned.1.call-update) | async-done | bytes 4194320 | tf_op jit(solution)/shard_map/all_gather | solution.py:119
  168.7 4.3 %fusion.4 = bf16[35,4,8,128]{3,2,1,0:T(8,128)(2,1)S(1)} fusion(bf16[4096,512]{1,0:T(8,128)(2,1)} %all-gather.5.cloned.1.call-done, bf16[280,4096]{1,0:T(8,128)(2,1)} %copy-done.4, f32[4096]{0:T(1024)S(1)} %copy-done.3, f32[280]{0:T(512)S(1)} %add_rsqrt_fusion), kind=kOutput, calls=%fused_computation.10 | convolution fusion | flops 1179136000 | bytes 6792288 | tf_op jit(solution)/shard_map/dot_general | solution.py:117
  173.0 0.1 fusion.8
  173.2 0.1 broadcast_in_dim.43
  173.3 1.4 reduce.14
  174.7 0.7 reshape.203
  175.4 9.4 %all-to-all-start.5 = ((bf16[128,2,256]{2,1,0:T(2,128)(2,1)}), bf16[128,2,256]{2,1,0:T(2,128)(2,1)S(1)}, u32[]{:S(2)}, u32[]{:S(2)}) async-start(bf16[128,2,256]{2,1,0:T(2,128)(2,1)} %reshape.203), calls=%async_computation.5 | async-start | bytes 262144 | tf_op jit(solution)/shard_map/all_to_all | solution.py:24
  184.8 0.3 reduce-scatter.2.cloned.1.call-start
  185.1 0.8 dynamic_slice.15
  185.8 11.7 %all-to-all-done.5 = bf16[128,2,256]{2,1,0:T(2,128)(2,1)S(1)} async-done(((bf16[128,2,256]{2,1,0:T(2,128)(2,1)}), bf16[128,2,256]{2,1,0:T(2,128)(2,1)S(1)}, u32[]{:S(2)}, u32[]{:S(2)}) %all-to-all-start.5) | async-done | bytes 131104 | tf_op jit(solution)/shard_map/all_to_all | solution.py:24
  197.6 1.5 fusion.13
  199.2 15.4 %reduce-scatter.2.cloned.1.call-done = f32[32,32]{1,0:T(8,128)} async-done(((f32[128,32]{1,0:T(8,128)}), f32[32,32]{1,0:T(8,128)}) %reduce-scatter.2.cloned.1.call-update) | async-done | bytes 4112 | tf_op jit(solution)/shard_map/reduce_scatter | solution.py:140
  214.7 0.8 multiply_convert_fusion
  215.8 0.1 broadcast_in_dim.44
  215.9 1.6 reshape.205
  217.5 33.0 %all_to_all.52 = bf16[128,2,544]{2,1,0:T(2,128)(2,1)} all-to-all(bf16[128,2,544]{2,1,0:T(2,128)(2,1)S(1)} %reshape.205), channel_id=1, replica_groups=mesh['fsdp'=128,'seq'=4] {'fsdp'}, dimensions={0} | all-to-all | bytes 557056 | tf_op jit(solution)/shard_map/all_to_all | solution.py:24
  250.5 2.9 %reshape.206 = bf16[128,32,34]{2,1,0:T(8,128)(2,1)S(1)} reshape(bf16[128,2,544]{2,1,0:T(2,128)(2,1)} %all_to_all.52) | data formatting | bytes 557056
  253.5 0.5 convert_reduce_fusion
  254.0 0.4 copy.85
  254.4 1.1 reshape.187
  255.5 0.6 convolution_reduce_fusion
  256.1 0.5 rsqrt_multiply_fusion
  256.7 16.5 %all_to_all.53 = f32[128,1,32]{2,1,0:T(1,128)S(1)} all-to-all(f32[128,1,32]{2,1,0:T(1,128)S(1)} %broadcast_in_dim.45), channel_id=1, replica_groups=mesh['fsdp'=128,'seq'=4] {'fsdp'}, dimensions={0} | all-to-all | bytes 32768 | tf_op jit(solution)/shard_map/all_to_all | solution.py:24
  273.1 0.7 reduce_max.29
  (49 shorter events, 2.3 us)
Async XLA Ops:
  7.2 248.4 %copy-start = (bf16[4096,250]{1,0:T(8,128)(2,1)S(1)}, bf16[4096,250]{1,0:T(8,128)(2,1)}, u32[]{:S(2)}) copy-start(bf16[4096,250]{1,0:T(8,128)(2,1)} %param.23) | copy-start | bytes 6144004
  7.2 131.3 %all-gather.3.cloned.1.call-start = ((), (), s32[]{:S(2)}) async-start(), calls=%async_computation.9 | async-start | bytes 2621440 | tf_op jit(solution)/shard_map/all_gather | solution.py:105
  8.3 46.4 %copy-start.3 = (f32[4096]{0:T(1024)S(1)}, f32[4096]{0:T(1024)}, u32[]{:S(2)}) copy-start(f32[4096]{0:T(1024)} %param.17) | copy-start | bytes 49156
  11.0 63.1 %copy-start.1 = (bf16[32,512]{1,0:T(8,128)(2,1)S(1)}, bf16[32,512]{1,0:T(8,128)(2,1)}, u32[]{:S(2)}) copy-start(bf16[32,512]{1,0:T(8,128)(2,1)} %param.18) | copy-start | bytes 98308
  51.1 117.6 %all-gather.5.cloned.1.call-start = ((), (), s32[]{:S(2)}) async-start(), calls=%async_computation.10 | async-start | bytes 4227072 | tf_op jit(solution)/shard_map/all_gather | solution.py:119
  56.0 62.5 %copy-start.2 = (bf16[32,512]{1,0:T(8,128)(2,1)S(1)}, bf16[32,512]{1,0:T(8,128)(2,1)}, u32[]{:S(2)}) copy-start(bf16[32,512]{1,0:T(8,128)(2,1)} %param.19) | copy-start | bytes 98308
  75.4 20.9 %all-to-all-start.1 = ((f32[128,1,512]{2,1,0:T(1,128)}), f32[128,1,512]{2,1,0:T(1,128)S(1)}, u32[]{:S(2)}, u32[]{:S(2)}) async-start(f32[128,1,512]{2,1,0:T(1,128)} %copy.77), calls=%async_computation.1 | async-start | bytes 524288 | tf_op jit(solution)/shard_map/all_to_all | solution.py:24
  99.3 19.0 %all-to-all-start.2 = ((bf16[128,2,256]{2,1,0:T(2,128)(2,1)}), bf16[128,2,256]{2,1,0:T(2,128)(2,1)S(1)}, u32[]{:S(2)}, u32[]{:S(2)}) async-start(bf16[128,2,256]{2,1,0:T(2,128)(2,1)} %reshape.199), calls=%async_computation.2 | async-start | bytes 262144 | tf_op jit(solution)/shard_map/all_to_all | solution.py:24
  119.7 17.1 %all-to-all-start.3 = ((f32[128,1,128]{2,1,0:T(1,128)}), f32[128,1,128]{2,1,0:T(1,128)S(1)}, u32[]{:S(2)}, u32[]{:S(2)}) async-start(f32[128,1,128]{2,1,0:T(1,128)} %reshape.201), calls=%async_computation.3 | async-start | bytes 131072 | tf_op jit(solution)/shard_map/all_to_all | solution.py:24
  141.8 2.1 copy-start.4
  175.4 22.1 %all-to-all-start.5 = ((bf16[128,2,256]{2,1,0:T(2,128)(2,1)}), bf16[128,2,256]{2,1,0:T(2,128)(2,1)S(1)}, u32[]{:S(2)}, u32[]{:S(2)}) async-start(bf16[128,2,256]{2,1,0:T(2,128)(2,1)} %reshape.203), calls=%async_computation.5 | async-start | bytes 262144 | tf_op jit(solution)/shard_map/all_to_all | solution.py:24
  184.8 29.9 %reduce-scatter.2.cloned.1.call-start = ((), (), s32[]{:S(2)}) async-start(), calls=%async_computation.11 | async-start | bytes 81920 | tf_op jit(solution)/shard_map/reduce_scatter | solution.py:140
Sparse Core Ops, SparseCore 0:
  51.2 28.6 all-gather.2
  83.0 85.6 all-gather.4
  199.3 15.2 reduce-scatter.1

commit v8 on v6

--- a/solution.py
+++ b/solution.py
@@ -147,7 +147,9 @@
     square_high = square_part.astype(jnp.bfloat16)
     square_low = (square_part - square_high.astype(jnp.float32)).astype(jnp.bfloat16)
     payload = jnp.concatenate([scaled_part, square_high, square_low], axis=1)
-    payload_all = gather_by_exchange(payload, "fsdp", groups)
+    payload_all = gather_by_exchange(payload.reshape(-1), "fsdp", groups).reshape(
+        (groups,) + payload.shape
+    )
     scaled_out = jnp.transpose(payload_all[:, :, :dpiece], (1, 0, 2)).reshape(quarter, width)
     square_sum = jnp.sum(
         payload_all[:, :, dpiece:].astype(jnp.float32), axis=(0, 2)

time: 280 us -> 280 us (level)
    unnamed x21, local copies, waits for them, and re-layouts: 7.11 us -> 3.53 us
where the time goes in v8:
time: 280 us; the launch traced here: 279 us
  blocking collectives  101 us (36%)
  waiting for transfers between devices  88.2 us (32%)
  starting transfers between devices  29.7 us (11%)
  between operations  16.5 us (6%)
  other arithmetic  16 us (6%)
  local copies, waits for them, and re-layouts  13.8 us (5%)
  matrix products  13.4 us (5%)
    all_to_all x4, blocking collectives, exchange(): lax.all_to_all(rows, axis_name, split_axis=0, concat_axis=0, tiled=True)  101 us
    all_to_all x5, waiting for transfers between devices, exchange(): lax.all_to_all(rows, axis_name, split_axis=0, concat_axis=0, tiled=True)  73.8 us
    all_to_all x5, starting transfers between devices, exchange(): lax.all_to_all(rows, axis_name, split_axis=0, concat_axis=0, tiled=True)  29.4 us
    reduce_scatter x1, waiting for transfers between devices, local(): lax.psum_scatter(partial_out, 'seq', scatter_dimension=0, tiled=True)  13.6 us
  transfers between devices with their start and end apart: 7, of which 6 were waited for; matrix products, arithmetic and copies ran while one was open for 9% of the time, Pallas kernels for 0%

profile of v8, /device:TPU:1, one launch (start us, length us, event | category | flops | bytes accessed | tf_op | source)
XLA Modules:
  0.0 278.5 jit_solution(10407712970428165834)
XLA Ops:
  7.2 0.7 all-gather.2.cloned.1.call-update
  8.6 1.5 multiply_reduce_fusion.1
  10.8 0.9 fusion.31
  11.9 0.7 fusion.18
  12.6 0.2 reduce_window_sum.32
  12.8 0.8 fusion.20
  13.9 31.1 %all_to_all.56 = bf16[128,3,32]{2,1,0:T(4,128)(2,1)S(1)} all-to-all(bf16[128,3,32]{2,1,0:T(4,128)(2,1)S(1)} %copy.84), channel_id=1, replica_groups=mesh['fsdp'=128,'seq'=4] {'fsdp'}, dimensions={0} | all-to-all | bytes 49152 | tf_op jit(solution)/shard_map/all_to_all | solution.py:24
  45.2 1.0 convolution_bitcast_fusion
  46.2 0.3 copy.87
  46.4 20.4 %all_to_all.57 = f32[128,1,512]{2,1,0:T(1,128)S(1)} all-to-all(f32[128,1,512]{2,1,0:T(1,128)S(1)} %copy.87), channel_id=1, replica_groups=mesh['fsdp'=128,'seq'=4] {'fsdp'}, dimensions={0} | all-to-all | bytes 524288 | tf_op jit(solution)/shard_map/all_to_all | solution.py:24
  66.8 0.2 reduce_sum.76
  67.2 0.5 broadcast.88
  67.7 1.3 reduce.12
  69.0 0.7 reshape.212
  69.7 5.5 %all-to-all-start.2 = ((bf16[128,2,256]{2,1,0:T(2,128)(2,1)}), bf16[128,2,256]{2,1,0:T(2,128)(2,1)S(1)}, u32[]{:S(2)}, u32[]{:S(2)}) async-start(bf16[128,2,256]{2,1,0:T(2,128)(2,1)} %reshape.212), calls=%async_computation.2 | async-start | bytes 262144 | tf_op jit(solution)/shard_map/all_to_all | solution.py:24
  75.3 0.3 convolution_convert_fusion.1
  75.6 1.0 reshape.196
  76.6 12.4 %all-to-all-done.2 = bf16[128,2,256]{2,1,0:T(2,128)(2,1)S(1)} async-done(((bf16[128,2,256]{2,1,0:T(2,128)(2,1)}), bf16[128,2,256]{2,1,0:T(2,128)(2,1)S(1)}, u32[]{:S(2)}, u32[]{:S(2)}) %all-to-all-start.2) | async-done | bytes 131104 | tf_op jit(solution)/shard_map/all_to_all | solution.py:24
  89.0 5.6 %all-to-all-start.4 = ((bf16[128,2,1024]{2,1,0:T(2,128)(2,1)}), bf16[128,2,1024]{2,1,0:T(2,128)(2,1)S(1)}, u32[]{:S(2)}, u32[]{:S(2)}) async-start(bf16[128,2,1024]{2,1,0:T(2,128)(2,1)} %reshape.196), calls=%async_computation.4 | async-start | bytes 1048576 | tf_op jit(solution)/shard_map/all_to_all | solution.py:24
  94.7 0.2 copy.88
  95.0 0.2 copy.91
  95.2 0.8 reshape.214
  96.0 18.9 %all-to-all-done.4 = bf16[128,2,1024]{2,1,0:T(2,128)(2,1)S(1)} async-done(((bf16[128,2,1024]{2,1,0:T(2,128)(2,1)}), bf16[128,2,1024]{2,1,0:T(2,128)(2,1)S(1)}, u32[]{:S(2)}, u32[]{:S(2)}) %all-to-all-start.4) | async-done | bytes 524320 | tf_op jit(solution)/shard_map/all_to_all | solution.py:24
  114.9 7.3 %all-to-all-start.3 = ((f32[128,1,128]{2,1,0:T(1,128)}), f32[128,1,128]{2,1,0:T(1,128)S(1)}, u32[]{:S(2)}, u32[]{:S(2)}) async-start(f32[128,1,128]{2,1,0:T(1,128)} %reshape.214), calls=%async_computation.3 | async-start | bytes 131072 | tf_op jit(solution)/shard_map/all_to_all | solution.py:24
  122.2 0.2 broadcast_in_dim.47
  122.4 0.2 copy.93
  122.6 11.0 %all-to-all-done.3 = f32[128,1,128]{2,1,0:T(1,128)S(1)} async-done(((f32[128,1,128]{2,1,0:T(1,128)}), f32[128,1,128]{2,1,0:T(1,128)S(1)}, u32[]{:S(2)}, u32[]{:S(2)}) %all-to-all-start.3) | async-done | bytes 65568 | tf_op jit(solution)/shard_map/all_to_all | solution.py:24
  133.6 1.5 broadcast_in_dim.48
  135.1 4.4 %all-to-all-start.5 = ((bf16[4,256,1024]{1,2,0:T(8,128)(2,1)}), bf16[4,256,1024]{1,2,0:T(8,128)(2,1)}, u32[]{:S(2)}, u32[]{:S(2)}) async-start(bf16[4,256,1024]{1,2,0:T(8,128)(2,1)} %broadcast_in_dim.48), calls=%async_computation.5 | async-start | bytes 4194304 | tf_op jit(solution)/shard_map/all_to_all | solution.py:24
  140.4 2.4 fusion.16
  142.9 0.2 lt.65
  143.1 0.3 reduce-window.9
  143.9 0.2 fusion.11
  144.1 0.5 broadcast.89
  144.6 0.8 reduce.13
  145.4 0.2 reshape.215
  145.6 0.2 reshape.194
  145.7 19.7 %all-to-all-done.5 = bf16[4,256,1024]{1,2,0:T(8,128)(2,1)} async-done(((bf16[4,256,1024]{1,2,0:T(8,128)(2,1)}), bf16[4,256,1024]{1,2,0:T(8,128)(2,1)}, u32[]{:S(2)}, u32[]{:S(2)}) %all-to-all-start.5) | async-done | bytes 2097184 | tf_op jit(solution)/shard_map/all_to_all | solution.py:24
  165.5 3.3 %fusion.1 = (f32[280]{0:T(512)S(1)}, bf16[280,4096]{1,0:T(8,128)(2,1)S(1)}) fusion(bf16[280,4096]{1,0:T(8,128)(2,1)} %param.12, bf16[256,4096]{0,1:T(8,128)(2,1)} %bitcast.12, s32[256]{0:T(256)S(1)} %compare_select_fusion, pred[280]{0:T(512)(128)(4,1)S(1)} %fusion.11), kind=kOutput, calls=%fused_computation.4 | convolution fusion | flops 593008384 | bytes 6687096 | tf_op jit(solution)/shard_map/dot_general | solution.py:33
  168.8 2.1 fusion.33
  171.0 0.2 fusion.26
  171.2 4.3 %fusion.4 = bf16[35,4,8,128]{3,2,1,0:T(8,128)(2,1)S(1)} fusion(bf16[4096,512]{1,0:T(8,128)(2,1)} %all-gather.2.cloned.1.call-done, bf16[280,4096]{1,0:T(8,128)(2,1)} %copy-done.5, f32[4096]{0:T(1024)S(1)} %copy-done.3, f32[280]{0:T(512)S(1)} %add_rsqrt_fusion), kind=kOutput, calls=%fused_computation.9 | convolution fusion | flops 1179136000 | bytes 6792288 | tf_op jit(solution)/shard_map/dot_general | solution.py:118
  175.9 1.3 reduce.14
  177.2 0.7 reshape.216
  177.9 6.6 %all-to-all-start.6 = ((bf16[128,2,256]{2,1,0:T(2,128)(2,1)}), bf16[128,2,256]{2,1,0:T(2,128)(2,1)S(1)}, u32[]{:S(2)}, u32[]{:S(2)}) async-start(bf16[128,2,256]{2,1,0:T(2,128)(2,1)} %reshape.216), calls=%async_computation.6 | async-start | bytes 262144 | tf_op jit(solution)/shard_map/all_to_all | solution.py:24
  184.5 0.3 reduce-scatter.2.cloned.1.call-start
  184.8 0.8 dynamic_slice.15
  185.5 11.8 %all-to-all-done.6 = bf16[128,2,256]{2,1,0:T(2,128)(2,1)S(1)} async-done(((bf16[128,2,256]{2,1,0:T(2,128)(2,1)}), bf16[128,2,256]{2,1,0:T(2,128)(2,1)S(1)}, u32[]{:S(2)}, u32[]{:S(2)}) %all-to-all-start.6) | async-done | bytes 131104 | tf_op jit(solution)/shard_map/all_to_all | solution.py:24
  197.4 1.5 fusion.13
  199.0 13.6 %reduce-scatter.2.cloned.1.call-done = f32[32,32]{1,0:T(8,128)} async-done(((f32[128,32]{1,0:T(8,128)}), f32[32,32]{1,0:T(8,128)}) %reduce-scatter.2.cloned.1.call-update) | async-done | bytes 4112 | tf_op jit(solution)/shard_map/reduce_scatter | solution.py:141
  212.7 0.8 multiply_convert_fusion
  213.9 0.3 broadcast_in_dim.87
  214.2 2.4 reduce.15
  216.6 0.3 reshape.218
  217.0 32.9 %all_to_all.58 = bf16[128,2,544]{2,1,0:T(2,128)(2,1)S(1)} all-to-all(bf16[128,2,544]{2,1,0:T(2,128)(2,1)S(1)} %reshape.218), channel_id=1, replica_groups=mesh['fsdp'=128,'seq'=4] {'fsdp'}, dimensions={0} | all-to-all | bytes 557056 | tf_op jit(solution)/shard_map/all_to_all | solution.py:24
  249.9 0.5 reshape.219
  250.4 0.9 copy.96
  251.5 0.3 convert_reduce_fusion
  251.8 0.5 copy.97
  252.3 1.1 reshape.200
  253.4 0.6 convolution_reduce_fusion
  254.0 0.5 rsqrt_multiply_fusion
  254.6 16.5 %all_to_all.59 = f32[128,1,32]{2,1,0:T(1,128)S(1)} all-to-all(f32[128,1,32]{2,1,0:T(1,128)S(1)} %broadcast_in_dim.88), channel_id=1, replica_groups=mesh['fsdp'=128,'seq'=4] {'fsdp'}, dimensions={0} | all-to-all | bytes 32768 | tf_op jit(solution)/shard_map/all_to_all | solution.py:24
  271.0 0.7 reduce_max.29
  (56 shorter events, 2.9 us)
Async XLA Ops:
  7.2 246.2 %copy-start = (bf16[4096,250]{1,0:T(8,128)(2,1)S(1)}, bf16[4096,250]{1,0:T(8,128)(2,1)}, u32[]{:S(2)}) copy-start(bf16[4096,250]{1,0:T(8,128)(2,1)} %param.23) | copy-start | bytes 6144004
  7.2 68.1 %copy-start.4 = (s32[128,1]{0,1:T(1,128)S(1)}, s32[128,1]{0,1:T(1,128)}, u32[]{:S(2)}) copy-start(s32[128,1]{0,1:T(1,128)} %param.14) | copy-start | bytes 1540
  7.2 68.1 %copy-start.1 = (bf16[128,1024]{1,0:T(8,128)(2,1)S(1)}, bf16[128,1024]{1,0:T(8,128)(2,1)}, u32[]{:S(2)}) copy-start(bf16[128,1024]{1,0:T(8,128)(2,1)} %param.13) | copy-start | bytes 786436
  7.2 164.0 %all-gather.2.cloned.1.call-start = ((), (), s32[]{:S(2)}) async-start(), calls=%async_computation.10 | async-start | bytes 4227072 | tf_op jit(solution)/shard_map/all_gather | solution.py:120
  67.7 27.1 %copy-start.2 = (bf16[32,512]{1,0:T(8,128)(2,1)S(1)}, bf16[32,512]{1,0:T(8,128)(2,1)}, u32[]{:S(2)}) copy-start(bf16[32,512]{1,0:T(8,128)(2,1)} %param.19) | copy-start | bytes 98308
  69.7 19.2 %all-to-all-start.2 = ((bf16[128,2,256]{2,1,0:T(2,128)(2,1)}), bf16[128,2,256]{2,1,0:T(2,128)(2,1)S(1)}, u32[]{:S(2)}, u32[]{:S(2)}) async-start(bf16[128,2,256]{2,1,0:T(2,128)(2,1)} %reshape.212), calls=%async_computation.2 | async-start | bytes 262144 | tf_op jit(solution)/shard_map/all_to_all | solution.py:24
  89.0 25.9 %all-to-all-start.4 = ((bf16[128,2,1024]{2,1,0:T(2,128)(2,1)}), bf16[128,2,1024]{2,1,0:T(2,128)(2,1)S(1)}, u32[]{:S(2)}, u32[]{:S(2)}) async-start(bf16[128,2,1024]{2,1,0:T(2,128)(2,1)} %reshape.196), calls=%async_computation.4 | async-start | bytes 1048576 | tf_op jit(solution)/shard_map/all_to_all | solution.py:24
  114.9 18.7 %all-to-all-start.3 = ((f32[128,1,128]{2,1,0:T(1,128)}), f32[128,1,128]{2,1,0:T(1,128)S(1)}, u32[]{:S(2)}, u32[]{:S(2)}) async-start(f32[128,1,128]{2,1,0:T(1,128)} %reshape.214), calls=%async_computation.3 | async-start | bytes 131072 | tf_op jit(solution)/shard_map/all_to_all | solution.py:24
  135.1 30.4 %all-to-all-start.5 = ((bf16[4,256,1024]{1,2,0:T(8,128)(2,1)}), bf16[4,256,1024]{1,2,0:T(8,128)(2,1)}, u32[]{:S(2)}, u32[]{:S(2)}) async-start(bf16[4,256,1024]{1,2,0:T(8,128)(2,1)} %broadcast_in_dim.48), calls=%async_computation.5 | async-start | bytes 4194304 | tf_op jit(solution)/shard_map/all_to_all | solution.py:24
  165.5 3.4 %copy-start.3 = (f32[4096]{0:T(1024)S(1)}, f32[4096]{0:T(1024)}, u32[]{:S(2)}) copy-start(f32[4096]{0:T(1024)} %param.17) | copy-start | bytes 49156
  168.8 2.1 copy-start.5
  177.9 19.4 %all-to-all-start.6 = ((bf16[128,2,256]{2,1,0:T(2,128)(2,1)}), bf16[128,2,256]{2,1,0:T(2,128)(2,1)S(1)}, u32[]{:S(2)}, u32[]{:S(2)}) async-start(bf16[128,2,256]{2,1,0:T(2,128)(2,1)} %reshape.216), calls=%async_computation.6 | async-start | bytes 262144 | tf_op jit(solution)/shard_map/all_to_all | solution.py:24
  184.5 28.2 %reduce-scatter.2.cloned.1.call-start = ((), (), s32[]{:S(2)}) async-start(), calls=%async_computation.11 | async-start | bytes 81920 | tf_op jit(solution)/shard_map/reduce_scatter | solution.py:141
Sparse Core Ops, SparseCore 0:
  11.2 97.0 all-gather.1
  199.1 13.4 reduce-scatter.1

commit v9 on v7

--- a/solution.py
+++ b/solution.py
@@ -85,6 +85,8 @@
 
     query_partial = jnp.dot(normed_part, w_query, preferred_element_type=jnp.float32)
     query_mine = jnp.sum(exchange(query_partial, "fsdp"), axis=0).astype(jnp.bfloat16)
+    value_weights = lax.all_gather(w_value, "fsdp", axis=0, tiled=True)
+    query_mine, value_weights = lax.optimization_barrier((query_mine, value_weights))
     query_all = gather_by_exchange(query_mine, "fsdp", groups)
 
     query_heads = query_all.astype(jnp.float32).reshape(groups, heads_local, HD)
@@ -116,7 +118,7 @@
 
     value_sum = jnp.dot(
         normed,
-        lax.all_gather(w_value, "fsdp", axis=0, tiled=True),
+        value_weights,
         preferred_element_type=jnp.float32,
     )
     value_heads = value_sum.astype(jnp.bfloat16).reshape(seq_len, heads_local, HD)

time: 281 us -> 286 us (1.018)
  blocking collectives: 106 us -> 88.7 us
  starting transfers between devices: 26.6 us -> 42.3 us
  matrix products: 13.6 us -> 16.5 us
    all_gather x1, waiting for transfers between devices: 0.02 us -> 22.2 us  [local(): received = lax.all_gather(received_piece, 'seq', axis=1, tiled=True)]
    all_to_all x4 -> x3, blocking collectives: 106 us -> 88.7 us  [exchange(): lax.all_to_all(rows, axis_name, split_axis=0, concat_axis=0, tiled=True)]
    all_gather x1, waiting for transfers between devices: 24.5 us -> 7.08 us  [local(): value_weights = lax.all_gather(w_value, 'fsdp', axis=0, tiled=True)]
    all_to_all x4 -> x5, starting transfers between devices: 26.2 us -> 42 us  [exchange(): lax.all_to_all(rows, axis_name, split_axis=0, concat_axis=0, tiled=True)]
    all_to_all x4 -> x5, waiting for transfers between devices: 47.3 us -> 46.6 us  [exchange(): lax.all_to_all(rows, axis_name, split_axis=0, concat_axis=0, tiled=True)]
    unnamed x19 -> x17, local copies, waits for them, and re-layouts: 7.1 us -> 7.1 us
  transfers between devices with their start and end apart: 7 -> 8, of which waited for: 6 -> 7; matrix products, arithmetic and copies ran while one was open for 7% -> 9% of each run, Pallas kernels for 0% -> 0%
where the time goes in v9:
time: 286 us; the launch traced here: 285 us
  waiting for transfers between devices  90.7 us (32%)
  blocking collectives  88.7 us (31%)
  starting transfers between devices  42.3 us (15%)
  matrix products  16.5 us (6%)
  between operations  16.1 us (6%)
  local copies, waits for them, and re-layouts  15.7 us (5%)
  other arithmetic  14.6 us (5%)
    all_to_all x3, blocking collectives, exchange(): lax.all_to_all(rows, axis_name, split_axis=0, concat_axis=0, tiled=True)  88.7 us
    all_to_all x5, waiting for transfers between devices, exchange(): lax.all_to_all(rows, axis_name, split_axis=0, concat_axis=0, tiled=True)  46.6 us
    all_to_all x5, starting transfers between devices, exchange(): lax.all_to_all(rows, axis_name, split_axis=0, concat_axis=0, tiled=True)  42 us
    all_gather x1, waiting for transfers between devices, local(): received = lax.all_gather(received_piece, 'seq', axis=1, tiled=True)  22.2 us
    reduce_scatter x1, waiting for transfers between devices, local(): lax.psum_scatter(partial_out, 'seq', scatter_dimension=0, tiled=True)  14.2 us
    unnamed x17, local copies, waits for them, and re-layouts  7.1 us
    all_gather x1, waiting for transfers between devices, local(): value_weights = lax.all_gather(w_value, 'fsdp', axis=0, tiled=True)  7.08 us
    dot_general x2, matrix products, select_rows(): jnp.dot(selector.astype(jnp.bfloat16), rows, preferred_element_type=jnp.f...  5.85 us
  transfers between devices with their start and end apart: 8, of which 7 were waited for; matrix products, arithmetic and copies ran while one was open for 9% of the time, Pallas kernels for 0%

profile of v9, /device:TPU:1, one launch (start us, length us, event | category | flops | bytes accessed | tf_op | source)
XLA Modules:
  0.0 284.8 jit_solution(2833047957837101930)
XLA Ops:
  7.2 0.7 all-gather.3.cloned.1.call-update
  8.0 0.7 fusion.18
  8.7 0.2 reduce_window_sum.32
  8.9 0.8 select_reduce_fusion
  9.7 0.7 multiply_add_fusion
  10.4 1.2 convolution_convert_fusion.1
  11.6 0.2 reshape.181
  11.8 39.2 %all_to_all.50 = bf16[128,2,1024]{2,1,0:T(2,128)(2,1)S(1)} all-to-all(bf16[128,2,1024]{2,1,0:T(2,128)(2,1)S(1)} %reshape.181), channel_id=1, replica_groups=mesh['fsdp'=128,'seq'=4] {'fsdp'}, dimensions={0} | all-to-all | bytes 1048576 | tf_op jit(solution)/shard_map/all_to_all | solution.py:24
  51.1 1.0 reshape.182
  52.8 1.5 multiply_reduce_fusion.1
  54.9 0.9 fusion.31
  56.2 0.7 copy.74
  56.9 5.4 %all-to-all-start = ((bf16[128,3,32]{2,1,0:T(4,128)(2,1)}), bf16[128,3,32]{2,1,0:T(4,128)(2,1)S(1)}, u32[]{:S(2)}, u32[]{:S(2)}) async-start(bf16[128,3,32]{2,1,0:T(4,128)(2,1)} %copy.74), calls=%async_computation | async-start | bytes 262144 | tf_op jit(solution)/shard_map/all_to_all | solution.py:24
  63.2 11.9 %all-to-all-done = bf16[128,3,32]{2,1,0:T(4,128)(2,1)S(1)} async-done(((bf16[128,3,32]{2,1,0:T(4,128)(2,1)}), bf16[128,3,32]{2,1,0:T(4,128)(2,1)S(1)}, u32[]{:S(2)}, u32[]{:S(2)}) %all-to-all-start) | async-done | bytes 24608 | tf_op jit(solution)/shard_map/all_to_all | solution.py:24
  75.1 2.4 fusion.16
  77.6 0.2 lt.65
  78.0 0.2 convolution_bitcast_fusion
  78.2 1.0 copy.77
  79.2 5.5 %all-to-all-start.1 = ((f32[128,1,512]{2,1,0:T(1,128)}), f32[128,1,512]{2,1,0:T(1,128)S(1)}, u32[]{:S(2)}, u32[]{:S(2)}) async-start(f32[128,1,512]{2,1,0:T(1,128)} %copy.77), calls=%async_computation.1 | async-start | bytes 524288 | tf_op jit(solution)/shard_map/all_to_all | solution.py:24
  84.8 0.3 reduce-window.9
  85.6 0.2 fusion.11
  85.7 15.8 %all-to-all-done.1 = f32[128,1,512]{2,1,0:T(1,128)S(1)} async-done(((f32[128,1,512]{2,1,0:T(1,128)}), f32[128,1,512]{2,1,0:T(1,128)S(1)}, u32[]{:S(2)}, u32[]{:S(2)}) %all-to-all-start.1) | async-done | bytes 262176 | tf_op jit(solution)/shard_map/all_to_all | solution.py:24
  101.5 0.2 reduce_sum.76
  101.7 7.1 %all-gather.3.cloned.1.call-done = bf16[4096,512]{1,0:T(8,128)(2,1)} async-done(((bf16[32,512]{1,0:T(8,128)(2,1)}), bf16[4096,512]{1,0:T(8,128)(2,1)}) %all-gather.3.cloned.1.call-update) | async-done | bytes 4194320 | tf_op jit(solution)/shard_map/all_gather | solution.py:88
  108.9 0.5 broadcast.84
  109.4 1.4 reduce.12
  110.8 0.7 reshape.196
  111.5 10.2 %all-to-all-start.2 = ((bf16[128,2,256]{2,1,0:T(2,128)(2,1)}), bf16[128,2,256]{2,1,0:T(2,128)(2,1)S(1)}, u32[]{:S(2)}, u32[]{:S(2)}) async-start(bf16[128,2,256]{2,1,0:T(2,128)(2,1)} %reshape.196), calls=%async_computation.2 | async-start | bytes 262144 | tf_op jit(solution)/shard_map/all_to_all | solution.py:24
  121.7 22.2 %all-gather.5.cloned.1.call-done = bf16[256,4096]{1,0:T(8,128)(2,1)} async-done(((bf16[256,1024]{1,0:T(8,128)(2,1)}), bf16[256,4096]{1,0:T(8,128)(2,1)}) %all-gather.5.cloned.1.call-update) | async-done | bytes 2097168 | tf_op jit(solution)/shard_map/all_gather | solution.py:107
  143.9 4.6 %fusion.1 = (f32[280]{0:T(512)S(1)}, bf16[280,4096]{1,0:T(8,128)(2,1)}) fusion(bf16[280,4096]{1,0:T(8,128)(2,1)} %param.12, bf16[256,4096]{1,0:T(8,128)(2,1)} %all-gather.5.cloned.1.call-done, s32[256]{0:T(256)S(1)} %compare_select_fusion, pred[280]{0:T(512)(128)(4,1)S(1)} %fusion.11), kind=kOutput, calls=%fused_computation.4 | convolution fusion | flops 593008384 | bytes 6687096 | tf_op jit(solution)/shard_map/dot_general | solution.py:33
  148.7 0.2 copy.78
  148.9 0.1 convolution_bitcast_fusion.1
  149.0 0.2 copy.81
  149.2 0.8 reshape.198
  150.0 14.3 %all-to-all-start.3 = ((f32[128,1,128]{2,1,0:T(1,128)}), f32[128,1,128]{2,1,0:T(1,128)S(1)}, u32[]{:S(2)}, u32[]{:S(2)}) async-start(f32[128,1,128]{2,1,0:T(1,128)} %reshape.198), calls=%async_computation.3 | async-start | bytes 131072 | tf_op jit(solution)/shard_map/all_to_all | solution.py:24
  164.3 4.3 %fusion.4 = bf16[35,4,8,128]{3,2,1,0:T(8,128)(2,1)S(1)} fusion(bf16[4096,512]{1,0:T(8,128)(2,1)} %all-gather.3.cloned.1.call-done, bf16[280,4096]{1,0:T(8,128)(2,1)} %get-tuple-element.17, f32[4096]{0:T(1024)S(1)} %copy-done.3, f32[280]{0:T(512)S(1)} %add_rsqrt_fusion), kind=kOutput, calls=%fused_computation.10 | convolution fusion | flops 1179136000 | bytes 6792288 | tf_op jit(solution)/shard_map/dot_general | solution.py:119
  168.6 7.2 %all-to-all-done.3 = f32[128,1,128]{2,1,0:T(1,128)S(1)} async-done(((f32[128,1,128]{2,1,0:T(1,128)}), f32[128,1,128]{2,1,0:T(1,128)S(1)}, u32[]{:S(2)}, u32[]{:S(2)}) %all-to-all-start.3) | async-done | bytes 65568 | tf_op jit(solution)/shard_map/all_to_all | solution.py:24
  175.7 0.5 broadcast.85
  176.2 0.8 reduce.13
  177.0 0.2 reshape.199
  177.2 0.2 reshape.179
  177.4 3.8 %fusion.33 = (f32[4]{0:T(128)S(1)}, f32[4,280]{1,0:T(4,128)S(1)}) fusion(f32[4,4096]{1,0:T(4,128)S(1)} %reshape.179, bf16[280,4096]{1,0:T(8,128)(2,1)} %get-tuple-element.17, f32[4096]{0:T(1024)S(1)} %copy-done.3, f32[280]{0:T(512)S(1)} %add_rsqrt_fusion, pred[280]{0:T(512)(128)(4,1)S(1)} %iota_compare_fusion.6), kind=kOutput, calls=%fused_computation.72 | convolution fusion | flops 59641116 | bytes 2381576 | tf_op jit(solution)/shard_map/dot_general | solution.py:125
  181.2 0.2 fusion.26
  181.4 0.2 fusion.8
  181.6 0.1 broadcast_in_dim.43
  181.8 1.4 reduce.14
  183.2 0.7 reshape.200
  183.8 6.6 %all-to-all-start.5 = ((bf16[128,2,256]{2,1,0:T(2,128)(2,1)}), bf16[128,2,256]{2,1,0:T(2,128)(2,1)S(1)}, u32[]{:S(2)}, u32[]{:S(2)}) async-start(bf16[128,2,256]{2,1,0:T(2,128)(2,1)} %reshape.200), calls=%async_computation.5 | async-start | bytes 262144 | tf_op jit(solution)/shard_map/all_to_all | solution.py:24
  190.4 0.3 reduce-scatter.2.cloned.1.call-start
  190.7 0.8 dynamic_slice.15
  191.5 11.7 %all-to-all-done.5 = bf16[128,2,256]{2,1,0:T(2,128)(2,1)S(1)} async-done(((bf16[128,2,256]{2,1,0:T(2,128)(2,1)}), bf16[128,2,256]{2,1,0:T(2,128)(2,1)S(1)}, u32[]{:S(2)}, u32[]{:S(2)}) %all-to-all-start.5) | async-done | bytes 131104 | tf_op jit(solution)/shard_map/all_to_all | solution.py:24
  203.3 1.6 fusion.13
  204.9 14.2 %reduce-scatter.2.cloned.1.call-done = f32[32,32]{1,0:T(8,128)} async-done(((f32[128,32]{1,0:T(8,128)}), f32[32,32]{1,0:T(8,128)}) %reduce-scatter.2.cloned.1.call-update) | async-done | bytes 4112 | tf_op jit(solution)/shard_map/reduce_scatter | solution.py:142
  219.1 0.8 multiply_convert_fusion
  220.4 1.6 reshape.202
  222.0 33.0 %all_to_all.51 = bf16[128,2,544]{2,1,0:T(2,128)(2,1)} all-to-all(bf16[128,2,544]{2,1,0:T(2,128)(2,1)S(1)} %reshape.202), channel_id=1, replica_groups=mesh['fsdp'=128,'seq'=4] {'fsdp'}, dimensions={0} | all-to-all | bytes 557056 | tf_op jit(solution)/shard_map/all_to_all | solution.py:24
  254.9 2.9 %reshape.203 = bf16[128,32,34]{2,1,0:T(8,128)(2,1)S(1)} reshape(bf16[128,2,544]{2,1,0:T(2,128)(2,1)} %all_to_all.51) | data formatting | bytes 557056
  257.9 0.5 convert_reduce_fusion
  258.4 0.4 copy.85
  258.8 1.1 reshape.184
  260.0 0.6 convolution_reduce_fusion
  260.5 0.5 rsqrt_multiply_fusion
  261.1 16.5 %all_to_all.52 = f32[128,1,32]{2,1,0:T(1,128)S(1)} all-to-all(f32[128,1,32]{2,1,0:T(1,128)S(1)} %broadcast_in_dim.45), channel_id=1, replica_groups=mesh['fsdp'=128,'seq'=4] {'fsdp'}, dimensions={0} | all-to-all | bytes 32768 | tf_op jit(solution)/shard_map/all_to_all | solution.py:24
  277.6 0.7 reduce_max.29
  (48 shorter events, 2.4 us)
Async XLA Ops:
  7.2 252.8 %copy-start = (bf16[4096,250]{1,0:T(8,128)(2,1)S(1)}, bf16[4096,250]{1,0:T(8,128)(2,1)}, u32[]{:S(2)}) copy-start(bf16[4096,250]{1,0:T(8,128)(2,1)} %param.23) | copy-start | bytes 6144004
  7.2 101.6 %all-gather.3.cloned.1.call-start = ((), (), s32[]{:S(2)}) async-start(), calls=%async_computation.9 | async-start | bytes 4227072 | tf_op jit(solution)/shard_map/all_gather | solution.py:88
  7.9 136.0 %all-gather.5.cloned.1.call-start = ((), (), s32[]{:S(2)}) async-start(), calls=%async_computation.10 | async-start | bytes 2621440 | tf_op jit(solution)/shard_map/all_gather | solution.py:107
  8.9 46.1 %copy-start.3 = (f32[4096]{0:T(1024)S(1)}, f32[4096]{0:T(1024)}, u32[]{:S(2)}) copy-start(f32[4096]{0:T(1024)} %param.17) | copy-start | bytes 49156
  11.8 66.1 %copy-start.1 = (bf16[32,512]{1,0:T(8,128)(2,1)S(1)}, bf16[32,512]{1,0:T(8,128)(2,1)}, u32[]{:S(2)}) copy-start(bf16[32,512]{1,0:T(8,128)(2,1)} %param.18) | copy-start | bytes 98308
  56.9 18.2 %all-to-all-start = ((bf16[128,3,32]{2,1,0:T(4,128)(2,1)}), bf16[128,3,32]{2,1,0:T(4,128)(2,1)S(1)}, u32[]{:S(2)}, u32[]{:S(2)}) async-start(bf16[128,3,32]{2,1,0:T(4,128)(2,1)} %copy.74), calls=%async_computation | async-start | bytes 262144 | tf_op jit(solution)/shard_map/all_to_all | solution.py:24
  79.2 22.3 %all-to-all-start.1 = ((f32[128,1,512]{2,1,0:T(1,128)}), f32[128,1,512]{2,1,0:T(1,128)S(1)}, u32[]{:S(2)}, u32[]{:S(2)}) async-start(f32[128,1,512]{2,1,0:T(1,128)} %copy.77), calls=%async_computation.1 | async-start | bytes 524288 | tf_op jit(solution)/shard_map/all_to_all | solution.py:24
  111.5 37.0 %all-to-all-start.2 = ((bf16[128,2,256]{2,1,0:T(2,128)(2,1)}), bf16[128,2,256]{2,1,0:T(2,128)(2,1)S(1)}, u32[]{:S(2)}, u32[]{:S(2)}) async-start(bf16[128,2,256]{2,1,0:T(2,128)(2,1)} %reshape.196), calls=%async_computation.2 | async-start | bytes 262144 | tf_op jit(solution)/shard_map/all_to_all | solution.py:24
  121.7 27.1 %copy-start.2 = (bf16[32,512]{1,0:T(8,128)(2,1)S(1)}, bf16[32,512]{1,0:T(8,128)(2,1)}, u32[]{:S(2)}) copy-start(bf16[32,512]{1,0:T(8,128)(2,1)} %param.19) | copy-start | bytes 98308
  150.0 25.7 %all-to-all-start.3 = ((f32[128,1,128]{2,1,0:T(1,128)}), f32[128,1,128]{2,1,0:T(1,128)S(1)}, u32[]{:S(2)}, u32[]{:S(2)}) async-start(f32[128,1,128]{2,1,0:T(1,128)} %reshape.198), calls=%async_computation.3 | async-start | bytes 131072 | tf_op jit(solution)/shard_map/all_to_all | solution.py:24
  183.8 19.3 %all-to-all-start.5 = ((bf16[128,2,256]{2,1,0:T(2,128)(2,1)}), bf16[128,2,256]{2,1,0:T(2,128)(2,1)S(1)}, u32[]{:S(2)}, u32[]{:S(2)}) async-start(bf16[128,2,256]{2,1,0:T(2,128)(2,1)} %reshape.200), calls=%async_computation.5 | async-start | bytes 262144 | tf_op jit(solution)/shard_map/all_to_all | solution.py:24
  190.4 28.7 %reduce-scatter.2.cloned.1.call-start = ((), (), s32[]{:S(2)}) async-start(), calls=%async_computation.11 | async-start | bytes 81920 | tf_op jit(solution)/shard_map/reduce_scatter | solution.py:142
Sparse Core Ops, SparseCore 0:
  11.1 97.5 all-gather.2
  110.9 33.0 all-gather.4
  205.0 14.0 reduce-scatter.1

commit v10 on v6

--- a/solution.py
+++ b/solution.py
@@ -92,16 +92,26 @@
     probe_part = jnp.einsum(
         "rhc,dhc->rhd", query_heads, key_rows, precision=lax.Precision.HIGHEST
     )
-    probe_in = exchange(probe_part, "fsdp")
-    probe = jnp.transpose(probe_in, (1, 0, 2)).reshape(heads_local, width)
+    probe_flat = probe_part.reshape(groups, heads_local * dpiece)
+    probe_high = probe_flat.astype(jnp.bfloat16)
+    probe_low = (probe_flat - probe_high.astype(jnp.float32)).astype(jnp.bfloat16)
 
     piece_width = vision_tokens.shape[1]
     slot_of = destination * capacity + slot_index
     outbox_select = (
         jnp.arange(groups * capacity, dtype=jnp.int32)[:, None] == slot_of[None, :]
     )
-    outbox = select_rows(outbox_select, vision_tokens).reshape(groups, capacity, piece_width)
-    received_piece = exchange(outbox, "fsdp").reshape(groups * capacity, piece_width)
+    outbox = select_rows(outbox_select, vision_tokens).reshape(groups, capacity * piece_width)
+    bundle = jnp.concatenate([outbox, probe_high, probe_low], axis=1)
+    bundle_in = exchange(bundle, "fsdp")
+    vision_end = capacity * piece_width
+    probe_size = heads_local * dpiece
+    received_piece = bundle_in[:, :vision_end].reshape(groups * capacity, piece_width)
+    probe_in = (
+        bundle_in[:, vision_end : vision_end + probe_size].astype(jnp.float32)
+        + bundle_in[:, vision_end + probe_size :].astype(jnp.float32)
+    ).reshape(groups, heads_local, dpiece)
+    probe = jnp.transpose(probe_in, (1, 0, 2)).reshape(heads_local, width)
     received_all = gather_by_exchange(received_piece, "seq", seq_count)
     received = jnp.transpose(received_all, (1, 0, 2)).reshape(groups * capacity, width)
     occupied = (

time: 280 us -> 274 us (0.979)
  waiting for transfers between devices: 88.2 us -> 58.8 us
  blocking collectives: 101 us -> 128 us
  starting transfers between devices: 29.7 us -> 17.3 us
  local copies, waits for them, and re-layouts: 16 us -> 22.4 us
    all_to_all x5 -> x3, waiting for transfers between devices: 73.8 us -> 45.2 us  [exchange(): lax.all_to_all(rows, axis_name, split_axis=0, concat_axis=0, tiled=True)]
    all_to_all x4 -> x5, blocking collectives: 101 us -> 128 us  [exchange(): lax.all_to_all(rows, axis_name, split_axis=0, concat_axis=0, tiled=True)]
    all_to_all x5 -> x3, starting transfers between devices: 29.4 us -> 17 us  [exchange(): lax.all_to_all(rows, axis_name, split_axis=0, concat_axis=0, tiled=True)]
    unnamed x21 -> x19, local copies, waits for them, and re-layouts: 7.11 us -> 10.1 us
  transfers between devices with their start and end apart: 7 -> 5, of which waited for: 6 -> 4; matrix products, arithmetic and copies ran while one was open for 9% -> 12% of each run, Pallas kernels for 0% -> 0%
where the time goes in v10:
time: 274 us; the launch traced here: 273 us
  blocking collectives  128 us (47%)
  waiting for transfers between devices  58.8 us (21%)
  local copies, waits for them, and re-layouts  22.4 us (8%)
  starting transfers between devices  17.3 us (6%)
  between operations  16.5 us (6%)
  other arithmetic  15.1 us (6%)
  matrix products  14.2 us (5%)
    all_to_all x5, blocking collectives, exchange(): lax.all_to_all(rows, axis_name, split_axis=0, concat_axis=0, tiled=True)  128 us
    all_to_all x3, waiting for transfers between devices, exchange(): lax.all_to_all(rows, axis_name, split_axis=0, concat_axis=0, tiled=True)  45.2 us
    all_to_all x3, starting transfers between devices, exchange(): lax.all_to_all(rows, axis_name, split_axis=0, concat_axis=0, tiled=True)  17 us
    reduce_scatter x1, waiting for transfers between devices, local(): lax.psum_scatter(partial_out, 'seq', scatter_dimension=0, tiled=True)  12.9 us
    unnamed x19, local copies, waits for them, and re-layouts  10.1 us
  transfers between devices with their start and end apart: 5, of which 4 were waited for; matrix products, arithmetic and copies ran while one was open for 12% of the time, Pallas kernels for 0%

profile of v10, /device:TPU:1, one launch (start us, length us, event | category | flops | bytes accessed | tf_op | source)
XLA Modules:
  0.0 272.6 jit_solution(1725730353605473566)
XLA Ops:
  7.2 0.7 all-gather.2.cloned.1.call-update
  8.6 1.5 multiply_reduce_fusion.1
  10.8 0.9 fusion.32
  11.9 0.7 fusion.18
  12.6 0.2 reduce_window_sum.30
  12.8 0.8 select_reduce_fusion
  13.9 31.1 %all_to_all.57 = bf16[128,3,32]{2,1,0:T(4,128)(2,1)S(1)} all-to-all(bf16[128,3,32]{2,1,0:T(4,128)(2,1)S(1)} %copy.104), channel_id=1, replica_groups=mesh['fsdp'=128,'seq'=4] {'fsdp'}, dimensions={0} | all-to-all | bytes 49152 | tf_op jit(solution)/shard_map/all_to_all | solution.py:24
  45.0 0.7 fusion.33
  45.8 1.0 convolution_bitcast_fusion
  46.8 0.3 copy.107
  47.0 20.3 %all_to_all.58 = f32[128,1,512]{2,1,0:T(1,128)S(1)} all-to-all(f32[128,1,512]{2,1,0:T(1,128)S(1)} %copy.107), channel_id=1, replica_groups=mesh['fsdp'=128,'seq'=4] {'fsdp'}, dimensions={0} | all-to-all | bytes 524288 | tf_op jit(solution)/shard_map/all_to_all | solution.py:24
  67.3 0.2 reduce_sum.77
  67.7 0.5 broadcast.86
  68.2 1.4 reduce.12
  69.6 0.7 reshape.210
  70.3 5.5 %all-to-all-start.2 = ((bf16[128,2,256]{2,1,0:T(2,128)(2,1)}), bf16[128,2,256]{2,1,0:T(2,128)(2,1)S(1)}, u32[]{:S(2)}, u32[]{:S(2)}) async-start(bf16[128,2,256]{2,1,0:T(2,128)(2,1)} %reshape.210), calls=%async_computation.2 | async-start | bytes 262144 | tf_op jit(solution)/shard_map/all_to_all | solution.py:24
  75.8 0.3 convolution_convert_fusion.1
  76.1 0.2 reshape.189
  76.3 13.2 %all-to-all-done.2 = bf16[128,2,256]{2,1,0:T(2,128)(2,1)S(1)} async-done(((bf16[128,2,256]{2,1,0:T(2,128)(2,1)}), bf16[128,2,256]{2,1,0:T(2,128)(2,1)S(1)}, u32[]{:S(2)}, u32[]{:S(2)}) %all-to-all-start.2) | async-done | bytes 131104 | tf_op jit(solution)/shard_map/all_to_all | solution.py:24
  89.6 0.2 copy.108
  89.8 0.9 fusion.21
  90.9 1.1 reduce.13
  92.1 27.4 %all_to_all.59 = bf16[128,2,1152]{2,1,0:T(2,128)(2,1)} all-to-all(bf16[128,2,1152]{2,1,0:T(2,128)(2,1)S(1)} %reshape.212), channel_id=1, replica_groups=mesh['fsdp'=128,'seq'=4] {'fsdp'}, dimensions={0} | all-to-all | bytes 1179648 | tf_op jit(solution)/shard_map/all_to_all | solution.py:24
  119.5 3.9 %reshape.213 = bf16[128,1,2304]{2,1,0:T(2,128)(2,1)S(1)} reshape(bf16[128,2,1152]{2,1,0:T(2,128)(2,1)} %all_to_all.59) | data formatting | bytes 1179648
  123.4 2.1 copy.114
  125.5 1.1 slice.46
  126.5 0.2 copy.116
  126.8 0.2 broadcast_in_dim.45
  126.9 0.2 copy.117
  127.1 1.5 broadcast_in_dim.46
  128.6 4.4 %all-to-all-start.4 = ((bf16[4,256,1024]{1,2,0:T(8,128)(2,1)}), bf16[4,256,1024]{1,2,0:T(8,128)(2,1)}, u32[]{:S(2)}, u32[]{:S(2)}) async-start(bf16[4,256,1024]{1,2,0:T(8,128)(2,1)} %broadcast_in_dim.46), calls=%async_computation.4 | async-start | bytes 4194304 | tf_op jit(solution)/shard_map/all_to_all | solution.py:24
  133.9 2.4 fusion.16
  136.4 0.2 lt.65
  136.6 0.3 reduce-window.9
  137.4 0.2 fusion.11
  137.6 0.8 convert_add_fusion
  138.5 0.2 reshape.194
  138.7 20.4 %all-to-all-done.4 = bf16[4,256,1024]{1,2,0:T(8,128)(2,1)} async-done(((bf16[4,256,1024]{1,2,0:T(8,128)(2,1)}), bf16[4,256,1024]{1,2,0:T(8,128)(2,1)}, u32[]{:S(2)}, u32[]{:S(2)}) %all-to-all-start.4) | async-done | bytes 2097184 | tf_op jit(solution)/shard_map/all_to_all | solution.py:24
  159.0 3.3 %fusion.1 = (f32[280]{0:T(512)S(1)}, bf16[280,4096]{1,0:T(8,128)(2,1)S(1)}) fusion(bf16[280,4096]{1,0:T(8,128)(2,1)} %param.12, bf16[256,4096]{0,1:T(8,128)(2,1)} %bitcast.17, s32[256]{0:T(256)S(1)} %compare_select_fusion, pred[280]{0:T(512)(128)(4,1)S(1)} %fusion.11), kind=kOutput, calls=%fused_computation.4 | convolution fusion | flops 593008384 | bytes 6687096 | tf_op jit(solution)/shard_map/dot_general | solution.py:33
  162.4 2.1 fusion.34
  164.5 0.2 fusion.27
  164.8 4.3 %fusion.4 = bf16[35,4,8,128]{3,2,1,0:T(8,128)(2,1)S(1)} fusion(bf16[4096,512]{1,0:T(8,128)(2,1)} %all-gather.2.cloned.1.call-done, bf16[280,4096]{1,0:T(8,128)(2,1)} %copy-done.4, f32[4096]{0:T(1024)S(1)} %copy-done.2, f32[280]{0:T(512)S(1)} %add_rsqrt_fusion), kind=kOutput, calls=%fused_computation.10 | convolution fusion | flops 1179136000 | bytes 6792288 | tf_op jit(solution)/shard_map/dot_general | solution.py:128
  169.1 0.1 fusion.8
  169.3 0.1 broadcast_in_dim.49
  169.4 1.4 reduce.14
  170.8 0.7 reshape.214
  171.5 7.0 %all-to-all-start.5 = ((bf16[128,2,256]{2,1,0:T(2,128)(2,1)}), bf16[128,2,256]{2,1,0:T(2,128)(2,1)S(1)}, u32[]{:S(2)}, u32[]{:S(2)}) async-start(bf16[128,2,256]{2,1,0:T(2,128)(2,1)} %reshape.214), calls=%async_computation.5 | async-start | bytes 262144 | tf_op jit(solution)/shard_map/all_to_all | solution.py:24
  178.5 0.3 reduce-scatter.2.cloned.1.call-start
  178.8 0.8 dynamic_slice.15
  179.6 11.7 %all-to-all-done.5 = bf16[128,2,256]{2,1,0:T(2,128)(2,1)S(1)} async-done(((bf16[128,2,256]{2,1,0:T(2,128)(2,1)}), bf16[128,2,256]{2,1,0:T(2,128)(2,1)S(1)}, u32[]{:S(2)}, u32[]{:S(2)}) %all-to-all-start.5) | async-done | bytes 131104 | tf_op jit(solution)/shard_map/all_to_all | solution.py:24
  191.4 1.6 fusion.13
  193.0 0.7 constant_dynamic-slice_fusion
  193.7 12.9 %reduce-scatter.2.cloned.1.call-done = f32[32,32]{1,0:T(8,128)} async-done(((f32[128,32]{1,0:T(8,128)}), f32[32,32]{1,0:T(8,128)}) %reduce-scatter.2.cloned.1.call-update) | async-done | bytes 4112 | tf_op jit(solution)/shard_map/reduce_scatter | solution.py:151
  206.6 0.8 multiply_convert_fusion
  207.9 1.6 reshape.216
  209.5 33.0 %all_to_all.60 = bf16[128,2,544]{2,1,0:T(2,128)(2,1)} all-to-all(bf16[128,2,544]{2,1,0:T(2,128)(2,1)S(1)} %reshape.216), channel_id=1, replica_groups=mesh['fsdp'=128,'seq'=4] {'fsdp'}, dimensions={0} | all-to-all | bytes 557056 | tf_op jit(solution)/shard_map/all_to_all | solution.py:24
  242.4 2.9 %reshape.217 = bf16[128,32,34]{2,1,0:T(8,128)(2,1)S(1)} reshape(bf16[128,2,544]{2,1,0:T(2,128)(2,1)} %all_to_all.60) | data formatting | bytes 557056
  245.4 0.5 convert_reduce_fusion
  245.9 0.4 copy.120
  246.3 1.1 reshape.198
  247.5 0.6 convolution_reduce_fusion
  248.0 0.5 rsqrt_multiply_fusion
  248.6 16.5 %all_to_all.61 = f32[128,1,32]{2,1,0:T(1,128)S(1)} all-to-all(f32[128,1,32]{2,1,0:T(1,128)S(1)} %broadcast_in_dim.86), channel_id=1, replica_groups=mesh['fsdp'=128,'seq'=4] {'fsdp'}, dimensions={0} | all-to-all | bytes 32768 | tf_op jit(solution)/shard_map/all_to_all | solution.py:24
  265.1 0.7 reduce_max.29
  (52 shorter events, 2.8 us)
Async XLA Ops:
  7.2 240.3 %copy-start = (bf16[4096,250]{1,0:T(8,128)(2,1)S(1)}, bf16[4096,250]{1,0:T(8,128)(2,1)}, u32[]{:S(2)}) copy-start(bf16[4096,250]{1,0:T(8,128)(2,1)} %param.23) | copy-start | bytes 6144004
  7.2 68.6 %copy-start.3 = (s32[128,1]{0,1:T(1,128)S(1)}, s32[128,1]{0,1:T(1,128)}, u32[]{:S(2)}) copy-start(s32[128,1]{0,1:T(1,128)} %param.14) | copy-start | bytes 1540
  7.2 68.7 %copy-start.1 = (bf16[128,1024]{1,0:T(8,128)(2,1)S(1)}, bf16[128,1024]{1,0:T(8,128)(2,1)}, u32[]{:S(2)}) copy-start(bf16[128,1024]{1,0:T(8,128)(2,1)} %param.13) | copy-start | bytes 786436
  7.2 157.6 %all-gather.2.cloned.1.call-start = ((), (), s32[]{:S(2)}) async-start(), calls=%async_computation.9 | async-start | bytes 4227072 | tf_op jit(solution)/shard_map/all_gather | solution.py:130
  70.3 19.2 %all-to-all-start.2 = ((bf16[128,2,256]{2,1,0:T(2,128)(2,1)}), bf16[128,2,256]{2,1,0:T(2,128)(2,1)S(1)}, u32[]{:S(2)}, u32[]{:S(2)}) async-start(bf16[128,2,256]{2,1,0:T(2,128)(2,1)} %reshape.210), calls=%async_computation.2 | async-start | bytes 262144 | tf_op jit(solution)/shard_map/all_to_all | solution.py:24
  128.6 30.4 %all-to-all-start.4 = ((bf16[4,256,1024]{1,2,0:T(8,128)(2,1)}), bf16[4,256,1024]{1,2,0:T(8,128)(2,1)}, u32[]{:S(2)}, u32[]{:S(2)}) async-start(bf16[4,256,1024]{1,2,0:T(8,128)(2,1)} %broadcast_in_dim.46), calls=%async_computation.4 | async-start | bytes 4194304 | tf_op jit(solution)/shard_map/all_to_all | solution.py:24
  159.0 3.4 %copy-start.2 = (f32[4096]{0:T(1024)S(1)}, f32[4096]{0:T(1024)}, u32[]{:S(2)}) copy-start(f32[4096]{0:T(1024)} %param.17) | copy-start | bytes 49156
  162.4 2.1 copy-start.4
  171.5 19.8 %all-to-all-start.5 = ((bf16[128,2,256]{2,1,0:T(2,128)(2,1)}), bf16[128,2,256]{2,1,0:T(2,128)(2,1)S(1)}, u32[]{:S(2)}, u32[]{:S(2)}) async-start(bf16[128,2,256]{2,1,0:T(2,128)(2,1)} %reshape.214), calls=%async_computation.5 | async-start | bytes 262144 | tf_op jit(solution)/shard_map/all_to_all | solution.py:24
  178.5 28.0 %reduce-scatter.2.cloned.1.call-start = ((), (), s32[]{:S(2)}) async-start(), calls=%async_computation.10 | async-start | bytes 81920 | tf_op jit(solution)/shard_map/reduce_scatter | solution.py:151
Sparse Core Ops, SparseCore 0:
  11.2 96.3 all-gather.1
  193.1 13.4 reduce-scatter.1

commit v11 on v10

--- a/solution.py
+++ b/solution.py
@@ -101,15 +101,14 @@
     outbox_select = (
         jnp.arange(groups * capacity, dtype=jnp.int32)[:, None] == slot_of[None, :]
     )
-    outbox = select_rows(outbox_select, vision_tokens).reshape(groups, capacity * piece_width)
-    bundle = jnp.concatenate([outbox, probe_high, probe_low], axis=1)
+    outbox = select_rows(outbox_select, vision_tokens).reshape(groups, capacity, piece_width)
+    probe_halves = jnp.stack([probe_high, probe_low], axis=1)
+    bundle = jnp.concatenate([outbox, probe_halves], axis=2)
     bundle_in = exchange(bundle, "fsdp")
-    vision_end = capacity * piece_width
-    probe_size = heads_local * dpiece
-    received_piece = bundle_in[:, :vision_end].reshape(groups * capacity, piece_width)
+    received_piece = bundle_in[:, :, :piece_width].reshape(groups * capacity, piece_width)
     probe_in = (
-        bundle_in[:, vision_end : vision_end + probe_size].astype(jnp.float32)
-        + bundle_in[:, vision_end + probe_size :].astype(jnp.float32)
+        bundle_in[:, 0, piece_width:].astype(jnp.float32)
+        + bundle_in[:, 1, piece_width:].astype(jnp.float32)
     ).reshape(groups, heads_local, dpiece)
     probe = jnp.transpose(probe_in, (1, 0, 2)).reshape(heads_local, width)
     received_all = gather_by_exchange(received_piece, "seq", seq_count)

time: 274 us -> 268 us (0.978)
  blocking collectives: 128 us -> 101 us
  waiting for transfers between devices: 58.8 us -> 81.8 us
  local copies, waits for them, and re-layouts: 22.4 us -> 16.3 us
  starting transfers between devices: 17.3 us -> 22.1 us
    all_to_all x5 -> x4, blocking collectives: 128 us -> 101 us  [exchange(): lax.all_to_all(rows, axis_name, split_axis=0, concat_axis=0, tiled=True)]
    all_to_all x3 -> x4, waiting for transfers between devices: 45.2 us -> 67.5 us  [exchange(): lax.all_to_all(rows, axis_name, split_axis=0, concat_axis=0, tiled=True)]
    all_to_all x3 -> x4, starting transfers between devices: 17 us -> 21.8 us  [exchange(): lax.all_to_all(rows, axis_name, split_axis=0, concat_axis=0, tiled=True)]
    unnamed x19, local copies, waits for them, and re-layouts: 10.1 us -> 6.35 us
  transfers between devices with their start and end apart: 5 -> 6, of which waited for: 4 -> 5; matrix products, arithmetic and copies ran while one was open for 12% -> 10% of each run, Pallas kernels for 0% -> 0%
where the time goes in v11:
time: 268 us; the launch traced here: 267 us
  blocking collectives  101 us (38%)
  waiting for transfers between devices  81.8 us (31%)
  starting transfers between devices  22.1 us (8%)
  between operations  16.5 us (6%)
  local copies, waits for them, and re-layouts  16.3 us (6%)
  other arithmetic  14.8 us (6%)
  matrix products  14.4 us (5%)
    all_to_all x4, blocking collectives, exchange(): lax.all_to_all(rows, axis_name, split_axis=0, concat_axis=0, tiled=True)  101 us
    all_to_all x4, waiting for transfers between devices, exchange(): lax.all_to_all(rows, axis_name, split_axis=0, concat_axis=0, tiled=True)  67.5 us
    all_to_all x4, starting transfers between devices, exchange(): lax.all_to_all(rows, axis_name, split_axis=0, concat_axis=0, tiled=True)  21.8 us
    reduce_scatter x1, waiting for transfers between devices, local(): lax.psum_scatter(partial_out, 'seq', scatter_dimension=0, tiled=True)  13.6 us
    unnamed x19, local copies, waits for them, and re-layouts  6.35 us
  transfers between devices with their start and end apart: 6, of which 5 were waited for; matrix products, arithmetic and copies ran while one was open for 10% of the time, Pallas kernels for 0%

profile of v11, /device:TPU:1, one launch (start us, length us, event | category | flops | bytes accessed | tf_op | source)
XLA Modules:
  0.0 266.8 jit_solution(12947847600996170470)
XLA Ops:
  7.2 0.7 all-gather.2.cloned.1.call-update
  8.6 1.5 multiply_reduce_fusion.1
  10.8 0.9 fusion.32
  11.9 0.7 fusion.18
  12.6 0.2 reduce_window_sum.30
  12.8 0.8 select_reduce_fusion
  13.9 31.1 %all_to_all.50 = bf16[128,3,32]{2,1,0:T(4,128)(2,1)S(1)} all-to-all(bf16[128,3,32]{2,1,0:T(4,128)(2,1)S(1)} %copy.101), channel_id=1, replica_groups=mesh['fsdp'=128,'seq'=4] {'fsdp'}, dimensions={0} | all-to-all | bytes 49152 | tf_op jit(solution)/shard_map/all_to_all | solution.py:24
  45.2 1.0 convolution_bitcast_fusion
  46.1 0.3 copy.104
  46.4 20.4 %all_to_all.51 = f32[128,1,512]{2,1,0:T(1,128)S(1)} all-to-all(f32[128,1,512]{2,1,0:T(1,128)S(1)} %copy.104), channel_id=1, replica_groups=mesh['fsdp'=128,'seq'=4] {'fsdp'}, dimensions={0} | all-to-all | bytes 524288 | tf_op jit(solution)/shard_map/all_to_all | solution.py:24
  66.8 0.2 reduce_sum.77
  67.1 0.1 broadcast_in_dim.42
  67.2 0.5 broadcast.86
  67.7 1.4 reduce.12
  69.1 0.7 reshape.239
  69.8 5.5 %all-to-all-start.2 = ((bf16[128,2,256]{2,1,0:T(2,128)(2,1)}), bf16[128,2,256]{2,1,0:T(2,128)(2,1)S(1)}, u32[]{:S(2)}, u32[]{:S(2)}) async-start(bf16[128,2,256]{2,1,0:T(2,128)(2,1)} %reshape.239), calls=%async_computation.2 | async-start | bytes 262144 | tf_op jit(solution)/shard_map/all_to_all | solution.py:24
  75.4 1.2 convolution_convert_fusion.1
  76.6 0.2 reshape.219
  76.8 12.3 %all-to-all-done.2 = bf16[128,2,256]{2,1,0:T(2,128)(2,1)S(1)} async-done(((bf16[128,2,256]{2,1,0:T(2,128)(2,1)}), bf16[128,2,256]{2,1,0:T(2,128)(2,1)S(1)}, u32[]{:S(2)}, u32[]{:S(2)}) %all-to-all-start.2) | async-done | bytes 131104 | tf_op jit(solution)/shard_map/all_to_all | solution.py:24
  89.2 0.2 copy.105
  89.4 0.1 fusion.21
  89.8 1.5 maximum_maximum_fusion
  91.3 5.6 %all-to-all-start.3 = ((bf16[128,2,1152]{2,1,0:T(2,128)(2,1)}), bf16[128,2,1152]{2,1,0:T(2,128)(2,1)S(1)}, u32[]{:S(2)}, u32[]{:S(2)}) async-start(bf16[128,2,1152]{2,1,0:T(2,128)(2,1)} %maximum_maximum_fusion), calls=%async_computation.3 | async-start | bytes 1179648 | tf_op jit(solution)/shard_map/all_to_all | solution.py:24
  96.9 0.1 lt.62
  97.7 21.2 %all-to-all-done.3 = bf16[128,2,1152]{2,1,0:T(2,128)(2,1)S(1)} async-done(((bf16[128,2,1152]{2,1,0:T(2,128)(2,1)}), bf16[128,2,1152]{2,1,0:T(2,128)(2,1)S(1)}, u32[]{:S(2)}, u32[]{:S(2)}) %all-to-all-start.3) | async-done | bytes 589856 | tf_op jit(solution)/shard_map/all_to_all | solution.py:24
  118.9 0.4 slice.46
  119.2 1.0 broadcast_in_dim.45
  120.2 1.2 copy.113
  121.5 1.5 broadcast_in_dim.46
  123.0 4.5 %all-to-all-start.4 = ((bf16[4,256,1024]{1,2,0:T(8,128)(2,1)}), bf16[4,256,1024]{1,2,0:T(8,128)(2,1)}, u32[]{:S(2)}, u32[]{:S(2)}) async-start(bf16[4,256,1024]{1,2,0:T(8,128)(2,1)} %broadcast_in_dim.46), calls=%async_computation.4 | async-start | bytes 4194304 | tf_op jit(solution)/shard_map/all_to_all | solution.py:24
  127.5 2.4 fusion.16
  130.0 0.2 lt.65
  130.2 0.3 reduce-window.9
  130.7 0.1 reshape.230
  131.0 0.2 fusion.11
  131.5 0.1 copy.112
  131.7 0.2 reshape.223
  131.8 22.2 %all-to-all-done.4 = bf16[4,256,1024]{1,2,0:T(8,128)(2,1)} async-done(((bf16[4,256,1024]{1,2,0:T(8,128)(2,1)}), bf16[4,256,1024]{1,2,0:T(8,128)(2,1)}, u32[]{:S(2)}, u32[]{:S(2)}) %all-to-all-start.4) | async-done | bytes 2097184 | tf_op jit(solution)/shard_map/all_to_all | solution.py:24
  154.0 3.3 %fusion.1 = (f32[280]{0:T(512)S(1)}, bf16[280,4096]{1,0:T(8,128)(2,1)S(1)}) fusion(bf16[280,4096]{1,0:T(8,128)(2,1)} %param.12, bf16[256,4096]{0,1:T(8,128)(2,1)} %bitcast.15, s32[256]{0:T(256)S(1)} %compare_select_fusion, pred[280]{0:T(512)(128)(4,1)S(1)} %fusion.11), kind=kOutput, calls=%fused_computation.4 | convolution fusion | flops 593008384 | bytes 6687096 | tf_op jit(solution)/shard_map/dot_general | solution.py:33
  157.4 2.1 fusion.36
  159.5 0.2 fusion.27
  159.8 4.3 %fusion.4 = bf16[35,4,8,128]{3,2,1,0:T(8,128)(2,1)S(1)} fusion(bf16[4096,512]{1,0:T(8,128)(2,1)} %all-gather.2.cloned.1.call-done, bf16[280,4096]{1,0:T(8,128)(2,1)} %copy-done.4, f32[4096]{0:T(1024)S(1)} %copy-done.2, f32[280]{0:T(512)S(1)} %add_rsqrt_fusion), kind=kOutput, calls=%fused_computation.10 | convolution fusion | flops 1179136000 | bytes 6792288 | tf_op jit(solution)/shard_map/dot_general | solution.py:127
  164.1 0.1 fusion.8
  164.3 0.1 broadcast_in_dim.49
  164.4 1.4 reduce.13
  165.8 0.7 reshape.241
  166.5 6.2 %all-to-all-start.5 = ((bf16[128,2,256]{2,1,0:T(2,128)(2,1)}), bf16[128,2,256]{2,1,0:T(2,128)(2,1)S(1)}, u32[]{:S(2)}, u32[]{:S(2)}) async-start(bf16[128,2,256]{2,1,0:T(2,128)(2,1)} %reshape.241), calls=%async_computation.5 | async-start | bytes 262144 | tf_op jit(solution)/shard_map/all_to_all | solution.py:24
  172.7 0.3 reduce-scatter.2.cloned.1.call-start
  173.0 0.8 dynamic_slice.15
  173.8 11.8 %all-to-all-done.5 = bf16[128,2,256]{2,1,0:T(2,128)(2,1)S(1)} async-done(((bf16[128,2,256]{2,1,0:T(2,128)(2,1)}), bf16[128,2,256]{2,1,0:T(2,128)(2,1)S(1)}, u32[]{:S(2)}, u32[]{:S(2)}) %all-to-all-start.5) | async-done | bytes 131104 | tf_op jit(solution)/shard_map/all_to_all | solution.py:24
  185.6 1.6 fusion.13
  187.2 13.6 %reduce-scatter.2.cloned.1.call-done = f32[32,32]{1,0:T(8,128)} async-done(((f32[128,32]{1,0:T(8,128)}), f32[32,32]{1,0:T(8,128)}) %reduce-scatter.2.cloned.1.call-update) | async-done | bytes 4112 | tf_op jit(solution)/shard_map/reduce_scatter | solution.py:150
  200.8 0.8 multiply_convert_fusion
  201.9 0.1 broadcast_in_dim.50
  202.1 1.6 reshape.243
  203.7 33.0 %all_to_all.52 = bf16[128,2,544]{2,1,0:T(2,128)(2,1)} all-to-all(bf16[128,2,544]{2,1,0:T(2,128)(2,1)S(1)} %reshape.243), channel_id=1, replica_groups=mesh['fsdp'=128,'seq'=4] {'fsdp'}, dimensions={0} | all-to-all | bytes 557056 | tf_op jit(solution)/shard_map/all_to_all | solution.py:24
  236.7 2.9 %reshape.244 = bf16[128,32,34]{2,1,0:T(8,128)(2,1)S(1)} reshape(bf16[128,2,544]{2,1,0:T(2,128)(2,1)} %all_to_all.52) | data formatting | bytes 557056
  239.6 0.5 convert_reduce_fusion
  240.1 0.4 copy.116
  240.5 1.1 reshape.227
  241.7 0.6 convolution_reduce_fusion
  242.2 0.5 rsqrt_multiply_fusion
  242.8 16.5 %all_to_all.53 = f32[128,1,32]{2,1,0:T(1,128)S(1)} all-to-all(f32[128,1,32]{2,1,0:T(1,128)S(1)} %broadcast_in_dim.86), channel_id=1, replica_groups=mesh['fsdp'=128,'seq'=4] {'fsdp'}, dimensions={0} | all-to-all | bytes 32768 | tf_op jit(solution)/shard_map/all_to_all | solution.py:24
  259.3 0.7 reduce_max.29
  (51 shorter events, 2.4 us)
Async XLA Ops:
  7.2 234.5 %copy-start = (bf16[4096,250]{1,0:T(8,128)(2,1)S(1)}, bf16[4096,250]{1,0:T(8,128)(2,1)}, u32[]{:S(2)}) copy-start(bf16[4096,250]{1,0:T(8,128)(2,1)} %param.23) | copy-start | bytes 6144004
  7.2 68.2 %copy-start.3 = (s32[128,1]{0,1:T(1,128)S(1)}, s32[128,1]{0,1:T(1,128)}, u32[]{:S(2)}) copy-start(s32[128,1]{0,1:T(1,128)} %param.14) | copy-start | bytes 1540
  7.2 152.6 %all-gather.2.cloned.1.call-start = ((), (), s32[]{:S(2)}) async-start(), calls=%async_computation.9 | async-start | bytes 4227072 | tf_op jit(solution)/shard_map/all_gather | solution.py:129
  46.4 43.0 %copy-start.1 = (bf16[32,512]{1,0:T(8,128)(2,1)S(1)}, bf16[32,512]{1,0:T(8,128)(2,1)}, u32[]{:S(2)}) copy-start(bf16[32,512]{1,0:T(8,128)(2,1)} %param.19) | copy-start | bytes 98308
  69.8 19.3 %all-to-all-start.2 = ((bf16[128,2,256]{2,1,0:T(2,128)(2,1)}), bf16[128,2,256]{2,1,0:T(2,128)(2,1)S(1)}, u32[]{:S(2)}, u32[]{:S(2)}) async-start(bf16[128,2,256]{2,1,0:T(2,128)(2,1)} %reshape.239), calls=%async_computation.2 | async-start | bytes 262144 | tf_op jit(solution)/shard_map/all_to_all | solution.py:24
  91.3 27.6 %all-to-all-start.3 = ((bf16[128,2,1152]{2,1,0:T(2,128)(2,1)}), bf16[128,2,1152]{2,1,0:T(2,128)(2,1)S(1)}, u32[]{:S(2)}, u32[]{:S(2)}) async-start(bf16[128,2,1152]{2,1,0:T(2,128)(2,1)} %maximum_maximum_fusion), calls=%async_computation.3 | async-start | bytes 1179648 | tf_op jit(solution)/shard_map/all_to_all | solution.py:24
  123.0 31.1 %all-to-all-start.4 = ((bf16[4,256,1024]{1,2,0:T(8,128)(2,1)}), bf16[4,256,1024]{1,2,0:T(8,128)(2,1)}, u32[]{:S(2)}, u32[]{:S(2)}) async-start(bf16[4,256,1024]{1,2,0:T(8,128)(2,1)} %broadcast_in_dim.46), calls=%async_computation.4 | async-start | bytes 4194304 | tf_op jit(solution)/shard_map/all_to_all | solution.py:24
  154.0 3.4 %copy-start.2 = (f32[4096]{0:T(1024)S(1)}, f32[4096]{0:T(1024)}, u32[]{:S(2)}) copy-start(f32[4096]{0:T(1024)} %param.17) | copy-start | bytes 49156
  157.4 2.1 copy-start.4
  166.5 19.0 %all-to-all-start.5 = ((bf16[128,2,256]{2,1,0:T(2,128)(2,1)}), bf16[128,2,256]{2,1,0:T(2,128)(2,1)S(1)}, u32[]{:S(2)}, u32[]{:S(2)}) async-start(bf16[128,2,256]{2,1,0:T(2,128)(2,1)} %reshape.241), calls=%async_computation.5 | async-start | bytes 262144 | tf_op jit(solution)/shard_map/all_to_all | solution.py:24
  172.7 28.1 %reduce-scatter.2.cloned.1.call-start = ((), (), s32[]{:S(2)}) async-start(), calls=%async_computation.10 | async-start | bytes 81920 | tf_op jit(solution)/shard_map/reduce_scatter | solution.py:150
Sparse Core Ops, SparseCore 0:
  11.2 95.5 all-gather.1
  187.3 13.4 reduce-scatter.1

commit v12 on v11

--- a/solution.py
+++ b/solution.py
@@ -70,18 +70,8 @@
 
     final_text = lax.dynamic_slice_in_dim(text_embeds, last_index, 1, 0)
     last_normed = row_norm(final_text, attn_gain)
-    pieces = jnp.stack(
-        [
-            final_text.reshape(groups, dpiece),
-            last_normed.reshape(groups, dpiece),
-            jnp.broadcast_to(counts.astype(jnp.bfloat16)[:, None], (groups, dpiece)),
-        ],
-        axis=1,
-    )
-    pieces_in = exchange(pieces, "fsdp")
-    text_part = pieces_in[:, 0]
-    normed_part = pieces_in[:, 1]
-    arrived = pieces_in[:, 2, :1].astype(jnp.int32)
+    pieces_in = exchange(last_normed.reshape(groups, dpiece), "fsdp")
+    normed_part = pieces_in
 
     query_partial = jnp.dot(normed_part, w_query, preferred_element_type=jnp.float32)
     query_mine = jnp.sum(exchange(query_partial, "fsdp"), axis=0).astype(jnp.bfloat16)
@@ -102,13 +92,27 @@
         jnp.arange(groups * capacity, dtype=jnp.int32)[:, None] == slot_of[None, :]
     )
     outbox = select_rows(outbox_select, vision_tokens).reshape(groups, capacity, piece_width)
-    probe_halves = jnp.stack([probe_high, probe_low], axis=1)
+    side_high = jnp.concatenate(
+        [
+            probe_high,
+            final_text.reshape(groups, dpiece),
+            jnp.broadcast_to(counts.astype(jnp.bfloat16)[:, None], (groups, dpiece)),
+            jnp.zeros((groups, probe_high.shape[1] - 2 * dpiece), jnp.bfloat16),
+        ],
+        axis=1,
+    )
+    side_low = jnp.concatenate([probe_low, jnp.zeros_like(probe_low)], axis=1)
+    probe_halves = jnp.stack([side_high, side_low], axis=1)
     bundle = jnp.concatenate([outbox, probe_halves], axis=2)
     bundle_in = exchange(bundle, "fsdp")
     received_piece = bundle_in[:, :, :piece_width].reshape(groups * capacity, piece_width)
+    probe_size = heads_local * dpiece
+    side_start = piece_width + probe_size
+    text_part = bundle_in[:, 0, side_start : side_start + dpiece]
+    arrived = bundle_in[:, 0, side_start + dpiece : side_start + dpiece + 1].astype(jnp.int32)
     probe_in = (
-        bundle_in[:, 0, piece_width:].astype(jnp.float32)
-        + bundle_in[:, 1, piece_width:].astype(jnp.float32)
+        bundle_in[:, 0, piece_width:side_start].astype(jnp.float32)
+        + bundle_in[:, 1, piece_width:side_start].astype(jnp.float32)
     ).reshape(groups, heads_local, dpiece)
     probe = jnp.transpose(probe_in, (1, 0, 2)).reshape(heads_local, width)
     received_all = gather_by_exchange(received_piece, "seq", seq_count)

time: 268 us -> 268 us (level)
  blocking collectives: 101 us -> 79.1 us
  waiting for transfers between devices: 81.8 us -> 96.9 us
  starting transfers between devices: 22.1 us -> 28.9 us
    all_to_all x4 -> x3, blocking collectives: 101 us -> 79.1 us  [exchange(): lax.all_to_all(rows, axis_name, split_axis=0, concat_axis=0, tiled=True)]
    all_to_all x4 -> x5, waiting for transfers between devices: 67.5 us -> 82.7 us  [exchange(): lax.all_to_all(rows, axis_name, split_axis=0, concat_axis=0, tiled=True)]
    all_to_all x4 -> x5, starting transfers between devices: 21.8 us -> 28.6 us  [exchange(): lax.all_to_all(rows, axis_name, split_axis=0, concat_axis=0, tiled=True)]
    unnamed x19 -> x22, local copies, waits for them, and re-layouts: 6.35 us -> 6.28 us
  transfers between devices with their start and end apart: 6 -> 7, of which waited for: 5 -> 6; matrix products, arithmetic and copies ran while one was open for 10% -> 10% of each run, Pallas kernels for 0% -> 0%
where the time goes in v12:
time: 268 us; the launch traced here: 267 us
  waiting for transfers between devices  96.9 us (36%)
  blocking collectives  79.1 us (30%)
  starting transfers between devices  28.9 us (11%)
  local copies, waits for them, and re-layouts  17.7 us (7%)
  between operations  16.5 us (6%)
  other arithmetic  14.8 us (6%)
  matrix products  13.4 us (5%)
    all_to_all x5, waiting for transfers between devices, exchange(): lax.all_to_all(rows, axis_name, split_axis=0, concat_axis=0, tiled=True)  82.7 us
    all_to_all x3, blocking collectives, exchange(): lax.all_to_all(rows, axis_name, split_axis=0, concat_axis=0, tiled=True)  79.1 us
    all_to_all x5, starting transfers between devices, exchange(): lax.all_to_all(rows, axis_name, split_axis=0, concat_axis=0, tiled=True)  28.6 us
    reduce_scatter x1, waiting for transfers between devices, local(): lax.psum_scatter(partial_out, 'seq', scatter_dimension=0, tiled=True)  13.6 us
    unnamed x22, local copies, waits for them, and re-layouts  6.28 us
  transfers between devices with their start and end apart: 7, of which 6 were waited for; matrix products, arithmetic and copies ran while one was open for 10% of the time, Pallas kernels for 0%

profile of v12, /device:TPU:1, one launch (start us, length us, event | category | flops | bytes accessed | tf_op | source)
XLA Modules:
  0.0 267.4 jit_solution(9138057494891634836)
XLA Ops:
  7.2 0.7 all-gather.2.cloned.1.call-update
  8.6 1.5 multiply_reduce_fusion.1
  10.8 0.9 fusion.32
  11.8 29.7 %all_to_all.58 = bf16[128,1,32]{2,1,0:T(2,128)(2,1)S(1)} all-to-all(bf16[128,1,32]{2,1,0:T(2,128)(2,1)S(1)} %all_to_all.49), channel_id=1, replica_groups=mesh['fsdp'=128,'seq'=4] {'fsdp'}, dimensions={0} | all-to-all | bytes 16384 | tf_op jit(solution)/shard_map/all_to_all | solution.py:24
  41.6 1.0 convolution_bitcast_fusion
  42.5 1.0 copy.101
  43.5 5.7 %all-to-all-start.1 = ((f32[128,1,512]{2,1,0:T(1,128)}), f32[128,1,512]{2,1,0:T(1,128)S(1)}, u32[]{:S(2)}, u32[]{:S(2)}) async-start(f32[128,1,512]{2,1,0:T(1,128)} %copy.101), calls=%async_computation.1 | async-start | bytes 524288 | tf_op jit(solution)/shard_map/all_to_all | solution.py:24
  49.3 0.7 fusion.18
  50.0 0.2 reduce_window_sum.30
  50.2 0.8 select_reduce_fusion
  51.0 13.7 %all-to-all-done.1 = f32[128,1,512]{2,1,0:T(1,128)S(1)} async-done(((f32[128,1,512]{2,1,0:T(1,128)}), f32[128,1,512]{2,1,0:T(1,128)S(1)}, u32[]{:S(2)}, u32[]{:S(2)}) %all-to-all-start.1) | async-done | bytes 262176 | tf_op jit(solution)/shard_map/all_to_all | solution.py:24
  64.7 0.2 reduce_sum.76
  65.0 0.1 broadcast_in_dim.45
  65.1 0.5 broadcast.87
  65.6 1.4 reduce.12
  67.0 0.7 reshape.221
  67.7 5.5 %all-to-all-start.2 = ((bf16[128,2,256]{2,1,0:T(2,128)(2,1)}), bf16[128,2,256]{2,1,0:T(2,128)(2,1)S(1)}, u32[]{:S(2)}, u32[]{:S(2)}) async-start(bf16[128,2,256]{2,1,0:T(2,128)(2,1)} %reshape.221), calls=%async_computation.2 | async-start | bytes 262144 | tf_op jit(solution)/shard_map/all_to_all | solution.py:24
  73.2 0.7 reshape.204
  73.9 0.3 convolution_convert_fusion.1
  74.2 0.2 reshape.200
  74.5 12.8 %all-to-all-done.2 = bf16[128,2,256]{2,1,0:T(2,128)(2,1)S(1)} async-done(((bf16[128,2,256]{2,1,0:T(2,128)(2,1)}), bf16[128,2,256]{2,1,0:T(2,128)(2,1)S(1)}, u32[]{:S(2)}, u32[]{:S(2)}) %all-to-all-start.2) | async-done | bytes 131104 | tf_op jit(solution)/shard_map/all_to_all | solution.py:24
  87.4 0.2 copy.102
  87.6 0.1 fusion.21
  88.1 0.1 copy.107
  88.2 1.4 pad_maximum_fusion
  89.7 5.6 %all-to-all-start.3 = ((bf16[128,2,1280]{2,1,0:T(2,128)(2,1)}), bf16[128,2,1280]{2,1,0:T(2,128)(2,1)S(1)}, u32[]{:S(2)}, u32[]{:S(2)}) async-start(bf16[128,2,1280]{2,1,0:T(2,128)(2,1)} %pad_maximum_fusion), calls=%async_computation.3 | async-start | bytes 1310720 | tf_op jit(solution)/shard_map/all_to_all | solution.py:24
  96.1 22.9 %all-to-all-done.3 = bf16[128,2,1280]{2,1,0:T(2,128)(2,1)S(1)} async-done(((bf16[128,2,1280]{2,1,0:T(2,128)(2,1)}), bf16[128,2,1280]{2,1,0:T(2,128)(2,1)S(1)}, u32[]{:S(2)}, u32[]{:S(2)}) %all-to-all-start.3) | async-done | bytes 655392 | tf_op jit(solution)/shard_map/all_to_all | solution.py:24
  118.9 0.4 slice.41
  119.3 1.0 broadcast_in_dim.51
  120.3 1.2 copy.112
  121.5 1.5 broadcast_in_dim.52
  123.0 4.4 %all-to-all-start.4 = ((bf16[4,256,1024]{1,2,0:T(8,128)(2,1)}), bf16[4,256,1024]{1,2,0:T(8,128)(2,1)}, u32[]{:S(2)}, u32[]{:S(2)}) async-start(bf16[4,256,1024]{1,2,0:T(8,128)(2,1)} %broadcast_in_dim.52), calls=%async_computation.4 | async-start | bytes 4194304 | tf_op jit(solution)/shard_map/all_to_all | solution.py:24
  127.5 2.5 fusion.16
  130.1 0.2 lt.65
  130.3 0.3 reduce-window.9
  131.4 0.2 reshape.205
  131.8 0.2 fusion.11
  131.9 21.6 %all-to-all-done.4 = bf16[4,256,1024]{1,2,0:T(8,128)(2,1)} async-done(((bf16[4,256,1024]{1,2,0:T(8,128)(2,1)}), bf16[4,256,1024]{1,2,0:T(8,128)(2,1)}, u32[]{:S(2)}, u32[]{:S(2)}) %all-to-all-start.4) | async-done | bytes 2097184 | tf_op jit(solution)/shard_map/all_to_all | solution.py:24
  153.6 3.3 %fusion.1 = (f32[280]{0:T(512)S(1)}, bf16[280,4096]{1,0:T(8,128)(2,1)S(1)}) fusion(bf16[280,4096]{1,0:T(8,128)(2,1)} %param.12, bf16[256,4096]{0,1:T(8,128)(2,1)} %bitcast.17, s32[256]{0:T(256)S(1)} %compare_select_fusion, pred[280]{0:T(512)(128)(4,1)S(1)} %fusion.11), kind=kOutput, calls=%fused_computation.4 | convolution fusion | flops 593008384 | bytes 6687096 | tf_op jit(solution)/shard_map/dot_general | solution.py:33
  156.9 2.1 fusion.34
  159.1 0.2 fusion.27
  159.4 4.3 %fusion.4 = bf16[35,4,8,128]{3,2,1,0:T(8,128)(2,1)S(1)} fusion(bf16[4096,512]{1,0:T(8,128)(2,1)} %all-gather.2.cloned.1.call-done, bf16[280,4096]{1,0:T(8,128)(2,1)} %copy-done.6, f32[4096]{0:T(1024)S(1)} %copy-done.4, f32[280]{0:T(512)S(1)} %add_rsqrt_fusion), kind=kOutput, calls=%fused_computation.10 | convolution fusion | flops 1179136000 | bytes 6792288 | tf_op jit(solution)/shard_map/dot_general | solution.py:131
  163.6 0.1 fusion.8
  163.8 0.1 broadcast_in_dim.55
  164.0 1.4 reduce.13
  165.4 0.7 reshape.223
  166.0 7.3 %all-to-all-start.5 = ((bf16[128,2,256]{2,1,0:T(2,128)(2,1)}), bf16[128,2,256]{2,1,0:T(2,128)(2,1)S(1)}, u32[]{:S(2)}, u32[]{:S(2)}) async-start(bf16[128,2,256]{2,1,0:T(2,128)(2,1)} %reshape.223), calls=%async_computation.5 | async-start | bytes 262144 | tf_op jit(solution)/shard_map/all_to_all | solution.py:24
  173.4 0.3 reduce-scatter.2.cloned.1.call-start
  173.7 0.8 dynamic_slice.15
  174.5 11.6 %all-to-all-done.5 = bf16[128,2,256]{2,1,0:T(2,128)(2,1)S(1)} async-done(((bf16[128,2,256]{2,1,0:T(2,128)(2,1)}), bf16[128,2,256]{2,1,0:T(2,128)(2,1)S(1)}, u32[]{:S(2)}, u32[]{:S(2)}) %all-to-all-start.5) | async-done | bytes 131104 | tf_op jit(solution)/shard_map/all_to_all | solution.py:24
  186.2 1.6 fusion.13
  187.8 13.6 %reduce-scatter.2.cloned.1.call-done = f32[32,32]{1,0:T(8,128)} async-done(((f32[128,32]{1,0:T(8,128)}), f32[32,32]{1,0:T(8,128)}) %reduce-scatter.2.cloned.1.call-update) | async-done | bytes 4112 | tf_op jit(solution)/shard_map/reduce_scatter | solution.py:154
  201.4 0.8 multiply_convert_fusion
  202.5 0.1 broadcast_in_dim.96
  202.7 1.6 reshape.225
  204.3 33.0 %all_to_all.59 = bf16[128,2,544]{2,1,0:T(2,128)(2,1)} all-to-all(bf16[128,2,544]{2,1,0:T(2,128)(2,1)S(1)} %reshape.225), channel_id=1, replica_groups=mesh['fsdp'=128,'seq'=4] {'fsdp'}, dimensions={0} | all-to-all | bytes 557056 | tf_op jit(solution)/shard_map/all_to_all | solution.py:24
  237.2 2.9 %reshape.226 = bf16[128,32,34]{2,1,0:T(8,128)(2,1)S(1)} reshape(bf16[128,2,544]{2,1,0:T(2,128)(2,1)} %all_to_all.59) | data formatting | bytes 557056
  240.2 0.5 convert_reduce_fusion
  240.7 0.4 copy.115
  241.1 1.1 reshape.209
  242.3 0.6 convolution_reduce_fusion
  242.8 0.5 rsqrt_multiply_fusion
  243.4 16.5 %all_to_all.60 = f32[128,1,32]{2,1,0:T(1,128)S(1)} all-to-all(f32[128,1,32]{2,1,0:T(1,128)S(1)} %broadcast_in_dim.97), channel_id=1, replica_groups=mesh['fsdp'=128,'seq'=4] {'fsdp'}, dimensions={0} | all-to-all | bytes 32768 | tf_op jit(solution)/shard_map/all_to_all | solution.py:24
  259.9 0.7 reduce_max.29
  (59 shorter events, 2.7 us)
Async XLA Ops:
  7.2 235.1 %copy-start = (bf16[4096,250]{1,0:T(8,128)(2,1)S(1)}, bf16[4096,250]{1,0:T(8,128)(2,1)}, u32[]{:S(2)}) copy-start(bf16[4096,250]{1,0:T(8,128)(2,1)} %param.23) | copy-start | bytes 6144004
  7.2 66.0 %copy-start.5 = (s32[128,1]{0,1:T(1,128)S(1)}, s32[128,1]{0,1:T(1,128)}, u32[]{:S(2)}) copy-start(s32[128,1]{0,1:T(1,128)} %param.14) | copy-start | bytes 1540
  7.2 66.7 %copy-start.1 = (bf16[128,1024]{1,0:T(8,128)(2,1)S(1)}, bf16[128,1024]{1,0:T(8,128)(2,1)}, u32[]{:S(2)}) copy-start(bf16[128,1024]{1,0:T(8,128)(2,1)} %param.13) | copy-start | bytes 786436
  7.2 152.1 %all-gather.2.cloned.1.call-start = ((), (), s32[]{:S(2)}) async-start(), calls=%async_computation.9 | async-start | bytes 4227072 | tf_op jit(solution)/shard_map/all_gather | solution.py:133
  43.5 21.2 %all-to-all-start.1 = ((f32[128,1,512]{2,1,0:T(1,128)}), f32[128,1,512]{2,1,0:T(1,128)S(1)}, u32[]{:S(2)}, u32[]{:S(2)}) async-start(f32[128,1,512]{2,1,0:T(1,128)} %copy.101), calls=%async_computation.1 | async-start | bytes 524288 | tf_op jit(solution)/shard_map/all_to_all | solution.py:24
  49.2 38.3 %copy-start.3 = (bf16[32,512]{1,0:T(8,128)(2,1)S(1)}, bf16[32,512]{1,0:T(8,128)(2,1)}, u32[]{:S(2)}) copy-start(bf16[32,512]{1,0:T(8,128)(2,1)} %param.19) | copy-start | bytes 98308
  67.7 19.6 %all-to-all-start.2 = ((bf16[128,2,256]{2,1,0:T(2,128)(2,1)}), bf16[128,2,256]{2,1,0:T(2,128)(2,1)S(1)}, u32[]{:S(2)}, u32[]{:S(2)}) async-start(bf16[128,2,256]{2,1,0:T(2,128)(2,1)} %reshape.221), calls=%async_computation.2 | async-start | bytes 262144 | tf_op jit(solution)/shard_map/all_to_all | solution.py:24
  74.2 13.7 %copy-start.2 = (bf16[128,32]{1,0:T(8,128)(2,1)S(1)}, bf16[128,32]{1,0:T(8,128)(2,1)}, u32[]{:S(2)}) copy-start(bf16[128,32]{1,0:T(8,128)(2,1)} %reshape.204) | copy-start | bytes 24580
  89.7 29.3 %all-to-all-start.3 = ((bf16[128,2,1280]{2,1,0:T(2,128)(2,1)}), bf16[128,2,1280]{2,1,0:T(2,128)(2,1)S(1)}, u32[]{:S(2)}, u32[]{:S(2)}) async-start(bf16[128,2,1280]{2,1,0:T(2,128)(2,1)} %pad_maximum_fusion), calls=%async_computation.3 | async-start | bytes 1310720 | tf_op jit(solution)/shard_map/all_to_all | solution.py:24
  123.0 30.5 %all-to-all-start.4 = ((bf16[4,256,1024]{1,2,0:T(8,128)(2,1)}), bf16[4,256,1024]{1,2,0:T(8,128)(2,1)}, u32[]{:S(2)}, u32[]{:S(2)}) async-start(bf16[4,256,1024]{1,2,0:T(8,128)(2,1)} %broadcast_in_dim.52), calls=%async_computation.4 | async-start | bytes 4194304 | tf_op jit(solution)/shard_map/all_to_all | solution.py:24
  153.6 3.4 %copy-start.4 = (f32[4096]{0:T(1024)S(1)}, f32[4096]{0:T(1024)}, u32[]{:S(2)}) copy-start(f32[4096]{0:T(1024)} %param.17) | copy-start | bytes 49156
  156.9 2.1 copy-start.6
  166.0 20.1 %all-to-all-start.5 = ((bf16[128,2,256]{2,1,0:T(2,128)(2,1)}), bf16[128,2,256]{2,1,0:T(2,128)(2,1)S(1)}, u32[]{:S(2)}, u32[]{:S(2)}) async-start(bf16[128,2,256]{2,1,0:T(2,128)(2,1)} %reshape.223), calls=%async_computation.5 | async-start | bytes 262144 | tf_op jit(solution)/shard_map/all_to_all | solution.py:24
  173.4 28.0 %reduce-scatter.2.cloned.1.call-start = ((), (), s32[]{:S(2)}) async-start(), calls=%async_computation.10 | async-start | bytes 81920 | tf_op jit(solution)/shard_map/reduce_scatter | solution.py:154
Sparse Core Ops, SparseCore 0:
  11.2 97.7 all-gather.1
  187.9 13.4 reduce-scatter.1

commit v13 on v11

--- a/solution.py
+++ b/solution.py
@@ -147,7 +147,9 @@
     attended_seq = gather_by_exchange(attended, "fsdp", groups)
     out_rows = lax.dynamic_slice_in_dim(w_out, seq_index * columns, columns, 0)
     partial_out = jnp.dot(attended_seq, out_rows, preferred_element_type=jnp.float32)
-    out_mine = lax.psum_scatter(partial_out, "seq", scatter_dimension=0, tiled=True)
+    out_mine = jnp.sum(
+        exchange(partial_out.reshape(seq_count, quarter, dpiece), "seq"), axis=0
+    )
     text_mine = lax.dynamic_slice_in_dim(text_part, seq_index * quarter, quarter, 0)
     residual_out = text_mine.astype(jnp.float32) + out_mine
     gain_part = lax.dynamic_slice_in_dim(final_gain, lax.axis_index("fsdp") * dpiece, dpiece, 0)

time: 268 us -> 253 us (0.944)
  blocking collectives: 101 us -> 91.5 us
  waiting for transfers between devices: 81.8 us -> 72.5 us
  starting transfers between devices: 22.1 us -> 25.2 us
    reduce_scatter x1 -> x0, waiting for transfers between devices: 13.6 us -> none  [local(): lax.psum_scatter(partial_out, 'seq', scatter_dimension=0, tiled=True)]
    all_to_all x4, blocking collectives: 101 us -> 91.5 us  [exchange(): lax.all_to_all(rows, axis_name, split_axis=0, concat_axis=0, tiled=True)]
    all_to_all x4 -> x5, waiting for transfers between devices: 67.5 us -> 71.8 us  [exchange(): lax.all_to_all(rows, axis_name, split_axis=0, concat_axis=0, tiled=True)]
    all_to_all x4 -> x5, starting transfers between devices: 21.8 us -> 25.2 us  [exchange(): lax.all_to_all(rows, axis_name, split_axis=0, concat_axis=0, tiled=True)]
    unnamed x19 -> x22, local copies, waits for them, and re-layouts: 6.35 us -> 7.15 us
  transfers between devices with their start and end apart: 6 -> 6, of which waited for: 5 -> 5; matrix products, arithmetic and copies ran while one was open for 10% -> 11% of each run, Pallas kernels for 0% -> 0%
where the time goes in v13:
time: 253 us; the launch traced here: 252 us
  blocking collectives  91.5 us (36%)
  waiting for transfers between devices  72.5 us (29%)
  starting transfers between devices  25.2 us (10%)
  local copies, waits for them, and re-layouts  17.6 us (7%)
  between operations  16.5 us (7%)
  other arithmetic  14.8 us (6%)
  matrix products  13.7 us (5%)
    all_to_all x4, blocking collectives, exchange(): lax.all_to_all(rows, axis_name, split_axis=0, concat_axis=0, tiled=True)  91.5 us
    all_to_all x5, waiting for transfers between devices, exchange(): lax.all_to_all(rows, axis_name, split_axis=0, concat_axis=0, tiled=True)  71.8 us
    all_to_all x5, starting transfers between devices, exchange(): lax.all_to_all(rows, axis_name, split_axis=0, concat_axis=0, tiled=True)  25.2 us
    unnamed x22, local copies, waits for them, and re-layouts  7.15 us
  transfers between devices with their start and end apart: 6, of which 5 were waited for; matrix products, arithmetic and copies ran while one was open for 11% of the time, Pallas kernels for 0%

profile of v13, /device:TPU:1, one launch (start us, length us, event | category | flops | bytes accessed | tf_op | source)
XLA Modules:
  0.0 251.8 jit_solution(164413713257097214)
XLA Ops:
  7.2 0.7 all-gather.2.cloned.1.call-update
  8.6 1.5 multiply_reduce_fusion.1
  10.8 0.9 fusion.31
  11.9 0.7 fusion.15
  12.6 0.2 reduce_window_sum.30
  12.8 0.8 select_reduce_fusion
  13.9 31.1 %all_to_all.52 = bf16[128,3,32]{2,1,0:T(4,128)(2,1)S(1)} all-to-all(bf16[128,3,32]{2,1,0:T(4,128)(2,1)S(1)} %copy.81), channel_id=1, replica_groups=mesh['fsdp'=128,'seq'=4] {'fsdp'}, dimensions={0} | all-to-all | bytes 49152 | tf_op jit(solution)/shard_map/all_to_all | solution.py:24
  45.2 1.0 convolution_bitcast_fusion
  46.1 0.3 copy.83
  46.4 20.4 %all_to_all.53 = f32[128,1,512]{2,1,0:T(1,128)S(1)} all-to-all(f32[128,1,512]{2,1,0:T(1,128)S(1)} %copy.83), channel_id=1, replica_groups=mesh['fsdp'=128,'seq'=4] {'fsdp'}, dimensions={0} | all-to-all | bytes 524288 | tf_op jit(solution)/shard_map/all_to_all | solution.py:24
  66.8 0.2 reduce_sum.86
  67.1 0.1 broadcast_in_dim.42
  67.2 0.5 broadcast.86
  67.7 1.4 reduce.12
  69.1 0.7 reshape.243
  69.8 5.5 %all-to-all-start.2 = ((bf16[128,2,256]{2,1,0:T(2,128)(2,1)}), bf16[128,2,256]{2,1,0:T(2,128)(2,1)S(1)}, u32[]{:S(2)}, u32[]{:S(2)}) async-start(bf16[128,2,256]{2,1,0:T(2,128)(2,1)} %reshape.243), calls=%async_computation.2 | async-start | bytes 262144 | tf_op jit(solution)/shard_map/all_to_all | solution.py:24
  75.4 1.2 convolution_convert_fusion.1
  76.6 0.2 reshape.222
  76.8 12.3 %all-to-all-done.2 = bf16[128,2,256]{2,1,0:T(2,128)(2,1)S(1)} async-done(((bf16[128,2,256]{2,1,0:T(2,128)(2,1)}), bf16[128,2,256]{2,1,0:T(2,128)(2,1)S(1)}, u32[]{:S(2)}, u32[]{:S(2)}) %all-to-all-start.2) | async-done | bytes 131104 | tf_op jit(solution)/shard_map/all_to_all | solution.py:24
  89.3 0.2 copy.84
  89.4 0.1 fusion.18
  89.8 1.5 maximum_maximum_fusion
  91.3 5.6 %all-to-all-start.3 = ((bf16[128,2,1152]{2,1,0:T(2,128)(2,1)}), bf16[128,2,1152]{2,1,0:T(2,128)(2,1)S(1)}, u32[]{:S(2)}, u32[]{:S(2)}) async-start(bf16[128,2,1152]{2,1,0:T(2,128)(2,1)} %maximum_maximum_fusion), calls=%async_computation.3 | async-start | bytes 1179648 | tf_op jit(solution)/shard_map/all_to_all | solution.py:24
  97.7 21.2 %all-to-all-done.3 = bf16[128,2,1152]{2,1,0:T(2,128)(2,1)S(1)} async-done(((bf16[128,2,1152]{2,1,0:T(2,128)(2,1)}), bf16[128,2,1152]{2,1,0:T(2,128)(2,1)S(1)}, u32[]{:S(2)}, u32[]{:S(2)}) %all-to-all-start.3) | async-done | bytes 589856 | tf_op jit(solution)/shard_map/all_to_all | solution.py:24
  118.9 0.4 slice.46
  119.2 1.0 broadcast_in_dim.45
  120.2 1.2 copy.92
  121.5 1.5 broadcast_in_dim.46
  123.0 4.5 %all-to-all-start.4 = ((bf16[4,256,1024]{1,2,0:T(8,128)(2,1)}), bf16[4,256,1024]{1,2,0:T(8,128)(2,1)}, u32[]{:S(2)}, u32[]{:S(2)}) async-start(bf16[4,256,1024]{1,2,0:T(8,128)(2,1)} %broadcast_in_dim.46), calls=%async_computation.4 | async-start | bytes 4194304 | tf_op jit(solution)/shard_map/all_to_all | solution.py:24
  127.5 2.4 fusion.13
  130.0 0.2 lt.65
  130.1 0.3 reduce-window.9
  130.7 0.1 reshape.233
  131.0 0.2 fusion.11
  131.7 0.2 reshape.226
  131.8 22.3 %all-to-all-done.4 = bf16[4,256,1024]{1,2,0:T(8,128)(2,1)} async-done(((bf16[4,256,1024]{1,2,0:T(8,128)(2,1)}), bf16[4,256,1024]{1,2,0:T(8,128)(2,1)}, u32[]{:S(2)}, u32[]{:S(2)}) %all-to-all-start.4) | async-done | bytes 2097184 | tf_op jit(solution)/shard_map/all_to_all | solution.py:24
  154.1 3.3 %fusion.1 = (f32[280]{0:T(512)S(1)}, bf16[280,4096]{1,0:T(8,128)(2,1)S(1)}) fusion(bf16[280,4096]{1,0:T(8,128)(2,1)} %param.12, bf16[256,4096]{0,1:T(8,128)(2,1)} %bitcast.15, s32[256]{0:T(256)S(1)} %compare_select_fusion, pred[280]{0:T(512)(128)(4,1)S(1)} %fusion.11), kind=kOutput, calls=%fused_computation.4 | convolution fusion | flops 593008384 | bytes 6687096 | tf_op jit(solution)/shard_map/dot_general | solution.py:33
  157.5 2.1 fusion.35
  159.6 0.2 fusion.26
  159.9 4.3 %fusion.4 = bf16[35,4,8,128]{3,2,1,0:T(8,128)(2,1)S(1)} fusion(bf16[4096,512]{1,0:T(8,128)(2,1)} %all-gather.2.cloned.1.call-done, bf16[280,4096]{1,0:T(8,128)(2,1)} %copy-done.4, f32[4096]{0:T(1024)S(1)} %copy-done.2, f32[280]{0:T(512)S(1)} %add_rsqrt_fusion), kind=kOutput, calls=%fused_computation.10 | convolution fusion | flops 1179136000 | bytes 6792288 | tf_op jit(solution)/shard_map/dot_general | solution.py:127
  164.2 0.1 fusion.8
  164.4 0.1 broadcast_in_dim.49
  164.5 1.4 reduce.13
  165.9 0.7 reshape.245
  166.6 6.1 %all-to-all-start.5 = ((bf16[128,2,256]{2,1,0:T(2,128)(2,1)}), bf16[128,2,256]{2,1,0:T(2,128)(2,1)S(1)}, u32[]{:S(2)}, u32[]{:S(2)}) async-start(bf16[128,2,256]{2,1,0:T(2,128)(2,1)} %reshape.245), calls=%async_computation.5 | async-start | bytes 262144 | tf_op jit(solution)/shard_map/all_to_all | solution.py:24
  172.7 0.8 dynamic_slice.15
  173.5 12.0 %all-to-all-done.5 = bf16[128,2,256]{2,1,0:T(2,128)(2,1)S(1)} async-done(((bf16[128,2,256]{2,1,0:T(2,128)(2,1)}), bf16[128,2,256]{2,1,0:T(2,128)(2,1)S(1)}, u32[]{:S(2)}, u32[]{:S(2)}) %all-to-all-start.5) | async-done | bytes 131104 | tf_op jit(solution)/shard_map/all_to_all | solution.py:24
  185.7 0.9 fusion.21
  186.6 0.7 reshape.247
  187.3 3.5 %all-to-all-start.6 = ((f32[4,1,1024]{2,1,0:T(1,128)}), f32[4,1,1024]{2,1,0:T(1,128)S(1)}, u32[]{:S(2)}, u32[]{:S(2)}) async-start(f32[4,1,1024]{2,1,0:T(1,128)} %reshape.247), calls=%async_computation.6 | async-start | bytes 32768 | tf_op jit(solution)/shard_map/all_to_all | solution.py:24
  190.8 3.9 %all-to-all-done.6 = f32[4,1,1024]{2,1,0:T(1,128)S(1)} async-done(((f32[4,1,1024]{2,1,0:T(1,128)}), f32[4,1,1024]{2,1,0:T(1,128)S(1)}, u32[]{:S(2)}, u32[]{:S(2)}) %all-to-all-start.6) | async-done | bytes 16416 | tf_op jit(solution)/shard_map/all_to_all | solution.py:24
  194.7 0.5 broadcast.88
  195.2 0.7 reduce.14
  196.4 0.1 broadcast_in_dim.50
  196.6 1.6 reshape.249
  198.2 23.4 %all_to_all.54 = bf16[128,2,544]{2,1,0:T(2,128)(2,1)} all-to-all(bf16[128,2,544]{2,1,0:T(2,128)(2,1)S(1)} %reshape.249), channel_id=1, replica_groups=mesh['fsdp'=128,'seq'=4] {'fsdp'}, dimensions={0} | all-to-all | bytes 557056 | tf_op jit(solution)/shard_map/all_to_all | solution.py:24
  221.6 2.9 %reshape.250 = bf16[128,32,34]{2,1,0:T(8,128)(2,1)S(1)} reshape(bf16[128,2,544]{2,1,0:T(2,128)(2,1)} %all_to_all.54) | data formatting | bytes 557056
  224.6 0.5 convert_reduce_fusion
  225.1 0.4 copy.95
  225.5 1.1 reshape.230
  226.6 0.6 convolution_reduce_fusion
  227.2 0.5 rsqrt_multiply_fusion
  227.8 16.5 %all_to_all.55 = f32[128,1,32]{2,1,0:T(1,128)S(1)} all-to-all(f32[128,1,32]{2,1,0:T(1,128)S(1)} %broadcast_in_dim.86), channel_id=1, replica_groups=mesh['fsdp'=128,'seq'=4] {'fsdp'}, dimensions={0} | all-to-all | bytes 32768 | tf_op jit(solution)/shard_map/all_to_all | solution.py:24
  244.3 0.7 reduce_max.29
  (56 shorter events, 2.9 us)
Async XLA Ops:
  7.2 219.5 %copy-start = (bf16[4096,250]{1,0:T(8,128)(2,1)S(1)}, bf16[4096,250]{1,0:T(8,128)(2,1)}, u32[]{:S(2)}) copy-start(bf16[4096,250]{1,0:T(8,128)(2,1)} %param.23) | copy-start | bytes 6144004
  7.2 68.2 %copy-start.3 = (s32[128,1]{0,1:T(1,128)S(1)}, s32[128,1]{0,1:T(1,128)}, u32[]{:S(2)}) copy-start(s32[128,1]{0,1:T(1,128)} %param.14) | copy-start | bytes 1540
  7.2 152.7 %all-gather.2.cloned.1.call-start = ((), (), s32[]{:S(2)}) async-start(), calls=%async_computation.9 | async-start | bytes 4227072 | tf_op jit(solution)/shard_map/all_gather | solution.py:129
  46.4 43.0 %copy-start.1 = (bf16[32,512]{1,0:T(8,128)(2,1)S(1)}, bf16[32,512]{1,0:T(8,128)(2,1)}, u32[]{:S(2)}) copy-start(bf16[32,512]{1,0:T(8,128)(2,1)} %param.19) | copy-start | bytes 98308
  69.8 19.3 %all-to-all-start.2 = ((bf16[128,2,256]{2,1,0:T(2,128)(2,1)}), bf16[128,2,256]{2,1,0:T(2,128)(2,1)S(1)}, u32[]{:S(2)}, u32[]{:S(2)}) async-start(bf16[128,2,256]{2,1,0:T(2,128)(2,1)} %reshape.243), calls=%async_computation.2 | async-start | bytes 262144 | tf_op jit(solution)/shard_map/all_to_all | solution.py:24
  91.3 27.6 %all-to-all-start.3 = ((bf16[128,2,1152]{2,1,0:T(2,128)(2,1)}), bf16[128,2,1152]{2,1,0:T(2,128)(2,1)S(1)}, u32[]{:S(2)}, u32[]{:S(2)}) async-start(bf16[128,2,1152]{2,1,0:T(2,128)(2,1)} %maximum_maximum_fusion), calls=%async_computation.3 | async-start | bytes 1179648 | tf_op jit(solution)/shard_map/all_to_all | solution.py:24
  123.0 31.2 %all-to-all-start.4 = ((bf16[4,256,1024]{1,2,0:T(8,128)(2,1)}), bf16[4,256,1024]{1,2,0:T(8,128)(2,1)}, u32[]{:S(2)}, u32[]{:S(2)}) async-start(bf16[4,256,1024]{1,2,0:T(8,128)(2,1)} %broadcast_in_dim.46), calls=%async_computation.4 | async-start | bytes 4194304 | tf_op jit(solution)/shard_map/all_to_all | solution.py:24
  154.1 3.4 %copy-start.2 = (f32[4096]{0:T(1024)S(1)}, f32[4096]{0:T(1024)}, u32[]{:S(2)}) copy-start(f32[4096]{0:T(1024)} %param.17) | copy-start | bytes 49156
  157.5 2.1 copy-start.4
  166.6 18.9 %all-to-all-start.5 = ((bf16[128,2,256]{2,1,0:T(2,128)(2,1)}), bf16[128,2,256]{2,1,0:T(2,128)(2,1)S(1)}, u32[]{:S(2)}, u32[]{:S(2)}) async-start(bf16[128,2,256]{2,1,0:T(2,128)(2,1)} %reshape.245), calls=%async_computation.5 | async-start | bytes 262144 | tf_op jit(solution)/shard_map/all_to_all | solution.py:24
  187.3 7.4 %all-to-all-start.6 = ((f32[4,1,1024]{2,1,0:T(1,128)}), f32[4,1,1024]{2,1,0:T(1,128)S(1)}, u32[]{:S(2)}, u32[]{:S(2)}) async-start(f32[4,1,1024]{2,1,0:T(1,128)} %reshape.247), calls=%async_computation.6 | async-start | bytes 32768 | tf_op jit(solution)/shard_map/all_to_all | solution.py:24
Sparse Core Ops, SparseCore 0:
  11.2 95.5 all-gather.1
